TPU v7x, 512 devices: a whole 4x4x16 slice. The times are simulated.
512 devices in a mesh: dp: 16 (over z_lo, y), pipe: 4 (over x), tensor: 8 (over z_hi, core).
Axes of the slice: x: 4, y: 4, z: 16 (z_hi: 4, z_lo: 4; z = z_hi * 4 + z_lo), core: 2. Of those that a mesh axis runs over, the one named last changes fastest.
Arguments:
- section_out: bfloat16 [4, 2048, 12288], P('pipe', 'dp', 'tensor'), may hold values from -6 to 6
- embedded: bfloat16 [2048, 12288], P('dp', 'tensor'), may hold values from -6 to 6
- cot_norm: bfloat16 [4, 2048, 12288], P('pipe', 'dp', 'tensor'), may hold values from -3 to 3
- cot_res: bfloat16 [4, 2048, 12288], P('pipe', 'dp', 'tensor'), may hold values from -3 to 3
- gain: bfloat16 [4, 64, 12288], P('pipe', None, 'tensor'), may hold values from 0.25 to 1.75
- bias: bfloat16 [4, 64, 12288], P('pipe', None, 'tensor'), may hold values from -1.5 to 1.5
- lang_ids: int32 [2048], P('dp'), may hold values from 0 to 63
- mb_order: int32 [16, 4], P('dp'), may hold values from 0 to 3, each once within a row
Outputs:
- normed_out: bfloat16 [4, 2048, 12288], P('pipe', 'dp', 'tensor')
- returned_grad: bfloat16 [4, 2048, 12288], P('pipe', 'dp', 'tensor')
- gain_grad: float32 [4, 64, 12288], P('pipe', None, 'tensor')
- bias_grad: float32 [4, 64, 12288], P('pipe', None, 'tensor')
Inputs may be any that keep to these rules, and one draw needn't show every extreme that they name: `lang_ids`: a language id for every token. `mb_order`: each replica's row is a permutation of the 4 micro-batches.
All inputs are finite; a program needn't handle non-finite values.
Results may differ from a plain program's by a relative error of at most 0.0004.
Values may be sent and summed in bfloat16 or wider, within the bound.
No kernel may reach another device: no remote copies, remote signals or barrier semaphores. Data moves between devices by JAX's collectives and lax.ppermute only.
A program may use at most 64 MiB of HBM per device.

v0:
```python
import jax
import jax.numpy as jnp
from jax import lax
from jax.sharding import PartitionSpec as P

D = 12288
MB = 4


eps = 1e-05


def shifted(value, axis, steps):
    count = lax.axis_size(axis)
    leading, last = (max(0, -steps), min(count, count - steps))
    return lax.ppermute(value, axis, [(source, source + steps) for source in range(leading, last)])


def passed_along(array, axis, by):
    length = lax.axis_size(axis)
    return lax.ppermute(array, axis, [(i, (i + by) % length) for i in range(length)])


def reorder(values, order):
    shaped = values.reshape((MB, -1) + values.shape[1:])
    return jnp.take(shaped, order, axis=0).reshape(values.shape)


def invert(order):
    slots = jnp.arange(MB, dtype=jnp.int32)
    hits = (order[:, None] == slots[None, :]).astype(jnp.int32)
    return jnp.sum(slots[:, None] * hits, axis=0)


def local(section_out, embedded, cot_norm, cot_res, gain, bias, lang_ids, mb_order):
    local_width = embedded.shape[1]
    langs = gain.shape[1]
    received = shifted(section_out, "pipe", 1)
    is_first = lax.axis_index("pipe") == 0
    inputs = jnp.where(is_first, embedded, received[0]).astype(jnp.float32)
    order = mb_order[0]
    inverse = invert(order)
    cot_fwd = reorder(cot_norm[0], inverse).astype(jnp.float32)
    pass_fwd = reorder(cot_res[0], inverse).astype(jnp.float32)
    matches = lang_ids[:, None] == jnp.arange(langs, dtype=jnp.int32)[None, :]
    selector = matches.astype(jnp.bfloat16)
    gain_rows = jnp.dot(selector, gain[0], preferred_element_type=jnp.float32)
    bias_rows = jnp.dot(selector, bias[0], preferred_element_type=jnp.float32)
    scaled_cot = cot_fwd * gain_rows
    moment_one, moment_two = lax.psum(
        (jnp.sum(inputs, axis=1), jnp.sum(inputs * inputs, axis=1)), "tensor"
    )
    center = moment_one[:, None] / D
    spread = moment_two[:, None] / D - center * center
    inv_scale = lax.rsqrt(spread + eps)
    normalized = (inputs - center) * inv_scale
    cot_total, cross_total = lax.psum(
        (jnp.sum(scaled_cot, axis=1), jnp.sum(scaled_cot * normalized, axis=1)), "tensor"
    )
    mean_cot = cot_total[:, None] / D
    mean_cross = cross_total[:, None] / D
    normed = (normalized * gain_rows + bias_rows).astype(jnp.bfloat16)
    input_grad = (pass_fwd + inv_scale * (scaled_cot - mean_cot - normalized * mean_cross)).astype(
        jnp.bfloat16
    )
    sent_back = reorder(input_grad, order)
    returned = passed_along(sent_back[None], "pipe", -1)
    products = jnp.concatenate([cot_fwd * normalized, cot_fwd], axis=1)
    local_sums = jnp.dot(
        matches.astype(jnp.float32).T,
        products,
        precision=lax.Precision.HIGHEST,
        preferred_element_type=jnp.float32,
    )
    summed = lax.psum(local_sums, "dp")
    return (normed[None], returned, summed[:, :local_width][None], summed[:, local_width:][None])


def solution(mesh):
    return jax.shard_map(
        local,
        mesh=mesh,
        in_specs=(
            P("pipe", "dp", "tensor"),
            P("dp", "tensor"),
            P("pipe", "dp", "tensor"),
            P("pipe", "dp", "tensor"),
            P("pipe", None, "tensor"),
            P("pipe", None, "tensor"),
            P("dp"),
            P("dp", None),
        ),
        out_specs=(
            P("pipe", "dp", "tensor"),
            P("pipe", "dp", "tensor"),
            P("pipe", None, "tensor"),
            P("pipe", None, "tensor"),
        ),
        check_vma=False,
    )
```

profile of v0, /device:TPU:6, one launch (start us, length us, event | category | flops | bytes accessed | tf_op | source)
XLA Modules:
  0.0 227.5 jit_solution(1984460876628142965)
XLA Ops:
  7.2 0.0 copy-start
  7.2 0.0 copy-start.2
  7.2 0.0 all-reduce.4.cloned.1.call-start
  7.2 1.4 collective-permute-start
  8.7 0.7 select_reduce_fusion
  9.4 0.7 compare_select_fusion
  10.1 0.7 compare_and_fusion
  10.8 0.0 copy-done
  10.8 0.6 gather_fusion
  11.3 0.0 copy-done.2
  11.4 0.6 gather_fusion.1
  12.0 0.1 broadcast_select_fusion.1
  12.1 0.0 copy-start.1
  12.1 0.1 bitcast_convert_fusion
  12.2 0.0 copy-start.3
  12.2 0.0 copy-start.5
  12.2 8.1 %collective-permute-done = bf16[1,128,1536]{2,1,0:T(8,128)(2,1)S(1)} collective-permute-done((bf16[1,128,1536]{2,1,0:T(8,128)(2,1)}, bf16[1,128,1536]{2,1,0:T(8,128)(2,1)S(1)}, u32[]{:S(2)}, u32[]{:S(2)}) %collective-permute-start) | collective-permute-done | bytes 393248 | tf_op jit(solution)/shard_map/ppermute | solution.py:16
  20.3 0.0 copy-done.1
  20.3 0.2 convert_reduce_fusion
  20.6 27.2 %all-reduce.1 = (f32[128]{0:T(128)S(1)}, f32[128]{0:T(128)S(1)}) all-reduce(f32[128]{0:T(128)S(1)} %get-tuple-element.8, f32[128]{0:T(128)S(1)} %get-tuple-element.7), channel_id=1, replica_groups=mesh['dp'=16,'pipe'=4,'tensor'=8] {'tensor'}, use_global_device_ids=true, to_apply=%region_3.4 | all-reduce | flops 256 | bytes 2048 | tf_op jit(solution)/shard_map/psum | solution.py:50
  47.8 0.0 copy-done.3
  47.8 0.0 copy-done.5
  47.8 0.5 fusion.17
  48.3 1.7 fusion.2
  50.0 0.0 all-reduce.4.cloned.1.call-update
  50.0 18.7 %all-reduce = (f32[128]{0:T(128)S(1)}, f32[128]{0:T(128)S(1)}) all-reduce(f32[128]{0:T(128)S(1)} %get-tuple-element.6, f32[128]{0:T(128)S(1)} %get-tuple-element.5), channel_id=1, replica_groups=mesh['dp'=16,'pipe'=4,'tensor'=8] {'tensor'}, use_global_device_ids=true, to_apply=%region_8.10 | all-reduce | flops 256 | bytes 2048 | tf_op jit(solution)/shard_map/psum | solution.py:57
  68.7 0.4 fusion.15
  69.1 0.0 copy-start.4
  69.1 0.6 gather_fusion.2
  69.7 0.1 broadcast_select_fusion
  69.8 2.7 %collective-permute-start.1 = (bf16[1,128,1536]{2,1,0:T(8,128)(2,1)S(1)}, bf16[1,128,1536]{2,1,0:T(8,128)(2,1)S(1)}, u32[]{:S(2)}, u32[]{:S(2)}) collective-permute-start(bf16[1,128,1536]{2,1,0:T(8,128)(2,1)S(1)} %bitcast.42), channel_id=1, source_target_pairs={{0,24},{8,0},{16,8},{24,16},{1,25},{9,1},{17,9},{25,17},{2,26},{10... | collective-permute-start | bytes 1179656 | tf_op jit(solution)/shard_map/ppermute | solution.py:21
  72.6 0.0 copy-done.4
  72.6 1.1 fusion.1
  73.6 9.3 %collective-permute-done.1 = bf16[1,128,1536]{2,1,0:T(8,128)(2,1)S(1)} collective-permute-done((bf16[1,128,1536]{2,1,0:T(8,128)(2,1)S(1)}, bf16[1,128,1536]{2,1,0:T(8,128)(2,1)S(1)}, u32[]{:S(2)}, u32[]{:S(2)}) %collective-permute-start.1) | collective-permute-done | bytes 393248 | tf_op jit(solution)/shard_map/ppermute | solution.py:21
  82.9 135.0 %all-reduce.4.cloned.1.call-done = f32[64,3072]{1,0:T(8,128)} async-done(((f32[64,3072]{1,0:T(8,128)}), f32[64,3072]{1,0:T(8,128)}) %all-reduce.4.cloned.1.call-update) | async-done | bytes 786448 | tf_op jit(solution)/shard_map/psum | solution.py:75
  217.9 2.0 slice_bitcast_fusion
  219.9 0.7 copy.14
  (6 shorter events, 0.0 us)
Async XLA Ops:
  7.2 3.6 %copy-start = (bf16[1,128,1536]{2,1,0:T(8,128)(2,1)S(1)}, bf16[1,128,1536]{2,1,0:T(8,128)(2,1)}, u32[]{:S(2)}) copy-start(bf16[1,128,1536]{2,1,0:T(8,128)(2,1)} %param.13) | copy-start | bytes 1179652
  7.2 4.2 %copy-start.2 = (bf16[1,128,1536]{2,1,0:T(8,128)(2,1)S(1)}, bf16[1,128,1536]{2,1,0:T(8,128)(2,1)}, u32[]{:S(2)}) copy-start(bf16[1,128,1536]{2,1,0:T(8,128)(2,1)} %param.12) | copy-start | bytes 1179652
  7.2 210.7 %all-reduce.4.cloned.1.call-start = ((), (), s32[]{:S(2)}) async-start(), calls=%async_computation | async-start | bytes 1572864 | tf_op jit(solution)/shard_map/psum | solution.py:75
  7.2 13.1 %collective-permute-start = (bf16[1,128,1536]{2,1,0:T(8,128)(2,1)}, bf16[1,128,1536]{2,1,0:T(8,128)(2,1)S(1)}, u32[]{:S(2)}, u32[]{:S(2)}) collective-permute-start(bf16[1,128,1536]{2,1,0:T(8,128)(2,1)} %param.10), channel_id=1, source_target_pairs={{0,8},{8,16},{16,24},{1,9},{9,17},{17,25},{2,10},{10,18},{18,26},{... | collective-permute-start | bytes 1179656 | tf_op jit(solution)/shard_map/ppermute | solution.py:16
  12.1 8.2 %copy-start.1 = (bf16[128,1536]{1,0:T(8,128)(2,1)S(1)}, bf16[128,1536]{1,0:T(8,128)(2,1)}, u32[]{:S(2)}) copy-start(bf16[128,1536]{1,0:T(8,128)(2,1)} %param.11) | copy-start | bytes 1179652
  12.2 35.6 %copy-start.3 = (bf16[1,64,1536]{2,1,0:T(8,128)(2,1)S(1)}, bf16[1,64,1536]{2,1,0:T(8,128)(2,1)}, u32[]{:S(2)}) copy-start(bf16[1,64,1536]{2,1,0:T(8,128)(2,1)} %param.14) | copy-start | bytes 589828
  12.2 35.6 %copy-start.5 = (s32[128]{0:T(128)S(1)}, s32[128]{0:T(128)}, u32[]{:S(2)}) copy-start(s32[128]{0:T(128)} %param.16) | copy-start | bytes 1540
  69.1 3.5 %copy-start.4 = (bf16[1,64,1536]{2,1,0:T(8,128)(2,1)S(1)}, bf16[1,64,1536]{2,1,0:T(8,128)(2,1)}, u32[]{:S(2)}) copy-start(bf16[1,64,1536]{2,1,0:T(8,128)(2,1)} %param.15) | copy-start | bytes 589828
  69.8 13.1 %collective-permute-start.1 = (bf16[1,128,1536]{2,1,0:T(8,128)(2,1)S(1)}, bf16[1,128,1536]{2,1,0:T(8,128)(2,1)S(1)}, u32[]{:S(2)}, u32[]{:S(2)}) collective-permute-start(bf16[1,128,1536]{2,1,0:T(8,128)(2,1)S(1)} %bitcast.42), channel_id=1, source_target_pairs={{0,24},{8,0},{16,8},{24,16},{1,25},{9,1},{17,9},{25,17},{2,26},{10... | collective-permute-start | bytes 1179656 | tf_op jit(solution)/shard_map/ppermute | solution.py:21
Sparse Core Ops, SparseCore 0:
  50.1 167.7 all-reduce.3
where the time goes:
time: 228 us; the launch traced here: 227 us
  waiting for transfers between devices  152 us (67%)
  blocking collectives  45.9 us (20%)
  between operations  14.2 us (6%)
  local copies, waits for them, and re-layouts  4.55 us (2%)
  starting transfers between devices  4.2 us (2%)
  matrix products  3.23 us (1%)
  other arithmetic  3.06 us (1%)
    psum x1, waiting for transfers between devices, local(): summed = lax.psum(local_sums, 'dp')  135 us
    psum x1, blocking collectives, local(): lax.psum((jnp.sum(inputs, axis=1), jnp.sum(inputs * inputs, axis=1)), 'te...  27.2 us
    psum x1, blocking collectives, local(): lax.psum((jnp.sum(scaled_cot, axis=1), jnp.sum(scaled_cot * normalized, a...  18.7 us
    ppermute x1, waiting for transfers between devices, passed_along(): lax.ppermute(array, axis, [(i, (i + by) % length) for i in range(length)])  9.25 us
    ppermute x1, waiting for transfers between devices, shifted(): lax.ppermute(value, axis, [(source, source + steps) for source in range(l...  8.09 us
  transfers between devices with their start and end apart: 3, of which 3 were waited for; matrix products, arithmetic and copies ran while one was open for 2% of the time, Pallas kernels for 0%

commit v1 on v0

v1 whole, which is shorter than its diff:
```python
import jax
import jax.numpy as jnp
from jax import lax
from jax.experimental import pallas as pl
from jax.experimental.pallas import tpu as pltpu
from jax.sharding import Mesh, PartitionSpec as P

D = 12288
MB = 4
eps = 1e-05
bf16, f32 = jnp.bfloat16, jnp.float32
CORES = 2

VMEM = pl.BlockSpec(memory_space=pltpu.VMEM)
SMEM = pl.BlockSpec(memory_space=pltpu.SMEM)


def call(kernel, name, outs, scratch, in_specs, *args):
    return pl.pallas_call(
        kernel,
        name=name,
        out_shape=outs,
        in_specs=in_specs,
        out_specs=jax.tree.map(lambda _: VMEM, outs),
        scratch_shapes=scratch,
        compiler_params=pltpu.CompilerParams(vmem_limit_bytes=40 * 1024 * 1024),
    )(*args)


def rows_of(block, count):
    return pl.ds(pl.multiple_of(block * count, count), count)


def to_forward(order_ref, src_ref, dst_ref):
    rows = dst_ref.shape[0] // MB
    for j in range(MB):
        dst_ref[rows_of(order_ref[0, j], rows), :] = src_ref[0, j * rows : (j + 1) * rows, :]


def members(lang_ref, langs):
    tokens = lang_ref.shape[1]
    row = lax.broadcasted_iota(jnp.int32, (langs, tokens), 0)
    return jnp.where(row == lang_ref[...], 1.0, 0.0).astype(bf16)


def selector(lang_ref, langs):
    tokens = lang_ref.shape[1]
    column = jnp.transpose(jnp.broadcast_to(lang_ref[...].astype(f32), (tokens, tokens)))
    lane = lax.broadcasted_iota(jnp.int32, (tokens, langs), 1).astype(f32)
    return jnp.where(column[:, :langs] == lane, 1.0, 0.0).astype(bf16)


def put_pieces(out_ref, sums):
    pieces, height, width = out_ref.shape
    halves = sums.shape[1] // width
    for k in range(pieces):
        top, left = (k // halves) * height, (k % halves) * width
        out_ref[k] = sums[top : top + height, left : left + width]


def bias_kernel(order_ref, lang_ref, cot_ref, out_ref, cot_scr):
    to_forward(order_ref, cot_ref, cot_scr)
    langs = out_ref.shape[0] * out_ref.shape[1] * out_ref.shape[2] // cot_scr.shape[1]
    put_pieces(out_ref, jnp.dot(members(lang_ref, langs), cot_scr[...], preferred_element_type=f32))


def sums_kernel(order_ref, first_ref, lang_ref, recv_ref, emb_ref, cot_ref, gain_ref, out_ref, x_ref, cot_scr, gain_scr):
    to_forward(order_ref, cot_ref, cot_scr)
    tokens = cot_scr.shape[0]
    gain_scr[...] = jnp.dot(selector(lang_ref, gain_ref.shape[1]), gain_ref[0], preferred_element_type=f32).astype(bf16)

    @pl.when(first_ref[0] == 1)
    def _():
        x_ref[...] = emb_ref[...]

    @pl.when(first_ref[0] != 1)
    def _():
        x_ref[...] = recv_ref[0]

    step = 16
    for top in range(0, tokens, step):
        rows = slice(top, top + step)
        x = x_ref[rows, :].astype(f32)
        scaled = cot_scr[rows, :].astype(f32) * gain_scr[rows, :].astype(f32)
        lane = lax.broadcasted_iota(jnp.int32, (step, tokens), 1)
        tile = jnp.zeros((step, tokens), f32)
        for i, term in enumerate((x, x * x, scaled, scaled * x)):
            tile = jnp.where(lane == i, jnp.sum(term, axis=1, keepdims=True), tile)
        out_ref[rows, :] = tile


def flip_kernel(wide_ref, out_ref):
    out_ref[...] = jnp.transpose(wide_ref[...])[: out_ref.shape[0], :]


def columns(sums_ref):
    tokens = sums_ref.shape[1]
    one, two, cot, cross = (sums_ref[i : i + 1, :] for i in range(4))
    center = one / D
    inv = lax.rsqrt(two / D - center * center + eps)
    mean_cross = inv * (cross - center * cot) / D
    row = lax.broadcasted_iota(jnp.int32, (tokens, tokens), 0)
    tile = jnp.where(row == 0, center, jnp.where(row == 1, inv, jnp.where(row == 2, cot / D, mean_cross)))
    return jnp.transpose(tile)


def gain_kernel(order_ref, lang_ref, sums_ref, x_ref, cot_ref, out_ref, cot_scr, high_scr, low_scr):
    to_forward(order_ref, cot_ref, cot_scr)
    langs = out_ref.shape[0] * out_ref.shape[1] * out_ref.shape[2] // cot_scr.shape[1]
    tokens, step = cot_scr.shape[0], 16
    figures = columns(sums_ref)
    for top in range(0, tokens, step):
        rows = slice(top, top + step)
        center, inv = figures[rows, 0:1], figures[rows, 1:2]
        product = cot_scr[rows, :].astype(f32) * ((x_ref[rows, :].astype(f32) - center) * inv)
        high = product.astype(bf16)
        high_scr[rows, :] = high
        low_scr[rows, :] = (product - high.astype(f32)).astype(bf16)
    who = members(lang_ref, langs)
    sums = jnp.dot(who, high_scr[...], preferred_element_type=f32) + jnp.dot(
        who, low_scr[...], preferred_element_type=f32
    )
    put_pieces(out_ref, sums)


def outs_kernel(
    order_ref, lang_ref, sums_ref, x_ref, cot_ref, res_ref, gain_ref, bias_ref, normed_ref, back_ref, fig_scr, gain_scr, bias_scr
):
    pick = selector(lang_ref, gain_ref.shape[1])
    gain_scr[...] = jnp.dot(pick, gain_ref[0], preferred_element_type=f32).astype(bf16)
    bias_scr[...] = jnp.dot(pick, bias_ref[0], preferred_element_type=f32).astype(bf16)
    fig_scr[...] = columns(sums_ref)
    tokens = x_ref.shape[0]
    rows, step = tokens // MB, 16
    for j in range(MB):
        for part in range(0, rows, step):
            here = pl.ds(pl.multiple_of(order_ref[0, j] * rows + part, step), step)
            slot = slice(j * rows + part, j * rows + part + step)
            fig = fig_scr[here, :]
            center, inv, mean_cot, mean_cross = (fig[:, i : i + 1] for i in range(4))
            normalized = (x_ref[here, :].astype(f32) - center) * inv
            gains = gain_scr[here, :].astype(f32)
            scaled = cot_ref[0, slot, :].astype(f32) * gains
            back_ref[0, slot, :] = (
                res_ref[0, slot, :].astype(f32) + inv * (scaled - mean_cot - normalized * mean_cross)
            ).astype(bf16)
            normed_ref[0, here, :] = (normalized * gains + bias_scr[here, :].astype(f32)).astype(bf16)


def add_kernel(parts_ref, out_ref):
    total = parts_ref[0]
    for k in range(1, parts_ref.shape[0]):
        total = total + parts_ref[k]
    for k in range(out_ref.shape[0]):
        out_ref[k] = total


def whole_kernel(parts_ref, out_ref):
    pieces, height, width = parts_ref.shape
    halves = out_ref.shape[2] // width
    for k in range(pieces):
        top, left = (k // halves) * height, (k % halves) * width
        out_ref[0, top : top + height, left : left + width] = parts_ref[k]


def shape(dims, kind):
    return jax.ShapeDtypeStruct(dims, kind)


def summed_over(pieces, axis):
    mine = lax.all_to_all(pieces, axis, 0, 0)
    total = call(add_kernel, "add_parts", shape(pieces.shape, f32), [], [VMEM], mine)
    return lax.all_to_all(total, axis, 0, 0)


def local(section_out, embedded, cot_norm, cot_res, gain, bias, lang_ids, mb_order):
    tokens, width = embedded.shape
    langs = gain.shape[1]
    replicas = lax.axis_size("dp")
    pieces = (replicas, 8, langs * width // (8 * replicas))
    lang = lang_ids.reshape(1, tokens)
    first = (lax.axis_index("pipe") == 0).astype(jnp.int32).reshape(1)
    stages = lax.axis_size("pipe")
    received = lax.ppermute(section_out, "pipe", [(i, i + 1) for i in range(stages - 1)])

    bias_part = call(
        bias_kernel, "bias_part", shape(pieces, f32), [pltpu.VMEM((tokens, width), bf16)], [SMEM, VMEM, VMEM], mb_order, lang, cot_norm
    )
    bias_all = summed_over(bias_part, "dp")

    wide, x = call(
        sums_kernel,
        "token_sums",
        (shape((tokens, tokens), f32), shape((tokens, width), bf16)),
        [pltpu.VMEM((tokens, width), bf16), pltpu.VMEM((tokens, width), bf16)],
        [SMEM, SMEM, VMEM, VMEM, VMEM, VMEM, VMEM],
        mb_order, first, lang, received, embedded, cot_norm, gain,
    )
    sums = call(flip_kernel, "flip", shape((8, tokens), f32), [], [VMEM], wide)
    sums = lax.psum(lax.psum(sums, "core"), "far")

    gain_part = call(
        gain_kernel,
        "gain_part",
        shape(pieces, f32),
        [pltpu.VMEM((tokens, width), bf16)] * 3,
        [SMEM, VMEM, VMEM, VMEM, VMEM],
        mb_order, lang, sums, x, cot_norm,
    )
    gain_all = summed_over(gain_part, "dp")
    normed, back = call(
        outs_kernel,
        "norm_and_grad",
        (shape((1, tokens, width), bf16), shape((1, tokens, width), bf16)),
        [pltpu.VMEM((tokens, tokens), f32), pltpu.VMEM((tokens, width), bf16), pltpu.VMEM((tokens, width), bf16)],
        [SMEM, VMEM, VMEM, VMEM, VMEM, VMEM, VMEM, VMEM],
        mb_order, lang, sums, x, cot_norm, cot_res, gain, bias,
    )
    returned = lax.ppermute(back, "pipe", [(i, (i - 1) % stages) for i in range(stages)])
    grads = shape((1, langs, width), f32)
    gain_grad = call(whole_kernel, "gain_whole", grads, [], [VMEM], gain_all)
    bias_grad = call(whole_kernel, "bias_whole", grads, [], [VMEM], bias_all)
    return normed, returned, gain_grad, bias_grad


def solution(mesh):
    dp, pipe, tensor = (mesh.shape[a] for a in ("dp", "pipe", "tensor"))
    split = Mesh(mesh.devices.reshape(dp, pipe, tensor // CORES, CORES), ("dp", "pipe", "far", "core"))
    tensor = ("far", "core")
    return jax.shard_map(
        local,
        mesh=split,
        in_specs=(
            P("pipe", "dp", tensor),
            P("dp", tensor),
            P("pipe", "dp", tensor),
            P("pipe", "dp", tensor),
            P("pipe", None, tensor),
            P("pipe", None, tensor),
            P("dp"),
            P("dp", None),
        ),
        out_specs=(
            P("pipe", "dp", tensor),
            P("pipe", "dp", tensor),
            P("pipe", None, tensor),
            P("pipe", None, tensor),
        ),
        check_vma=False,
    )
```

time: 228 us -> 106 us (0.46)
  waiting for transfers between devices: 152 us -> 42.9 us
  blocking collectives: 45.9 us -> 21 us
  starting transfers between devices: 4.2 us -> 28.2 us
  between operations: 14.2 us -> 0.74 us
  Pallas kernels: 0 us -> 10 us
  matrix products: 3.23 us -> 0 us
  other arithmetic: 3.06 us -> 0 us
    psum x1 -> x0, waiting for transfers between devices: 135 us -> none  [local(): summed = lax.psum(local_sums, 'dp')]
    psum x2, blocking collectives: 45.9 us -> 21 us  [local(): sums = lax.psum(lax.psum(sums, 'core'), 'far')]
    all_to_all x0 -> x4, starting transfers between devices: none -> 24.2 us  [the longest x2 16.1 us: summed_over(): mine = lax.all_to_all(pieces, axis, 0, 0)]
    all_to_all x0 -> x4, waiting for transfers between devices: none -> 21.9 us  [the longest x2 11.2 us: summed_over(): return lax.all_to_all(total, axis, 0, 0)]
    pallas_call x0 -> x9, Pallas kernels: none -> 10 us  [call(): pl.pallas_call(kernel, name=name, out_shape=outs, in_specs=in_specs, out_...]
    ppermute x2, waiting for transfers between devices: 17.3 us -> 21 us  [the longest x1 11.2 us: local(): lax.ppermute(section_out, 'pipe', [(i, i + 1) for i in range(stages - 1)])]
    dot_general x3 -> x0, matrix products: 3.23 us -> none  [the longest x1 1.68 us: local(): jnp.dot(matches.astype(jnp.float32).T, products, precision=lax.Precision....]
  transfers between devices with their start and end apart: 3 -> 6, of which waited for: 3 -> 4; matrix products, arithmetic and copies ran while one was open for 2% -> 0% of each run, Pallas kernels for 0% -> 7%
where the time goes in v1:
time: 106 us; the launch traced here: 105 us
  waiting for transfers between devices  42.9 us (40%)
  starting transfers between devices  28.2 us (27%)
  blocking collectives  21 us (20%)
  Pallas kernels  10 us (9%)
  local copies, waits for them, and re-layouts  2.42 us (2%)
    psum x2, blocking collectives, local(): sums = lax.psum(lax.psum(sums, 'core'), 'far')  21 us
    all_to_all x2, starting transfers between devices, summed_over(): mine = lax.all_to_all(pieces, axis, 0, 0)  16.1 us
    all_to_all x2, waiting for transfers between devices, summed_over(): return lax.all_to_all(total, axis, 0, 0)  11.2 us
    ppermute x1, waiting for transfers between devices, local(): lax.ppermute(section_out, 'pipe', [(i, i + 1) for i in range(stages - 1)])  11.2 us
    all_to_all x2, waiting for transfers between devices, summed_over(): mine = lax.all_to_all(pieces, axis, 0, 0)  10.7 us
    pallas_call x9, Pallas kernels, call(): pl.pallas_call(kernel, name=name, out_shape=outs, in_specs=in_specs, out_...  10 us
    ppermute x1, waiting for transfers between devices, local(): lax.ppermute(back, 'pipe', [(i, (i - 1) % stages) for i in range(stages)])  9.81 us
    all_to_all x2, starting transfers between devices, summed_over(): return lax.all_to_all(total, axis, 0, 0)  8.03 us
  transfers between devices with their start and end apart: 6, of which 4 were waited for; matrix products, arithmetic and copies ran while one was open for 0% of the time, Pallas kernels for 7%

profile of v1, /device:TPU:6, one launch (start us, length us, event | category | flops | bytes accessed | tf_op | source)
XLA Modules:
  0.0 105.3 jit_solution(7167755535069314017)
XLA Ops:
  0.6 0.0 copy-start.6
  0.6 0.0 copy-start.7
  0.7 0.6 copy-done.6
  1.3 0.0 copy-done.7
  1.3 0.0 copy-start
  1.3 1.0 copy-done
  2.3 0.0 copy-start.8
  2.3 0.0 copy-start.3
  2.3 1.5 %bias_part.1 = f32[16,8,768]{2,1,0:T(8,128)} custom-call(s32[1,4]{1,0:T(1,128)S(1)} %copy-done.6, s32[1,128]{1,0:T(1,128)S(1)} %bitcast.2, bf16[1,128,1536]{2,1,0:T(8,128)(2,1)S(1)} %copy-done), custom_call_target="tpu_custom_call" | custom-call | tf_op jit(solution)/shard_map/bias_part/pallas_call | solution.py:19
  3.8 0.0 copy-start.1
  3.8 0.0 copy-start.2
  3.8 8.8 %all-to-all-start.2 = ((f32[16,8,768]{2,1,0:T(8,128)}), f32[16,8,768]{2,1,0:T(8,128)S(1)}, u32[]{:S(2)}, u32[]{:S(2)}) async-start(f32[16,8,768]{2,1,0:T(8,128)} %bias_part.1), calls=%async_computation.2 | async-start | bytes 786432 | tf_op jit(solution)/shard_map/all_to_all | solution.py:171
  12.6 0.0 copy-done.8
  12.6 1.3 %collective-permute-start = (bf16[1,128,1536]{2,1,0:T(8,128)(2,1)S(1)}, bf16[1,128,1536]{2,1,0:T(8,128)(2,1)S(1)}, u32[]{:S(2)}, u32[]{:S(2)}) collective-permute-start(bf16[1,128,1536]{2,1,0:T(8,128)(2,1)S(1)} %copy-done.8), channel_id=1, source_target_pairs={{0,8},{8,16},{16,24},{1,9},{9,17},{17,25},{2,10},{10,18},{18,26},{... | collective-permute-start | bytes 1179656 | tf_op jit(solution)/shard_map/ppermute | solution.py:184
  13.9 11.2 %collective-permute-done.recv_ref = bf16[1,128,1536]{2,1,0:T(8,128)(2,1)S(1)} collective-permute-done((bf16[1,128,1536]{2,1,0:T(8,128)(2,1)S(1)}, bf16[1,128,1536]{2,1,0:T(8,128)(2,1)S(1)}, u32[]{:S(2)}, u32[]{:S(2)}) %collective-permute-start) | collective-permute-done | bytes 393248 | tf_op jit(solution)/shard_map/ppermute | solution.py:184
  25.1 0.0 copy-done.3
  25.1 0.0 copy-done.1
  25.1 0.0 copy-done.2
  25.1 1.2 %token_sums.1 = (f32[128,128]{1,0:T(8,128)S(1)}, bf16[128,1536]{1,0:T(8,128)(2,1)S(1)}) custom-call(s32[1,4]{1,0:T(1,128)S(1)} %copy-done.6, s32[1]{0:T(128)} %bitcast.1.first_ref, s32[1,128]{1,0:T(1,128)S(1)} %bitcast.3, bf16[1,128,1536]{2,1,0:T(8,128)(2,1)S(1)} %collective-permute-done.recv_ref, bf16[128,1536]{1,0:T(8,128)(2,1)S(1)} %copy-done.3, ...), custom_call_target="tpu_custom_call" | custom-call | tf_op jit(solution)/shard_map/token_sums/pallas_call | solution.py:19
  26.4 2.5 %psum.14 = f32[8,128]{1,0:T(8,128)S(1)} all-reduce(f32[8,128]{1,0:T(8,128)S(1)} %flip.1), channel_id=1, replica_groups=mesh['dp'=16,'pipe'=4,'far'=4,'core'=2] {'core'}, use_global_device_ids=true, to_apply=%region_0.0 | all-reduce | flops 1024 | bytes 8192 | tf_op jit(solution)/shard_map/psum | solution.py:200
  28.9 18.5 %psum.15.sums_ref = f32[8,128]{1,0:T(8,128)S(1)} all-reduce(f32[8,128]{1,0:T(8,128)S(1)} %psum.14), channel_id=1, replica_groups=mesh['dp'=16,'pipe'=4,'far'=4,'core'=2] {'far'}, use_global_device_ids=true, to_apply=%region_1.0 | all-reduce | flops 1024 | bytes 8192 | tf_op jit(solution)/shard_map/psum | solution.py:200
  47.4 1.9 %gain_part.1 = f32[16,8,768]{2,1,0:T(8,128)} custom-call(s32[1,4]{1,0:T(1,128)S(1)} %copy-done.6, s32[1,128]{1,0:T(1,128)S(1)} %bitcast.4, f32[8,128]{1,0:T(8,128)S(1)} %psum.15.sums_ref, bf16[128,1536]{1,0:T(8,128)(2,1)S(1)} %get-tuple-element.9.x_ref, bf16[1,128,1536]{2,1,0:T(8,128)(2,1)S(1)} %copy-done.1), custom_call_target="tpu_custom_call" | custom-call | tf_op jit(solution)/shard_map/gain_part/pallas_call | solution.py:19
  49.2 0.0 all-to-all-done.2.parts_ref
  49.2 7.4 %all-to-all-start = ((f32[16,8,768]{2,1,0:T(8,128)}), f32[16,8,768]{2,1,0:T(8,128)S(1)}, u32[]{:S(2)}, u32[]{:S(2)}) async-start(f32[16,8,768]{2,1,0:T(8,128)} %gain_part.1), calls=%async_computation | async-start | bytes 786432 | tf_op jit(solution)/shard_map/all_to_all | solution.py:171
  56.6 0.8 add_parts.3
  57.4 10.7 %all-to-all-done.parts_ref = f32[16,8,768]{2,1,0:T(8,128)S(1)} async-done(((f32[16,8,768]{2,1,0:T(8,128)}), f32[16,8,768]{2,1,0:T(8,128)S(1)}, u32[]{:S(2)}, u32[]{:S(2)}) %all-to-all-start) | async-done | bytes 393248 | tf_op jit(solution)/shard_map/all_to_all | solution.py:171
  68.1 4.0 %all-to-all-start.3 = ((f32[16,8,768]{2,1,0:T(8,128)}), f32[16,8,768]{2,1,0:T(8,128)S(1)}, u32[]{:S(2)}, u32[]{:S(2)}) async-start(f32[16,8,768]{2,1,0:T(8,128)} %add_parts.3), calls=%async_computation.3 | async-start | bytes 786432 | tf_op jit(solution)/shard_map/all_to_all | solution.py:173
  72.1 0.8 add_parts.2
  72.9 0.0 copy-start.4
  72.9 0.0 copy-start.5
  72.9 11.2 %all-to-all-done.3.parts_ref = f32[16,8,768]{2,1,0:T(8,128)S(1)} async-done(((f32[16,8,768]{2,1,0:T(8,128)}), f32[16,8,768]{2,1,0:T(8,128)S(1)}, u32[]{:S(2)}, u32[]{:S(2)}) %all-to-all-start.3) | async-done | bytes 393248 | tf_op jit(solution)/shard_map/all_to_all | solution.py:173
  84.1 4.0 %all-to-all-start.1 = ((f32[16,8,768]{2,1,0:T(8,128)}), f32[16,8,768]{2,1,0:T(8,128)S(1)}, u32[]{:S(2)}, u32[]{:S(2)}) async-start(f32[16,8,768]{2,1,0:T(8,128)} %add_parts.2), calls=%async_computation.1 | async-start | bytes 786432 | tf_op jit(solution)/shard_map/all_to_all | solution.py:173
  88.2 0.0 copy-done.4
  88.2 0.0 copy-done.5
  88.2 2.2 %norm_and_grad.1 = (bf16[1,128,1536]{2,1,0:T(8,128)(2,1)}, bf16[1,128,1536]{2,1,0:T(8,128)(2,1)S(1)}) custom-call(s32[1,4]{1,0:T(1,128)S(1)} %copy-done.6, s32[1,128]{1,0:T(1,128)S(1)} %bitcast.5, f32[8,128]{1,0:T(8,128)S(1)} %psum.15.sums_ref, bf16[128,1536]{1,0:T(8,128)(2,1)S(1)} %get-tuple-element.9.x_ref, bf16[1,128,1536]{2,1,0:T(8,128)(2,1)S(1)} %copy-done.1, ...), custom_call_target="tpu_custom_call" | custom-call | tf_op jit(solution)/shard_map/norm_and_grad/pallas_call | solution.py:19
  90.4 2.7 %collective-permute-start.1 = (bf16[1,128,1536]{2,1,0:T(8,128)(2,1)S(1)}, bf16[1,128,1536]{2,1,0:T(8,128)(2,1)S(1)}, u32[]{:S(2)}, u32[]{:S(2)}) collective-permute-start(bf16[1,128,1536]{2,1,0:T(8,128)(2,1)S(1)} %get-tuple-element.11), channel_id=1, source_target_pairs={{0,24},{8,0},{16,8},{24,16},{1,25},{9,1},{17,9},{25,17},{2,26},{10... | collective-permute-start | bytes 1179656 | tf_op jit(solution)/shard_map/ppermute | solution.py:219
  93.2 9.8 %collective-permute-done.1 = bf16[1,128,1536]{2,1,0:T(8,128)(2,1)S(1)} collective-permute-done((bf16[1,128,1536]{2,1,0:T(8,128)(2,1)S(1)}, bf16[1,128,1536]{2,1,0:T(8,128)(2,1)S(1)}, u32[]{:S(2)}, u32[]{:S(2)}) %collective-permute-start.1) | collective-permute-done | bytes 393248 | tf_op jit(solution)/shard_map/ppermute | solution.py:219
  103.0 0.8 bias_whole.1
  103.8 0.0 all-to-all-done.1.parts_ref
  103.8 0.8 gain_whole.1
  104.5 0.7 copy.13
  (1 shorter events, 0.0 us)
Async XLA Ops:
  0.6 0.7 copy-start.6
  0.6 0.7 copy-start.7
  1.3 1.0 copy-start
  2.3 10.3 %copy-start.8 = (bf16[1,128,1536]{2,1,0:T(8,128)(2,1)S(1)}, bf16[1,128,1536]{2,1,0:T(8,128)(2,1)}, u32[]{:S(2)}) copy-start(bf16[1,128,1536]{2,1,0:T(8,128)(2,1)} %param.8) | copy-start | bytes 1179652
  2.3 22.8 %copy-start.3 = (bf16[128,1536]{1,0:T(8,128)(2,1)S(1)}, bf16[128,1536]{1,0:T(8,128)(2,1)}, u32[]{:S(2)}) copy-start(bf16[128,1536]{1,0:T(8,128)(2,1)} %emb_ref.1) | copy-start | bytes 1179652
  3.8 21.3 %copy-start.1 = (bf16[1,128,1536]{2,1,0:T(8,128)(2,1)S(1)}, bf16[1,128,1536]{2,1,0:T(8,128)(2,1)}, u32[]{:S(2)}) copy-start(bf16[1,128,1536]{2,1,0:T(8,128)(2,1)} %cot_ref.7) | copy-start | bytes 1179652
  3.8 21.3 %copy-start.2 = (bf16[1,64,1536]{2,1,0:T(8,128)(2,1)S(1)}, bf16[1,64,1536]{2,1,0:T(8,128)(2,1)}, u32[]{:S(2)}) copy-start(bf16[1,64,1536]{2,1,0:T(8,128)(2,1)} %gain_ref.3) | copy-start | bytes 589828
  3.8 45.4 %all-to-all-start.2 = ((f32[16,8,768]{2,1,0:T(8,128)}), f32[16,8,768]{2,1,0:T(8,128)S(1)}, u32[]{:S(2)}, u32[]{:S(2)}) async-start(f32[16,8,768]{2,1,0:T(8,128)} %bias_part.1), calls=%async_computation.2 | async-start | bytes 786432 | tf_op jit(solution)/shard_map/all_to_all | solution.py:171
  12.6 12.5 %collective-permute-start = (bf16[1,128,1536]{2,1,0:T(8,128)(2,1)S(1)}, bf16[1,128,1536]{2,1,0:T(8,128)(2,1)S(1)}, u32[]{:S(2)}, u32[]{:S(2)}) collective-permute-start(bf16[1,128,1536]{2,1,0:T(8,128)(2,1)S(1)} %copy-done.8), channel_id=1, source_target_pairs={{0,8},{8,16},{16,24},{1,9},{9,17},{17,25},{2,10},{10,18},{18,26},{... | collective-permute-start | bytes 1179656 | tf_op jit(solution)/shard_map/ppermute | solution.py:184
  49.2 18.9 %all-to-all-start = ((f32[16,8,768]{2,1,0:T(8,128)}), f32[16,8,768]{2,1,0:T(8,128)S(1)}, u32[]{:S(2)}, u32[]{:S(2)}) async-start(f32[16,8,768]{2,1,0:T(8,128)} %gain_part.1), calls=%async_computation | async-start | bytes 786432 | tf_op jit(solution)/shard_map/all_to_all | solution.py:171
  68.1 16.1 %all-to-all-start.3 = ((f32[16,8,768]{2,1,0:T(8,128)}), f32[16,8,768]{2,1,0:T(8,128)S(1)}, u32[]{:S(2)}, u32[]{:S(2)}) async-start(f32[16,8,768]{2,1,0:T(8,128)} %add_parts.3), calls=%async_computation.3 | async-start | bytes 786432 | tf_op jit(solution)/shard_map/all_to_all | solution.py:173
  72.9 15.3 %copy-start.4 = (bf16[1,128,1536]{2,1,0:T(8,128)(2,1)S(1)}, bf16[1,128,1536]{2,1,0:T(8,128)(2,1)}, u32[]{:S(2)}) copy-start(bf16[1,128,1536]{2,1,0:T(8,128)(2,1)} %res_ref.1) | copy-start | bytes 1179652
  72.9 15.3 %copy-start.5 = (bf16[1,64,1536]{2,1,0:T(8,128)(2,1)S(1)}, bf16[1,64,1536]{2,1,0:T(8,128)(2,1)}, u32[]{:S(2)}) copy-start(bf16[1,64,1536]{2,1,0:T(8,128)(2,1)} %bias_ref.1) | copy-start | bytes 589828
  84.1 19.6 %all-to-all-start.1 = ((f32[16,8,768]{2,1,0:T(8,128)}), f32[16,8,768]{2,1,0:T(8,128)S(1)}, u32[]{:S(2)}, u32[]{:S(2)}) async-start(f32[16,8,768]{2,1,0:T(8,128)} %add_parts.2), calls=%async_computation.1 | async-start | bytes 786432 | tf_op jit(solution)/shard_map/all_to_all | solution.py:173
  90.4 12.6 %collective-permute-start.1 = (bf16[1,128,1536]{2,1,0:T(8,128)(2,1)S(1)}, bf16[1,128,1536]{2,1,0:T(8,128)(2,1)S(1)}, u32[]{:S(2)}, u32[]{:S(2)}) collective-permute-start(bf16[1,128,1536]{2,1,0:T(8,128)(2,1)S(1)} %get-tuple-element.11), channel_id=1, source_target_pairs={{0,24},{8,0},{16,8},{24,16},{1,25},{9,1},{17,9},{25,17},{2,26},{10... | collective-permute-start | bytes 1179656 | tf_op jit(solution)/shard_map/ppermute | solution.py:219

commit v2 on v1

--- a/solution.py
+++ b/solution.py
@@ -147,30 +147,32 @@
             normed_ref[0, here, :] = (normalized * gains + bias_scr[here, :].astype(f32)).astype(bf16)
 
 
-def add_kernel(parts_ref, out_ref):
-    total = parts_ref[0]
-    for k in range(1, parts_ref.shape[0]):
-        total = total + parts_ref[k]
-    for k in range(out_ref.shape[0]):
-        out_ref[k] = total
-
-
-def whole_kernel(parts_ref, out_ref):
+def add_kernel(gain_ref, bias_ref, out_ref):
+    height = gain_ref.shape[1]
+    for half, parts_ref in enumerate((gain_ref, bias_ref)):
+        total = parts_ref[0]
+        for k in range(1, parts_ref.shape[0]):
+            total = total + parts_ref[k]
+        for k in range(out_ref.shape[0]):
+            out_ref[k, half * height : (half + 1) * height, :] = total
+
+
+def whole_kernel(parts_ref, gain_ref, bias_ref):
     pieces, height, width = parts_ref.shape
-    halves = out_ref.shape[2] // width
+    height //= 2
+    halves = gain_ref.shape[2] // width
     for k in range(pieces):
         top, left = (k // halves) * height, (k % halves) * width
-        out_ref[0, top : top + height, left : left + width] = parts_ref[k]
+        gain_ref[0, top : top + height, left : left + width] = parts_ref[k, :height, :]
+        bias_ref[0, top : top + height, left : left + width] = parts_ref[k, height:, :]
 
 
 def shape(dims, kind):
     return jax.ShapeDtypeStruct(dims, kind)
 
 
-def summed_over(pieces, axis):
-    mine = lax.all_to_all(pieces, axis, 0, 0)
-    total = call(add_kernel, "add_parts", shape(pieces.shape, f32), [], [VMEM], mine)
-    return lax.all_to_all(total, axis, 0, 0)
+def exchanged(pieces):
+    return lax.all_to_all(pieces, "dp", 0, 0)
 
 
 def local(section_out, embedded, cot_norm, cot_res, gain, bias, lang_ids, mb_order):
@@ -184,9 +186,11 @@
     received = lax.ppermute(section_out, "pipe", [(i, i + 1) for i in range(stages - 1)])
 
     bias_part = call(
-        bias_kernel, "bias_part", shape(pieces, f32), [pltpu.VMEM((tokens, width), bf16)], [SMEM, VMEM, VMEM], mb_order, lang, cot_norm
-    )
-    bias_all = summed_over(bias_part, "dp")
+        bias_kernel, "bias_part", shape(pieces, f32), [pltpu.VMEM((tokens, width), bf16)], [SMEM, VMEM, VMEM], mb_order, lang, cot_norm,
+
+    )
+    received, bias_part = lax.optimization_barrier((received, bias_part))
+    bias_mine = exchanged(bias_part)
 
     wide, x = call(
         sums_kernel,
@@ -195,9 +199,11 @@
         [pltpu.VMEM((tokens, width), bf16), pltpu.VMEM((tokens, width), bf16)],
         [SMEM, SMEM, VMEM, VMEM, VMEM, VMEM, VMEM],
         mb_order, first, lang, received, embedded, cot_norm, gain,
+
     )
     sums = call(flip_kernel, "flip", shape((8, tokens), f32), [], [VMEM], wide)
     sums = lax.psum(lax.psum(sums, "core"), "far")
+    sums, bias_mine = lax.optimization_barrier((sums, bias_mine))
 
     gain_part = call(
         gain_kernel,
@@ -207,7 +213,7 @@
         [SMEM, VMEM, VMEM, VMEM, VMEM],
         mb_order, lang, sums, x, cot_norm,
     )
-    gain_all = summed_over(gain_part, "dp")
+    gain_mine = exchanged(gain_part)
     normed, back = call(
         outs_kernel,
         "norm_and_grad",
@@ -217,9 +223,11 @@
         mb_order, lang, sums, x, cot_norm, cot_res, gain, bias,
     )
     returned = lax.ppermute(back, "pipe", [(i, (i - 1) % stages) for i in range(stages)])
+    gain_mine, back = lax.optimization_barrier((gain_mine, back))
+    both = shape((pieces[0], 2 * pieces[1], pieces[2]), f32)
+    totals = exchanged(call(add_kernel, "add_parts", both, [], [VMEM, VMEM], gain_mine, bias_mine))
     grads = shape((1, langs, width), f32)
-    gain_grad = call(whole_kernel, "gain_whole", grads, [], [VMEM], gain_all)
-    bias_grad = call(whole_kernel, "bias_whole", grads, [], [VMEM], bias_all)
+    gain_grad, bias_grad = call(whole_kernel, "whole_grads", (grads, grads), [], [VMEM], totals)
     return normed, returned, gain_grad, bias_grad
 
 

time: 106 us -> 92.2 us (0.87)
  waiting for transfers between devices: 42.9 us -> 34.5 us
  starting transfers between devices: 28.2 us -> 24.6 us
  Pallas kernels: 10 us -> 8.82 us
    all_to_all x4 -> x3, waiting for transfers between devices: 21.9 us -> 15.6 us  [exchanged(): return lax.all_to_all(pieces, 'dp', 0, 0)]
    all_to_all x4 -> x3, starting transfers between devices: 24.2 us -> 20.4 us  [exchanged(): return lax.all_to_all(pieces, 'dp', 0, 0)]
    ppermute x1, waiting for transfers between devices: 11.2 us -> 9.12 us  [local(): lax.ppermute(section_out, 'pipe', [(i, i + 1) for i in range(stages - 1)])]
    pallas_call x9 -> x7, Pallas kernels: 10 us -> 8.82 us  [call(): pl.pallas_call(kernel, name=name, out_shape=outs, in_specs=in_specs, out_...]
    unnamed x19 -> x17, local copies, waits for them, and re-layouts: 2.42 us -> 1.76 us
  transfers between devices with their start and end apart: 6 -> 5, of which waited for: 4 -> 4; matrix products, arithmetic and copies ran while one was open for 0% -> 0% of each run, Pallas kernels for 7% -> 6%
where the time goes in v2:
time: 92.2 us; the launch traced here: 91.5 us
  waiting for transfers between devices  34.5 us (37%)
  starting transfers between devices  24.6 us (27%)
  blocking collectives  21 us (23%)
  Pallas kernels  8.82 us (10%)
  local copies, waits for them, and re-layouts  1.76 us (2%)
    psum x2, blocking collectives, local(): sums = lax.psum(lax.psum(sums, 'core'), 'far')  21 us
    all_to_all x3, starting transfers between devices, exchanged(): return lax.all_to_all(pieces, 'dp', 0, 0)  20.4 us
    all_to_all x3, waiting for transfers between devices, exchanged(): return lax.all_to_all(pieces, 'dp', 0, 0)  15.6 us
    ppermute x1, waiting for transfers between devices, local(): lax.ppermute(back, 'pipe', [(i, (i - 1) % stages) for i in range(stages)])  9.81 us
    ppermute x1, waiting for transfers between devices, local(): lax.ppermute(section_out, 'pipe', [(i, i + 1) for i in range(stages - 1)])  9.12 us
    pallas_call x7, Pallas kernels, call(): pl.pallas_call(kernel, name=name, out_shape=outs, in_specs=in_specs, out_...  8.82 us
    ppermute x1, starting transfers between devices, local(): lax.ppermute(back, 'pipe', [(i, (i - 1) % stages) for i in range(stages)])  2.74 us
  transfers between devices with their start and end apart: 5, of which 4 were waited for; matrix products, arithmetic and copies ran while one was open for 0% of the time, Pallas kernels for 6%

profile of v2, /device:TPU:6, one launch (start us, length us, event | category | flops | bytes accessed | tf_op | source)
XLA Modules:
  0.0 91.5 jit_solution(13020301849229510556)
XLA Ops:
  0.6 0.0 copy-start.6
  0.6 0.0 copy-start.7
  0.7 1.4 %collective-permute-start = (bf16[1,128,1536]{2,1,0:T(8,128)(2,1)}, bf16[1,128,1536]{2,1,0:T(8,128)(2,1)S(1)}, u32[]{:S(2)}, u32[]{:S(2)}) collective-permute-start(bf16[1,128,1536]{2,1,0:T(8,128)(2,1)} %param.8), channel_id=1, source_target_pairs={{0,8},{8,16},{16,24},{1,9},{9,17},{17,25},{2,10},{10,18},{18,26},{... | collective-permute-start | bytes 1179656 | tf_op jit(solution)/shard_map/ppermute | solution.py:186
  2.1 0.0 copy-done.6
  2.1 0.0 copy-done.7
  2.1 0.0 copy-start
  2.1 1.0 %copy-done = bf16[1,128,1536]{2,1,0:T(8,128)(2,1)S(1)} copy-done((bf16[1,128,1536]{2,1,0:T(8,128)(2,1)S(1)}, bf16[1,128,1536]{2,1,0:T(8,128)(2,1)}, u32[]{:S(2)}) %copy-start) | copy-done | bytes 393240
  3.1 0.0 copy-start.3
  3.1 1.5 %bias_part.1 = f32[16,8,768]{2,1,0:T(8,128)} custom-call(s32[1,4]{1,0:T(1,128)S(1)} %copy-done.6, s32[1,128]{1,0:T(1,128)S(1)} %bitcast.2, bf16[1,128,1536]{2,1,0:T(8,128)(2,1)S(1)} %copy-done), custom_call_target="tpu_custom_call" | custom-call | tf_op jit(solution)/shard_map/bias_part/pallas_call | solution.py:19
  4.6 0.0 copy-start.1
  4.6 0.0 copy-start.2
  4.6 9.1 %collective-permute-done.recv_ref = bf16[1,128,1536]{2,1,0:T(8,128)(2,1)S(1)} collective-permute-done((bf16[1,128,1536]{2,1,0:T(8,128)(2,1)}, bf16[1,128,1536]{2,1,0:T(8,128)(2,1)S(1)}, u32[]{:S(2)}, u32[]{:S(2)}) %collective-permute-start) | collective-permute-done | bytes 393248 | tf_op jit(solution)/shard_map/ppermute | solution.py:186
  13.7 8.6 %all-to-all-start = ((f32[16,8,768]{2,1,0:T(8,128)}), f32[16,8,768]{2,1,0:T(8,128)S(1)}, u32[]{:S(2)}, u32[]{:S(2)}) async-start(f32[16,8,768]{2,1,0:T(8,128)} %bias_part.1), calls=%async_computation | async-start | bytes 786432 | tf_op jit(solution)/shard_map/all_to_all | solution.py:175
  22.4 0.0 copy-done.3
  22.4 0.0 copy-done.1
  22.4 0.0 copy-done.2
  22.4 1.2 %token_sums.1 = (f32[128,128]{1,0:T(8,128)S(1)}, bf16[128,1536]{1,0:T(8,128)(2,1)S(1)}) custom-call(s32[1,4]{1,0:T(1,128)S(1)} %copy-done.6, s32[1]{0:T(128)} %bitcast.1.first_ref, s32[1,128]{1,0:T(1,128)S(1)} %bitcast.3, bf16[1,128,1536]{2,1,0:T(8,128)(2,1)S(1)} %collective-permute-done.recv_ref, bf16[128,1536]{1,0:T(8,128)(2,1)S(1)} %copy-done.3, ...), custom_call_target="tpu_custom_call" | custom-call | tf_op jit(solution)/shard_map/token_sums/pallas_call | solution.py:19
  23.7 2.5 %psum.14 = f32[8,128]{1,0:T(8,128)S(1)} all-reduce(f32[8,128]{1,0:T(8,128)S(1)} %flip.1), channel_id=1, replica_groups=mesh['dp'=16,'pipe'=4,'far'=4,'core'=2] {'core'}, use_global_device_ids=true, to_apply=%region_0.0 | all-reduce | flops 1024 | bytes 8192 | tf_op jit(solution)/shard_map/psum | solution.py:205
  26.2 18.5 %psum.15.sums_ref = f32[8,128]{1,0:T(8,128)S(1)} all-reduce(f32[8,128]{1,0:T(8,128)S(1)} %psum.14), channel_id=1, replica_groups=mesh['dp'=16,'pipe'=4,'far'=4,'core'=2] {'far'}, use_global_device_ids=true, to_apply=%region_1.0 | all-reduce | flops 1024 | bytes 8192 | tf_op jit(solution)/shard_map/psum | solution.py:205
  44.7 0.0 all-to-all-done.bias_ref
  44.7 1.9 %gain_part.1 = f32[16,8,768]{2,1,0:T(8,128)} custom-call(s32[1,4]{1,0:T(1,128)S(1)} %copy-done.6, s32[1,128]{1,0:T(1,128)S(1)} %bitcast.4, f32[8,128]{1,0:T(8,128)S(1)} %psum.15.sums_ref, bf16[128,1536]{1,0:T(8,128)(2,1)S(1)} %get-tuple-element.19.x_ref, bf16[1,128,1536]{2,1,0:T(8,128)(2,1)S(1)} %copy-done.1), custom_call_target="tpu_custom_call" | custom-call | tf_op jit(solution)/shard_map/gain_part/pallas_call | solution.py:19
  46.6 0.0 copy-start.4
  46.6 0.0 copy-start.5
  46.6 7.8 %all-to-all-start.1 = ((f32[16,8,768]{2,1,0:T(8,128)}), f32[16,8,768]{2,1,0:T(8,128)S(1)}, u32[]{:S(2)}, u32[]{:S(2)}) async-start(f32[16,8,768]{2,1,0:T(8,128)} %gain_part.1), calls=%async_computation.1 | async-start | bytes 786432 | tf_op jit(solution)/shard_map/all_to_all | solution.py:175
  54.4 0.0 copy-done.4
  54.4 0.0 copy-done.5
  54.4 2.3 %norm_and_grad.1 = (bf16[1,128,1536]{2,1,0:T(8,128)(2,1)}, bf16[1,128,1536]{2,1,0:T(8,128)(2,1)S(1)}) custom-call(s32[1,4]{1,0:T(1,128)S(1)} %copy-done.6, s32[1,128]{1,0:T(1,128)S(1)} %bitcast.5, f32[8,128]{1,0:T(8,128)S(1)} %psum.15.sums_ref, bf16[128,1536]{1,0:T(8,128)(2,1)S(1)} %get-tuple-element.19.x_ref, bf16[1,128,1536]{2,1,0:T(8,128)(2,1)S(1)} %copy-done.1, ...), custom_call_target="tpu_custom_call" | custom-call | tf_op jit(solution)/shard_map/norm_and_grad/pallas_call | solution.py:19
  56.6 9.2 %all-to-all-done.1.gain_ref = f32[16,8,768]{2,1,0:T(8,128)S(1)} async-done(((f32[16,8,768]{2,1,0:T(8,128)}), f32[16,8,768]{2,1,0:T(8,128)S(1)}, u32[]{:S(2)}, u32[]{:S(2)}) %all-to-all-start.1) | async-done | bytes 393248 | tf_op jit(solution)/shard_map/all_to_all | solution.py:175
  65.8 1.0 %add_parts.1 = f32[16,16,768]{2,1,0:T(8,128)} custom-call(f32[16,8,768]{2,1,0:T(8,128)S(1)} %all-to-all-done.1.gain_ref, f32[16,8,768]{2,1,0:T(8,128)S(1)} %all-to-all-done.bias_ref), custom_call_target="tpu_custom_call" | custom-call | tf_op jit(solution)/shard_map/add_parts/pallas_call | solution.py:19
  66.8 4.0 %all-to-all-start.2 = ((f32[16,16,768]{2,1,0:T(8,128)}), f32[16,16,768]{2,1,0:T(8,128)S(1)}, u32[]{:S(2)}, u32[]{:S(2)}) async-start(f32[16,16,768]{2,1,0:T(8,128)} %add_parts.1), calls=%async_computation.2 | async-start | bytes 1572864 | tf_op jit(solution)/shard_map/all_to_all | solution.py:175
  70.8 2.7 %collective-permute-start.1 = (bf16[1,128,1536]{2,1,0:T(8,128)(2,1)S(1)}, bf16[1,128,1536]{2,1,0:T(8,128)(2,1)S(1)}, u32[]{:S(2)}, u32[]{:S(2)}) collective-permute-start(bf16[1,128,1536]{2,1,0:T(8,128)(2,1)S(1)} %get-tuple-element.21), channel_id=1, source_target_pairs={{0,24},{8,0},{16,8},{24,16},{1,25},{9,1},{17,9},{25,17},{2,26},{10... | collective-permute-start | bytes 1179656 | tf_op jit(solution)/shard_map/ppermute | solution.py:225
  73.6 9.8 %collective-permute-done.1 = bf16[1,128,1536]{2,1,0:T(8,128)(2,1)S(1)} collective-permute-done((bf16[1,128,1536]{2,1,0:T(8,128)(2,1)S(1)}, bf16[1,128,1536]{2,1,0:T(8,128)(2,1)S(1)}, u32[]{:S(2)}, u32[]{:S(2)}) %collective-permute-start.1) | collective-permute-done | bytes 393248 | tf_op jit(solution)/shard_map/ppermute | solution.py:225
  83.4 6.4 %all-to-all-done.2.parts_ref = f32[16,16,768]{2,1,0:T(8,128)S(1)} async-done(((f32[16,16,768]{2,1,0:T(8,128)}), f32[16,16,768]{2,1,0:T(8,128)S(1)}, u32[]{:S(2)}, u32[]{:S(2)}) %all-to-all-start.2) | async-done | bytes 786464 | tf_op jit(solution)/shard_map/all_to_all | solution.py:175
  89.8 0.9 %whole_grads.1 = (f32[1,64,1536]{2,1,0:T(8,128)}, f32[1,64,1536]{2,1,0:T(8,128)}) custom-call(f32[16,16,768]{2,1,0:T(8,128)S(1)} %all-to-all-done.2.parts_ref), custom_call_target="tpu_custom_call" | custom-call | tf_op jit(solution)/shard_map/whole_grads/pallas_call | solution.py:19
  90.7 0.7 copy.13
  (1 shorter events, 0.0 us)
Async XLA Ops:
  0.6 1.5 %copy-start.6 = (s32[1,4]{1,0:T(1,128)S(1)}, s32[1,4]{1,0:T(1,128)}, u32[]{:S(2)}) copy-start(s32[1,4]{1,0:T(1,128)} %order_ref.7) | copy-start | bytes 52
  0.6 1.5 %copy-start.7 = (s32[128]{0:T(128)S(1)}, s32[128]{0:T(128)}, u32[]{:S(2)}) copy-start(s32[128]{0:T(128)} %param.14) | copy-start | bytes 1540
  0.7 13.1 %collective-permute-start = (bf16[1,128,1536]{2,1,0:T(8,128)(2,1)}, bf16[1,128,1536]{2,1,0:T(8,128)(2,1)S(1)}, u32[]{:S(2)}, u32[]{:S(2)}) collective-permute-start(bf16[1,128,1536]{2,1,0:T(8,128)(2,1)} %param.8), channel_id=1, source_target_pairs={{0,8},{8,16},{16,24},{1,9},{9,17},{17,25},{2,10},{10,18},{18,26},{... | collective-permute-start | bytes 1179656 | tf_op jit(solution)/shard_map/ppermute | solution.py:186
  2.1 1.0 %copy-start = (bf16[1,128,1536]{2,1,0:T(8,128)(2,1)S(1)}, bf16[1,128,1536]{2,1,0:T(8,128)(2,1)}, u32[]{:S(2)}) copy-start(bf16[1,128,1536]{2,1,0:T(8,128)(2,1)} %cot_ref.7) | copy-start | bytes 1179652
  3.1 19.3 %copy-start.3 = (bf16[128,1536]{1,0:T(8,128)(2,1)S(1)}, bf16[128,1536]{1,0:T(8,128)(2,1)}, u32[]{:S(2)}) copy-start(bf16[128,1536]{1,0:T(8,128)(2,1)} %emb_ref.1) | copy-start | bytes 1179652
  4.6 17.8 %copy-start.1 = (bf16[1,128,1536]{2,1,0:T(8,128)(2,1)S(1)}, bf16[1,128,1536]{2,1,0:T(8,128)(2,1)}, u32[]{:S(2)}) copy-start(bf16[1,128,1536]{2,1,0:T(8,128)(2,1)} %cot_ref.7) | copy-start | bytes 1179652
  4.6 17.8 %copy-start.2 = (bf16[1,64,1536]{2,1,0:T(8,128)(2,1)S(1)}, bf16[1,64,1536]{2,1,0:T(8,128)(2,1)}, u32[]{:S(2)}) copy-start(bf16[1,64,1536]{2,1,0:T(8,128)(2,1)} %gain_ref.3) | copy-start | bytes 589828
  13.7 31.0 %all-to-all-start = ((f32[16,8,768]{2,1,0:T(8,128)}), f32[16,8,768]{2,1,0:T(8,128)S(1)}, u32[]{:S(2)}, u32[]{:S(2)}) async-start(f32[16,8,768]{2,1,0:T(8,128)} %bias_part.1), calls=%async_computation | async-start | bytes 786432 | tf_op jit(solution)/shard_map/all_to_all | solution.py:175
  46.6 7.8 %copy-start.4 = (bf16[1,128,1536]{2,1,0:T(8,128)(2,1)S(1)}, bf16[1,128,1536]{2,1,0:T(8,128)(2,1)}, u32[]{:S(2)}) copy-start(bf16[1,128,1536]{2,1,0:T(8,128)(2,1)} %res_ref.1) | copy-start | bytes 1179652
  46.6 7.8 %copy-start.5 = (bf16[1,64,1536]{2,1,0:T(8,128)(2,1)S(1)}, bf16[1,64,1536]{2,1,0:T(8,128)(2,1)}, u32[]{:S(2)}) copy-start(bf16[1,64,1536]{2,1,0:T(8,128)(2,1)} %bias_ref.1) | copy-start | bytes 589828
  46.6 19.3 %all-to-all-start.1 = ((f32[16,8,768]{2,1,0:T(8,128)}), f32[16,8,768]{2,1,0:T(8,128)S(1)}, u32[]{:S(2)}, u32[]{:S(2)}) async-start(f32[16,8,768]{2,1,0:T(8,128)} %gain_part.1), calls=%async_computation.1 | async-start | bytes 786432 | tf_op jit(solution)/shard_map/all_to_all | solution.py:175
  66.8 23.0 %all-to-all-start.2 = ((f32[16,16,768]{2,1,0:T(8,128)}), f32[16,16,768]{2,1,0:T(8,128)S(1)}, u32[]{:S(2)}, u32[]{:S(2)}) async-start(f32[16,16,768]{2,1,0:T(8,128)} %add_parts.1), calls=%async_computation.2 | async-start | bytes 1572864 | tf_op jit(solution)/shard_map/all_to_all | solution.py:175
  70.8 12.6 %collective-permute-start.1 = (bf16[1,128,1536]{2,1,0:T(8,128)(2,1)S(1)}, bf16[1,128,1536]{2,1,0:T(8,128)(2,1)S(1)}, u32[]{:S(2)}, u32[]{:S(2)}) collective-permute-start(bf16[1,128,1536]{2,1,0:T(8,128)(2,1)S(1)} %get-tuple-element.21), channel_id=1, source_target_pairs={{0,24},{8,0},{16,8},{24,16},{1,25},{9,1},{17,9},{25,17},{2,26},{10... | collective-permute-start | bytes 1179656 | tf_op jit(solution)/shard_map/ppermute | solution.py:225

commit v3 on v2

--- a/solution.py
+++ b/solution.py
@@ -15,7 +15,7 @@
 SMEM = pl.BlockSpec(memory_space=pltpu.SMEM)
 
 
-def call(kernel, name, outs, scratch, in_specs, *args):
+def call(kernel, name, outs, scratch, in_specs, *args, cover=0):
     return pl.pallas_call(
         kernel,
         name=name,
@@ -23,6 +23,7 @@
         in_specs=in_specs,
         out_specs=jax.tree.map(lambda _: VMEM, outs),
         scratch_shapes=scratch,
+        cost_estimate=pl.CostEstimate(flops=cover, transcendentals=0, bytes_accessed=0) if cover else None,
         compiler_params=pltpu.CompilerParams(vmem_limit_bytes=40 * 1024 * 1024),
     )(*args)
 
@@ -189,8 +190,8 @@
         bias_kernel, "bias_part", shape(pieces, f32), [pltpu.VMEM((tokens, width), bf16)], [SMEM, VMEM, VMEM], mb_order, lang, cot_norm,
 
     )
+    bias_mine = exchanged(bias_part)
     received, bias_part = lax.optimization_barrier((received, bias_part))
-    bias_mine = exchanged(bias_part)
 
     wide, x = call(
         sums_kernel,
@@ -199,6 +200,7 @@
         [pltpu.VMEM((tokens, width), bf16), pltpu.VMEM((tokens, width), bf16)],
         [SMEM, SMEM, VMEM, VMEM, VMEM, VMEM, VMEM],
         mb_order, first, lang, received, embedded, cot_norm, gain,
+        cover=10**11,
 
     )
     sums = call(flip_kernel, "flip", shape((8, tokens), f32), [], [VMEM], wide)

time: 92.2 us -> 85.2 us (0.924)
  waiting for transfers between devices: 34.5 us -> 25.4 us
  blocking collectives: 21 us -> 23.7 us
  starting transfers between devices: 24.6 us -> 23.4 us
    ppermute x1, waiting for transfers between devices: 9.12 us -> 0.33 us  [local(): lax.ppermute(section_out, 'pipe', [(i, i + 1) for i in range(stages - 1)])]
    psum x2, blocking collectives: 21 us -> 23.7 us  [local(): sums = lax.psum(lax.psum(sums, 'core'), 'far')]
    all_to_all x3, starting transfers between devices: 20.4 us -> 18.8 us  [exchanged(): return lax.all_to_all(pieces, 'dp', 0, 0)]
where the time goes in v3:
time: 85.2 us; the launch traced here: 83.8 us
  waiting for transfers between devices  25.4 us (30%)
  blocking collectives  23.7 us (28%)
  starting transfers between devices  23.4 us (27%)
  Pallas kernels  8.83 us (10%)
  local copies, waits for them, and re-layouts  1.76 us (2%)
    psum x2, blocking collectives, local(): sums = lax.psum(lax.psum(sums, 'core'), 'far')  23.7 us
    all_to_all x3, starting transfers between devices, exchanged(): return lax.all_to_all(pieces, 'dp', 0, 0)  18.8 us
    all_to_all x3, waiting for transfers between devices, exchanged(): return lax.all_to_all(pieces, 'dp', 0, 0)  15.6 us
    ppermute x1, waiting for transfers between devices, local(): lax.ppermute(back, 'pipe', [(i, (i - 1) % stages) for i in range(stages)])  9.43 us
    pallas_call x7, Pallas kernels, call(): pl.pallas_call(kernel, name=name, out_shape=outs, in_specs=in_specs, out_...  8.83 us
    ppermute x1, starting transfers between devices, local(): lax.ppermute(back, 'pipe', [(i, (i - 1) % stages) for i in range(stages)])  3.13 us
    unnamed x17, local copies, waits for them, and re-layouts  1.76 us
  transfers between devices with their start and end apart: 5, of which 4 were waited for; matrix products, arithmetic and copies ran while one was open for 0% of the time, Pallas kernels for 6%

profile of v3, /device:TPU:6, one launch (start us, length us, event | category | flops | bytes accessed | tf_op | source)
XLA Modules:
  0.0 83.8 jit_solution(17482285443635347969)
XLA Ops:
  0.6 0.0 copy-start.5
  0.6 0.0 copy-start.6
  0.7 1.4 %collective-permute-start = (bf16[1,128,1536]{2,1,0:T(8,128)(2,1)}, bf16[1,128,1536]{2,1,0:T(8,128)(2,1)S(1)}, u32[]{:S(2)}, u32[]{:S(2)}) collective-permute-start(bf16[1,128,1536]{2,1,0:T(8,128)(2,1)} %param.8), channel_id=1, source_target_pairs={{0,8},{8,16},{16,24},{1,9},{9,17},{17,25},{2,10},{10,18},{18,26},{... | collective-permute-start | bytes 1179656 | tf_op jit(solution)/shard_map/ppermute | solution.py:187
  2.1 0.0 copy-done.5
  2.1 0.0 copy-done.6
  2.1 0.0 copy-start
  2.1 1.0 %copy-done = bf16[1,128,1536]{2,1,0:T(8,128)(2,1)S(1)} copy-done((bf16[1,128,1536]{2,1,0:T(8,128)(2,1)S(1)}, bf16[1,128,1536]{2,1,0:T(8,128)(2,1)}, u32[]{:S(2)}) %copy-start) | copy-done | bytes 393240
  3.1 0.0 copy-start.7
  3.1 1.5 %bias_part.1 = f32[16,8,768]{2,1,0:T(8,128)} custom-call(s32[1,4]{1,0:T(1,128)S(1)} %copy-done.5, s32[1,128]{1,0:T(1,128)S(1)} %bitcast.2, bf16[1,128,1536]{2,1,0:T(8,128)(2,1)S(1)} %copy-done), custom_call_target="tpu_custom_call" | custom-call | tf_op jit(solution)/shard_map/bias_part/pallas_call | solution.py:19
  4.6 0.0 copy-start.1
  4.6 0.0 copy-start.3
  4.6 8.8 %all-to-all-start = ((f32[16,8,768]{2,1,0:T(8,128)}), f32[16,8,768]{2,1,0:T(8,128)S(1)}, u32[]{:S(2)}, u32[]{:S(2)}) async-start(f32[16,8,768]{2,1,0:T(8,128)} %bias_part.1), calls=%async_computation | async-start | bytes 786432 | tf_op jit(solution)/shard_map/all_to_all | solution.py:176
  13.4 0.3 collective-permute-done.recv_ref
  13.7 0.0 copy-done.7
  13.7 0.0 copy-done.1
  13.7 0.0 copy-done.3
  13.8 1.2 %token_sums.1 = (f32[128,128]{1,0:T(8,128)S(1)}, bf16[128,1536]{1,0:T(8,128)(2,1)S(1)}) custom-call(s32[1,4]{1,0:T(1,128)S(1)} %copy-done.5, s32[1]{0:T(128)} %bitcast.1.first_ref, s32[1,128]{1,0:T(1,128)S(1)} %bitcast.3, bf16[1,128,1536]{2,1,0:T(8,128)(2,1)S(1)} %collective-permute-done.recv_ref, bf16[128,1536]{1,0:T(8,128)(2,1)S(1)} %copy-done.7, ...), custom_call_target="tpu_custom_call" | custom-call | flops 99999997952 | tf_op jit(solution)/shard_map/token_sums/pallas_call | solution.py:19
  15.0 2.5 %psum.14 = f32[8,128]{1,0:T(8,128)S(1)} all-reduce(f32[8,128]{1,0:T(8,128)S(1)} %flip.1), channel_id=1, replica_groups=mesh['dp'=16,'pipe'=4,'far'=4,'core'=2] {'core'}, use_global_device_ids=true, to_apply=%region_0.0 | all-reduce | flops 1024 | bytes 8192 | tf_op jit(solution)/shard_map/psum | solution.py:207
  17.5 21.2 %psum.15.sums_ref = f32[8,128]{1,0:T(8,128)S(1)} all-reduce(f32[8,128]{1,0:T(8,128)S(1)} %psum.14), channel_id=1, replica_groups=mesh['dp'=16,'pipe'=4,'far'=4,'core'=2] {'far'}, use_global_device_ids=true, to_apply=%region_1.0 | all-reduce | flops 1024 | bytes 8192 | tf_op jit(solution)/shard_map/psum | solution.py:207
  38.8 0.0 all-to-all-done.bias_ref
  38.8 1.9 %gain_part.1 = f32[16,8,768]{2,1,0:T(8,128)} custom-call(s32[1,4]{1,0:T(1,128)S(1)} %copy-done.5, s32[1,128]{1,0:T(1,128)S(1)} %bitcast.4, f32[8,128]{1,0:T(8,128)S(1)} %psum.15.sums_ref, bf16[128,1536]{1,0:T(8,128)(2,1)S(1)} %get-tuple-element.17.x_ref, bf16[1,128,1536]{2,1,0:T(8,128)(2,1)S(1)} %copy-done.1), custom_call_target="tpu_custom_call" | custom-call | tf_op jit(solution)/shard_map/gain_part/pallas_call | solution.py:19
  40.6 0.0 copy-start.2
  40.6 0.0 copy-start.4
  40.6 6.0 %all-to-all-start.1 = ((f32[16,8,768]{2,1,0:T(8,128)}), f32[16,8,768]{2,1,0:T(8,128)S(1)}, u32[]{:S(2)}, u32[]{:S(2)}) async-start(f32[16,8,768]{2,1,0:T(8,128)} %gain_part.1), calls=%async_computation.1 | async-start | bytes 786432 | tf_op jit(solution)/shard_map/all_to_all | solution.py:176
  46.7 0.0 copy-done.2
  46.7 0.0 copy-done.4
  46.7 2.2 %norm_and_grad.1 = (bf16[1,128,1536]{2,1,0:T(8,128)(2,1)}, bf16[1,128,1536]{2,1,0:T(8,128)(2,1)S(1)}) custom-call(s32[1,4]{1,0:T(1,128)S(1)} %copy-done.5, s32[1,128]{1,0:T(1,128)S(1)} %bitcast.5, f32[8,128]{1,0:T(8,128)S(1)} %psum.15.sums_ref, bf16[128,1536]{1,0:T(8,128)(2,1)S(1)} %get-tuple-element.17.x_ref, bf16[1,128,1536]{2,1,0:T(8,128)(2,1)S(1)} %copy-done.1, ...), custom_call_target="tpu_custom_call" | custom-call | tf_op jit(solution)/shard_map/norm_and_grad/pallas_call | solution.py:19
  48.9 9.2 %all-to-all-done.1.gain_ref = f32[16,8,768]{2,1,0:T(8,128)S(1)} async-done(((f32[16,8,768]{2,1,0:T(8,128)}), f32[16,8,768]{2,1,0:T(8,128)S(1)}, u32[]{:S(2)}, u32[]{:S(2)}) %all-to-all-start.1) | async-done | bytes 393248 | tf_op jit(solution)/shard_map/all_to_all | solution.py:176
  58.1 1.0 %add_parts.1 = f32[16,16,768]{2,1,0:T(8,128)} custom-call(f32[16,8,768]{2,1,0:T(8,128)S(1)} %all-to-all-done.1.gain_ref, f32[16,8,768]{2,1,0:T(8,128)S(1)} %all-to-all-done.bias_ref), custom_call_target="tpu_custom_call" | custom-call | tf_op jit(solution)/shard_map/add_parts/pallas_call | solution.py:19
  59.1 4.0 %all-to-all-start.2 = ((f32[16,16,768]{2,1,0:T(8,128)}), f32[16,16,768]{2,1,0:T(8,128)S(1)}, u32[]{:S(2)}, u32[]{:S(2)}) async-start(f32[16,16,768]{2,1,0:T(8,128)} %add_parts.1), calls=%async_computation.2 | async-start | bytes 1572864 | tf_op jit(solution)/shard_map/all_to_all | solution.py:176
  63.2 3.1 %collective-permute-start.1 = (bf16[1,128,1536]{2,1,0:T(8,128)(2,1)S(1)}, bf16[1,128,1536]{2,1,0:T(8,128)(2,1)S(1)}, u32[]{:S(2)}, u32[]{:S(2)}) collective-permute-start(bf16[1,128,1536]{2,1,0:T(8,128)(2,1)S(1)} %get-tuple-element.19), channel_id=1, source_target_pairs={{0,24},{8,0},{16,8},{24,16},{1,25},{9,1},{17,9},{25,17},{2,26},{10... | collective-permute-start | bytes 1179656 | tf_op jit(solution)/shard_map/ppermute | solution.py:227
  66.3 9.4 %collective-permute-done.1 = bf16[1,128,1536]{2,1,0:T(8,128)(2,1)S(1)} collective-permute-done((bf16[1,128,1536]{2,1,0:T(8,128)(2,1)S(1)}, bf16[1,128,1536]{2,1,0:T(8,128)(2,1)S(1)}, u32[]{:S(2)}, u32[]{:S(2)}) %collective-permute-start.1) | collective-permute-done | bytes 393248 | tf_op jit(solution)/shard_map/ppermute | solution.py:227
  75.7 6.4 %all-to-all-done.2.parts_ref = f32[16,16,768]{2,1,0:T(8,128)S(1)} async-done(((f32[16,16,768]{2,1,0:T(8,128)}), f32[16,16,768]{2,1,0:T(8,128)S(1)}, u32[]{:S(2)}, u32[]{:S(2)}) %all-to-all-start.2) | async-done | bytes 786464 | tf_op jit(solution)/shard_map/all_to_all | solution.py:176
  82.1 0.9 %whole_grads.1 = (f32[1,64,1536]{2,1,0:T(8,128)}, f32[1,64,1536]{2,1,0:T(8,128)}) custom-call(f32[16,16,768]{2,1,0:T(8,128)S(1)} %all-to-all-done.2.parts_ref), custom_call_target="tpu_custom_call" | custom-call | tf_op jit(solution)/shard_map/whole_grads/pallas_call | solution.py:19
  83.0 0.7 copy.13
  (1 shorter events, 0.0 us)
Async XLA Ops:
  0.6 1.5 %copy-start.5 = (s32[1,4]{1,0:T(1,128)S(1)}, s32[1,4]{1,0:T(1,128)}, u32[]{:S(2)}) copy-start(s32[1,4]{1,0:T(1,128)} %order_ref.7) | copy-start | bytes 52
  0.6 1.5 %copy-start.6 = (s32[128]{0:T(128)S(1)}, s32[128]{0:T(128)}, u32[]{:S(2)}) copy-start(s32[128]{0:T(128)} %param.14) | copy-start | bytes 1540
  0.7 13.1 %collective-permute-start = (bf16[1,128,1536]{2,1,0:T(8,128)(2,1)}, bf16[1,128,1536]{2,1,0:T(8,128)(2,1)S(1)}, u32[]{:S(2)}, u32[]{:S(2)}) collective-permute-start(bf16[1,128,1536]{2,1,0:T(8,128)(2,1)} %param.8), channel_id=1, source_target_pairs={{0,8},{8,16},{16,24},{1,9},{9,17},{17,25},{2,10},{10,18},{18,26},{... | collective-permute-start | bytes 1179656 | tf_op jit(solution)/shard_map/ppermute | solution.py:187
  2.1 1.0 %copy-start = (bf16[1,128,1536]{2,1,0:T(8,128)(2,1)S(1)}, bf16[1,128,1536]{2,1,0:T(8,128)(2,1)}, u32[]{:S(2)}) copy-start(bf16[1,128,1536]{2,1,0:T(8,128)(2,1)} %cot_ref.7) | copy-start | bytes 1179652
  3.1 10.6 %copy-start.7 = (bf16[128,1536]{1,0:T(8,128)(2,1)S(1)}, bf16[128,1536]{1,0:T(8,128)(2,1)}, u32[]{:S(2)}) copy-start(bf16[128,1536]{1,0:T(8,128)(2,1)} %emb_ref.1) | copy-start | bytes 1179652
  4.6 9.1 %copy-start.1 = (bf16[1,128,1536]{2,1,0:T(8,128)(2,1)S(1)}, bf16[1,128,1536]{2,1,0:T(8,128)(2,1)}, u32[]{:S(2)}) copy-start(bf16[1,128,1536]{2,1,0:T(8,128)(2,1)} %cot_ref.7) | copy-start | bytes 1179652
  4.6 9.1 %copy-start.3 = (bf16[1,64,1536]{2,1,0:T(8,128)(2,1)S(1)}, bf16[1,64,1536]{2,1,0:T(8,128)(2,1)}, u32[]{:S(2)}) copy-start(bf16[1,64,1536]{2,1,0:T(8,128)(2,1)} %gain_ref.3) | copy-start | bytes 589828
  4.6 34.1 %all-to-all-start = ((f32[16,8,768]{2,1,0:T(8,128)}), f32[16,8,768]{2,1,0:T(8,128)S(1)}, u32[]{:S(2)}, u32[]{:S(2)}) async-start(f32[16,8,768]{2,1,0:T(8,128)} %bias_part.1), calls=%async_computation | async-start | bytes 786432 | tf_op jit(solution)/shard_map/all_to_all | solution.py:176
  40.6 6.1 %copy-start.2 = (bf16[1,128,1536]{2,1,0:T(8,128)(2,1)S(1)}, bf16[1,128,1536]{2,1,0:T(8,128)(2,1)}, u32[]{:S(2)}) copy-start(bf16[1,128,1536]{2,1,0:T(8,128)(2,1)} %res_ref.1) | copy-start | bytes 1179652
  40.6 6.1 %copy-start.4 = (bf16[1,64,1536]{2,1,0:T(8,128)(2,1)S(1)}, bf16[1,64,1536]{2,1,0:T(8,128)(2,1)}, u32[]{:S(2)}) copy-start(bf16[1,64,1536]{2,1,0:T(8,128)(2,1)} %bias_ref.1) | copy-start | bytes 589828
  40.6 17.5 %all-to-all-start.1 = ((f32[16,8,768]{2,1,0:T(8,128)}), f32[16,8,768]{2,1,0:T(8,128)S(1)}, u32[]{:S(2)}, u32[]{:S(2)}) async-start(f32[16,8,768]{2,1,0:T(8,128)} %gain_part.1), calls=%async_computation.1 | async-start | bytes 786432 | tf_op jit(solution)/shard_map/all_to_all | solution.py:176
  59.1 23.0 %all-to-all-start.2 = ((f32[16,16,768]{2,1,0:T(8,128)}), f32[16,16,768]{2,1,0:T(8,128)S(1)}, u32[]{:S(2)}, u32[]{:S(2)}) async-start(f32[16,16,768]{2,1,0:T(8,128)} %add_parts.1), calls=%async_computation.2 | async-start | bytes 1572864 | tf_op jit(solution)/shard_map/all_to_all | solution.py:176
  63.2 12.6 %collective-permute-start.1 = (bf16[1,128,1536]{2,1,0:T(8,128)(2,1)S(1)}, bf16[1,128,1536]{2,1,0:T(8,128)(2,1)S(1)}, u32[]{:S(2)}, u32[]{:S(2)}) collective-permute-start(bf16[1,128,1536]{2,1,0:T(8,128)(2,1)S(1)} %get-tuple-element.19), channel_id=1, source_target_pairs={{0,24},{8,0},{16,8},{24,16},{1,25},{9,1},{17,9},{25,17},{2,26},{10... | collective-permute-start | bytes 1179656 | tf_op jit(solution)/shard_map/ppermute | solution.py:227

commit v4 on v3

v4 whole, which is shorter than its diff:
```python
import jax
import jax.numpy as jnp
from jax import lax
from jax.experimental import pallas as pl
from jax.experimental.pallas import tpu as pltpu
from jax.sharding import Mesh, PartitionSpec as P

D = 12288
MB = 4
eps = 1e-05
bf16, f32 = jnp.bfloat16, jnp.float32
CORES = 2

VMEM = pl.BlockSpec(memory_space=pltpu.VMEM)
SMEM = pl.BlockSpec(memory_space=pltpu.SMEM)
HBM = pl.BlockSpec(memory_space=pltpu.HBM)


def call(kernel, name, outs, scratch, in_specs, *args, cover=0, out_specs=None):
    return pl.pallas_call(
        kernel,
        name=name,
        out_shape=outs,
        in_specs=in_specs,
        out_specs=jax.tree.map(lambda _: VMEM, outs) if out_specs is None else out_specs,
        scratch_shapes=scratch,
        cost_estimate=pl.CostEstimate(flops=cover, transcendentals=0, bytes_accessed=0) if cover else None,
        compiler_params=pltpu.CompilerParams(vmem_limit_bytes=40 * 1024 * 1024),
    )(*args)


def rows_of(block, count):
    return pl.ds(pl.multiple_of(block * count, count), count)


def run_copies(copies):
    for copy in copies:
        copy.start()
    for copy in copies:
        copy.wait()


def members(lang_ref, langs):
    tokens = lang_ref.shape[1]
    row = lax.broadcasted_iota(jnp.int32, (langs, tokens), 0)
    return jnp.where(row == lang_ref[...], 1.0, 0.0).astype(bf16)


def selector(lang_ref, langs):
    tokens = lang_ref.shape[1]
    column = jnp.transpose(jnp.broadcast_to(lang_ref[...].astype(f32), (tokens, tokens)))
    lane = lax.broadcasted_iota(jnp.int32, (tokens, langs), 1).astype(f32)
    return jnp.where(column[:, :langs] == lane, 1.0, 0.0).astype(bf16)


def put_pieces(out_ref, sums):
    pieces, height, width = out_ref.shape
    halves = sums.shape[1] // width
    for k in range(pieces):
        top, left = (k // halves) * height, (k % halves) * width
        out_ref[k] = sums[top : top + height, left : left + width]


def bias_kernel(order_ref, lang_ref, cot_ref, out_ref, forward_ref, sems):
    rows = forward_ref.shape[0] // MB
    run_copies(
        [
            pltpu.make_async_copy(
                cot_ref.at[0, pl.ds(j * rows, rows), :], forward_ref.at[rows_of(order_ref[0, j], rows), :], sems.at[j]
            )
            for j in range(MB)
        ]
    )
    langs = out_ref.shape[0] * out_ref.shape[1] * out_ref.shape[2] // forward_ref.shape[1]
    put_pieces(out_ref, jnp.dot(members(lang_ref, langs), forward_ref[...], preferred_element_type=f32))


def sums_kernel(first_ref, lang_ref, recv_ref, emb_ref, cot_ref, gain_ref, out_ref, x_ref, gain_scr, wide_scr):
    tokens = cot_ref.shape[0]
    gain_scr[...] = jnp.dot(selector(lang_ref, gain_ref.shape[1]), gain_ref[0], preferred_element_type=f32).astype(bf16)

    @pl.when(first_ref[0] == 1)
    def _():
        x_ref[...] = emb_ref[...]

    @pl.when(first_ref[0] != 1)
    def _():
        x_ref[...] = recv_ref[0]

    step = 16
    for top in range(0, tokens, step):
        rows = slice(top, top + step)
        x = x_ref[rows, :].astype(f32)
        scaled = cot_ref[rows, :].astype(f32) * gain_scr[rows, :].astype(f32)
        lane = lax.broadcasted_iota(jnp.int32, (step, tokens), 1)
        tile = jnp.zeros((step, tokens), f32)
        for i, term in enumerate((x, x * x, scaled, scaled * x)):
            tile = jnp.where(lane == i, jnp.sum(term, axis=1, keepdims=True), tile)
        wide_scr[rows, :] = tile
    out_ref[...] = jnp.transpose(wide_scr[...])[: out_ref.shape[0], :]


def columns(sums_ref):
    tokens = sums_ref.shape[1]
    one, two, cot, cross = (sums_ref[i : i + 1, :] for i in range(4))
    center = one / D
    inv = lax.rsqrt(two / D - center * center + eps)
    mean_cross = inv * (cross - center * cot) / D
    row = lax.broadcasted_iota(jnp.int32, (tokens, tokens), 0)
    tile = jnp.where(row == 0, center, jnp.where(row == 1, inv, jnp.where(row == 2, cot / D, mean_cross)))
    return jnp.transpose(tile)


def gain_kernel(lang_ref, sums_ref, x_ref, cot_ref, out_ref, high_scr, low_scr, piece_scr, sems):
    pieces, height, width = piece_scr.shape
    halves = x_ref.shape[1] // width
    langs = pieces // halves * height
    tokens, step = cot_ref.shape[0], 16
    figures = columns(sums_ref)
    who = members(lang_ref, langs)
    copies = [pltpu.make_async_copy(piece_scr.at[k], out_ref.at[k], sems.at[k]) for k in range(pieces)]
    for half in range(halves):
        wide = slice(half * width, (half + 1) * width)
        for top in range(0, tokens, step):
            rows = slice(top, top + step)
            center, inv = figures[rows, 0:1], figures[rows, 1:2]
            product = cot_ref[rows, wide].astype(f32) * ((x_ref[rows, wide].astype(f32) - center) * inv)
            high = product.astype(bf16)
            high_scr[rows, wide] = high
            low_scr[rows, wide] = (product - high.astype(f32)).astype(bf16)
        sums = jnp.dot(who, high_scr[:, wide], preferred_element_type=f32) + jnp.dot(
            who, low_scr[:, wide], preferred_element_type=f32
        )
        for top in range(0, langs, height):
            k = top // height * halves + half
            piece_scr[k] = sums[top : top + height, :]
            copies[k].start()
    for copy in copies:
        copy.wait()


def outs_kernel(
    order_ref, lang_ref, sums_ref, x_ref, cot_ref, res_ref, gain_ref, bias_ref, normed_ref, back_ref, fig_scr, gain_scr, bias_scr
):
    pick = selector(lang_ref, gain_ref.shape[1])
    gain_scr[...] = jnp.dot(pick, gain_ref[0], preferred_element_type=f32).astype(bf16)
    bias_scr[...] = jnp.dot(pick, bias_ref[0], preferred_element_type=f32).astype(bf16)
    fig_scr[...] = columns(sums_ref)
    tokens = x_ref.shape[0]
    rows, step = tokens // MB, 16
    for j in range(MB):
        for part in range(0, rows, step):
            here = pl.ds(pl.multiple_of(order_ref[0, j] * rows + part, step), step)
            slot = slice(j * rows + part, j * rows + part + step)
            fig = fig_scr[here, :]
            center, inv, mean_cot, mean_cross = (fig[:, i : i + 1] for i in range(4))
            normalized = (x_ref[here, :].astype(f32) - center) * inv
            gains = gain_scr[here, :].astype(f32)
            scaled = cot_ref[here, :].astype(f32) * gains
            back_ref[0, slot, :] = (
                res_ref[0, slot, :].astype(f32) + inv * (scaled - mean_cot - normalized * mean_cross)
            ).astype(bf16)
            normed_ref[0, here, :] = (normalized * gains + bias_scr[here, :].astype(f32)).astype(bf16)


def added(parts_ref):
    total = parts_ref[0]
    for k in range(1, parts_ref.shape[0]):
        total = total + parts_ref[k]
    return total


def total_kernel(parts_ref, out_ref):
    out_ref[...] = added(parts_ref)


def add_kernel(gain_ref, bias_ref, out_ref, total_scr, sems):
    height = bias_ref.shape[0]
    total_scr[height:, :] = bias_ref[...]
    total_scr[:height, :] = added(gain_ref)
    run_copies([pltpu.make_async_copy(total_scr, out_ref.at[k], sems.at[k]) for k in range(out_ref.shape[0])])


def whole_kernel(parts_ref, gain_ref, bias_ref, sems):
    pieces, height, width = parts_ref.shape
    height //= 2
    halves = gain_ref.shape[2] // width
    copies = []
    for i, out_ref in enumerate((gain_ref, bias_ref)):
        for k in range(pieces):
            place = out_ref.at[0, pl.ds((k // halves) * height, height), pl.ds((k % halves) * width, width)]
            copies.append(pltpu.make_async_copy(parts_ref.at[k, pl.ds(i * height, height), :], place, sems.at[i, k]))
    run_copies(copies)


def settle_kernel(value_ref, out_ref, sem):
    run_copies([pltpu.make_async_copy(value_ref, out_ref, sem)])


def shape(dims, kind):
    return jax.ShapeDtypeStruct(dims, kind)


def exchanged(pieces):
    return lax.all_to_all(pieces, "dp", 0, 0)


def local(section_out, embedded, cot_norm, cot_res, gain, bias, lang_ids, mb_order):
    tokens, width = embedded.shape
    langs = gain.shape[1]
    replicas = lax.axis_size("dp")
    pieces = (replicas, 8, langs * width // (8 * replicas))
    lang = lang_ids.reshape(1, tokens)
    first = (lax.axis_index("pipe") == 0).astype(jnp.int32).reshape(1)
    stages = lax.axis_size("pipe")
    received = lax.ppermute(section_out, "pipe", [(i, i + 1) for i in range(stages - 1)])

    sems = pltpu.SemaphoreType.DMA
    forward = shape((tokens, width), bf16)
    bias_part, cot = call(
        bias_kernel,
        "bias_part",
        (shape(pieces, f32), forward),
        [sems((MB,))],
        [SMEM, VMEM, HBM],
        mb_order, lang, cot_norm,
    )
    bias_mine = exchanged(bias_part)
    received, bias_part = lax.optimization_barrier((received, bias_part))

    sums, x = call(
        sums_kernel,
        "token_sums",
        (shape((8, tokens), f32), forward),
        [pltpu.VMEM((tokens, width), bf16), pltpu.VMEM((tokens, tokens), f32)],
        [SMEM, VMEM, VMEM, VMEM, VMEM, VMEM],
        first, lang, received, embedded, cot, gain,
        cover=10**11,
    )
    sums = lax.psum(lax.psum(sums, "core"), "far")
    sums, bias_mine = lax.optimization_barrier((sums, bias_mine))

    gain_part = call(
        gain_kernel,
        "gain_part",
        shape(pieces, f32),
        [pltpu.VMEM((tokens, width), bf16), pltpu.VMEM((tokens, width), bf16), pltpu.VMEM(pieces, f32), sems((replicas,))],
        [VMEM, VMEM, VMEM, VMEM],
        lang, sums, x, cot,
        out_specs=HBM,
    )
    gain_mine = exchanged(gain_part)
    bias_total = call(total_kernel, "bias_total", shape(pieces[1:], f32), [], [VMEM], bias_mine)
    normed, back = call(
        outs_kernel,
        "norm_and_grad",
        (shape((1, tokens, width), bf16), shape((1, tokens, width), bf16)),
        [pltpu.VMEM((tokens, tokens), f32), pltpu.VMEM((tokens, width), bf16), pltpu.VMEM((tokens, width), bf16)],
        [SMEM, VMEM, VMEM, VMEM, VMEM, VMEM, VMEM, VMEM],
        mb_order, lang, sums, x, cot, cot_res, gain, bias,
    )
    returned = lax.ppermute(back, "pipe", [(i, (i - 1) % stages) for i in range(stages)])
    gain_mine, back, bias_total = lax.optimization_barrier((gain_mine, back, bias_total))
    both = (pieces[0], 2 * pieces[1], pieces[2])
    totals = exchanged(
        call(
            add_kernel,
            "add_parts",
            shape(both, f32),
            [pltpu.VMEM(both[1:], f32), sems((replicas,))],
            [VMEM, VMEM],
            gain_mine, bias_total,
            out_specs=HBM,
        )
    )
    returned = call(settle_kernel, "settle", shape(back.shape, bf16), [sems(())], [VMEM], returned, out_specs=HBM)
    totals, returned = lax.optimization_barrier((totals, returned))
    grads = shape((1, langs, width), f32)
    gain_grad, bias_grad = call(
        whole_kernel, "whole_grads", (grads, grads), [sems((2, replicas))], [VMEM], totals, out_specs=(HBM, HBM)
    )
    return normed, returned, gain_grad, bias_grad


def solution(mesh):
    dp, pipe, tensor = (mesh.shape[a] for a in ("dp", "pipe", "tensor"))
    split = Mesh(mesh.devices.reshape(dp, pipe, tensor // CORES, CORES), ("dp", "pipe", "far", "core"))
    tensor = ("far", "core")
    return jax.shard_map(
        local,
        mesh=split,
        in_specs=(
            P("pipe", "dp", tensor),
            P("dp", tensor),
            P("pipe", "dp", tensor),
            P("pipe", "dp", tensor),
            P("pipe", None, tensor),
            P("pipe", None, tensor),
            P("dp"),
            P("dp", None),
        ),
        out_specs=(
            P("pipe", "dp", tensor),
            P("pipe", "dp", tensor),
            P("pipe", None, tensor),
            P("pipe", None, tensor),
        ),
        check_vma=False,
    )
```

time: 85.2 us -> 84.2 us (0.988)
  the two profiles are of different devices: /device:TPU:6 before, /device:TPU:32 now
where the time goes in v4:
time: 84.2 us; the launch traced here: 83.6 us
  starting transfers between devices  28.2 us (33%)
  waiting for transfers between devices  22.2 us (26%)
  blocking collectives  21.2 us (25%)
  Pallas kernels  9.28 us (11%)
  local copies, waits for them, and re-layouts  1.96 us (2%)
    all_to_all x3, starting transfers between devices, exchanged(): return lax.all_to_all(pieces, 'dp', 0, 0)  21.3 us
    psum x2, blocking collectives, local(): sums = lax.psum(lax.psum(sums, 'core'), 'far')  21.2 us
    all_to_all x3, waiting for transfers between devices, exchanged(): return lax.all_to_all(pieces, 'dp', 0, 0)  14.5 us
    pallas_call x8, Pallas kernels, call(): pl.pallas_call(kernel, name=name, out_shape=outs, in_specs=in_specs, out_...  9.28 us
    ppermute x1, waiting for transfers between devices, local(): lax.ppermute(back, 'pipe', [(i, (i - 1) % stages) for i in range(stages)])  7.71 us
    ppermute x1, starting transfers between devices, local(): lax.ppermute(section_out, 'pipe', [(i, i + 1) for i in range(stages - 1)])  3.55 us
    ppermute x1, starting transfers between devices, local(): lax.ppermute(back, 'pipe', [(i, (i - 1) % stages) for i in range(stages)])  3.35 us
    unnamed x14, local copies, waits for them, and re-layouts  1.96 us
  transfers between devices with their start and end apart: 5, of which 3 were waited for; matrix products, arithmetic and copies ran while one was open for 0% of the time, Pallas kernels for 7%

profile of v4, /device:TPU:32, one launch (start us, length us, event | category | flops | bytes accessed | tf_op | source)
XLA Modules:
  0.0 83.6 jit_solution(980203851789038250)
XLA Ops:
  0.6 0.0 copy-start.5
  0.6 0.0 copy-start.4
  0.7 3.6 %collective-permute-start = (bf16[1,128,1536]{2,1,0:T(8,128)(2,1)}, bf16[1,128,1536]{2,1,0:T(8,128)(2,1)S(1)}, u32[]{:S(2)}, u32[]{:S(2)}) collective-permute-start(bf16[1,128,1536]{2,1,0:T(8,128)(2,1)} %param.8), channel_id=1, source_target_pairs={{0,8},{8,16},{16,24},{1,9},{9,17},{17,25},{2,10},{10,18},{18,26},{... | collective-permute-start | bytes 1179656 | tf_op jit(solution)/shard_map/ppermute | solution.py:216
  4.2 0.0 copy-done.5
  4.2 0.0 copy-done.4
  4.2 0.0 copy-start
  4.2 1.0 %copy-done = bf16[1,128,1536]{2,1,0:T(8,128)(2,1)S(1)} copy-done((bf16[1,128,1536]{2,1,0:T(8,128)(2,1)S(1)}, bf16[1,128,1536]{2,1,0:T(8,128)(2,1)}, u32[]{:S(2)}) %copy-start) | copy-done | bytes 393240
  5.2 2.0 %bias_part.1 = (f32[16,8,768]{2,1,0:T(8,128)}, bf16[128,1536]{1,0:T(8,128)(2,1)S(1)}) custom-call(s32[1,4]{1,0:T(1,128)S(1)} %copy-done.5, s32[1,128]{1,0:T(1,128)S(1)} %bitcast.2, bf16[1,128,1536]{2,1,0:T(8,128)(2,1)S(1)} %copy-done), custom_call_target="tpu_custom_call" | custom-call | tf_op jit(solution)/shard_map/bias_part/pallas_call | solution.py:20
  7.3 0.0 copy-start.2
  7.3 0.0 copy-start.6
  7.3 8.8 %all-to-all-start = ((f32[16,8,768]{2,1,0:T(8,128)}), f32[16,8,768]{2,1,0:T(8,128)S(1)}, u32[]{:S(2)}, u32[]{:S(2)}) async-start(f32[16,8,768]{2,1,0:T(8,128)} %get-tuple-element.19), calls=%async_computation | async-start | bytes 786432 | tf_op jit(solution)/shard_map/all_to_all | solution.py:205
  16.1 0.0 collective-permute-done.recv_ref
  16.1 0.0 copy-done.2
  16.1 0.0 copy-done.6
  16.1 0.0 copy-start.3
  16.1 0.7 token_sums.1
  16.8 2.5 %psum.14 = f32[8,128]{1,0:T(8,128)S(1)} all-reduce(f32[8,128]{1,0:T(8,128)S(1)} %get-tuple-element.22), channel_id=1, replica_groups=mesh['dp'=16,'pipe'=4,'far'=4,'core'=2] {'core'}, use_global_device_ids=true, to_apply=%region_0.0 | all-reduce | flops 1024 | bytes 8192 | tf_op jit(solution)/shard_map/psum | solution.py:240
  19.3 18.8 %psum.15.sums_ref = f32[8,128]{1,0:T(8,128)S(1)} all-reduce(f32[8,128]{1,0:T(8,128)S(1)} %psum.14), channel_id=1, replica_groups=mesh['dp'=16,'pipe'=4,'far'=4,'core'=2] {'far'}, use_global_device_ids=true, to_apply=%region_1.0 | all-reduce | flops 1024 | bytes 8192 | tf_op jit(solution)/shard_map/psum | solution.py:240
  38.1 0.0 all-to-all-done.parts_ref
  38.1 1.3 %gain_part.1 = f32[16,8,768]{2,1,0:T(8,128)} custom-call(s32[1,128]{1,0:T(1,128)S(1)} %bitcast.4, f32[8,128]{1,0:T(8,128)S(1)} %psum.15.sums_ref, bf16[128,1536]{1,0:T(8,128)(2,1)S(1)} %get-tuple-element.24.x_ref, bf16[128,1536]{1,0:T(8,128)(2,1)S(1)} %get-tuple-element.21.cot_ref), custom_call_target="tpu_custom_call" | custom-call | tf_op jit(solution)/shard_map/gain_part/pallas_call | solution.py:20
  39.4 7.3 %all-to-all-start.1 = ((f32[16,8,768]{2,1,0:T(8,128)}), f32[16,8,768]{2,1,0:T(8,128)S(1)}, u32[]{:S(2)}, u32[]{:S(2)}) async-start(f32[16,8,768]{2,1,0:T(8,128)} %gain_part.1), calls=%async_computation.1 | async-start | bytes 786432 | tf_op jit(solution)/shard_map/all_to_all | solution.py:205
  46.7 0.0 copy-start.1
  46.8 0.0 copy-done.3
  46.8 0.9 %copy-done.1 = bf16[1,128,1536]{2,1,0:T(8,128)(2,1)S(1)} copy-done((bf16[1,128,1536]{2,1,0:T(8,128)(2,1)S(1)}, bf16[1,128,1536]{2,1,0:T(8,128)(2,1)}, u32[]{:S(2)}) %copy-start.1) | copy-done | bytes 393240
  47.7 2.2 %norm_and_grad.1 = (bf16[1,128,1536]{2,1,0:T(8,128)(2,1)}, bf16[1,128,1536]{2,1,0:T(8,128)(2,1)S(1)}) custom-call(s32[1,4]{1,0:T(1,128)S(1)} %copy-done.5, s32[1,128]{1,0:T(1,128)S(1)} %bitcast.5, f32[8,128]{1,0:T(8,128)S(1)} %psum.15.sums_ref, bf16[128,1536]{1,0:T(8,128)(2,1)S(1)} %get-tuple-element.24.x_ref, ...), custom_call_target="tpu_custom_call" | custom-call | tf_op jit(solution)/shard_map/norm_and_grad/pallas_call | solution.py:20
  50.0 7.1 %all-to-all-done.1.gain_ref = f32[16,8,768]{2,1,0:T(8,128)S(1)} async-done(((f32[16,8,768]{2,1,0:T(8,128)}), f32[16,8,768]{2,1,0:T(8,128)S(1)}, u32[]{:S(2)}, u32[]{:S(2)}) %all-to-all-start.1) | async-done | bytes 393248 | tf_op jit(solution)/shard_map/all_to_all | solution.py:205
  57.1 1.1 %add_parts.1 = f32[16,16,768]{2,1,0:T(8,128)} custom-call(f32[16,8,768]{2,1,0:T(8,128)S(1)} %all-to-all-done.1.gain_ref, f32[8,768]{1,0:T(8,128)S(1)} %bias_total.1.bias_ref), custom_call_target="tpu_custom_call" | custom-call | tf_op jit(solution)/shard_map/add_parts/pallas_call | solution.py:20
  58.2 5.1 %all-to-all-start.2 = ((f32[16,16,768]{2,1,0:T(8,128)}), f32[16,16,768]{2,1,0:T(8,128)S(1)}, u32[]{:S(2)}, u32[]{:S(2)}) async-start(f32[16,16,768]{2,1,0:T(8,128)} %add_parts.1), calls=%async_computation.2 | async-start | bytes 1572864 | tf_op jit(solution)/shard_map/all_to_all | solution.py:205
  63.3 3.3 %collective-permute-start.1 = (bf16[1,128,1536]{2,1,0:T(8,128)(2,1)S(1)}, bf16[1,128,1536]{2,1,0:T(8,128)(2,1)S(1)}, u32[]{:S(2)}, u32[]{:S(2)}) collective-permute-start(bf16[1,128,1536]{2,1,0:T(8,128)(2,1)S(1)} %get-tuple-element.26), channel_id=1, source_target_pairs={{0,24},{8,0},{16,8},{24,16},{1,25},{9,1},{17,9},{25,17},{2,26},{10... | collective-permute-start | bytes 1179656 | tf_op jit(solution)/shard_map/ppermute | solution.py:262
  66.7 7.7 %collective-permute-done.1.value_ref = bf16[1,128,1536]{2,1,0:T(8,128)(2,1)S(1)} collective-permute-done((bf16[1,128,1536]{2,1,0:T(8,128)(2,1)S(1)}, bf16[1,128,1536]{2,1,0:T(8,128)(2,1)S(1)}, u32[]{:S(2)}, u32[]{:S(2)}) %collective-permute-start.1) | collective-permute-done | bytes 393248 | tf_op jit(solution)/shard_map/ppermute | solution.py:262
  74.4 0.8 settle.1
  75.1 7.3 %all-to-all-done.2.parts_ref = f32[16,16,768]{2,1,0:T(8,128)S(1)} async-done(((f32[16,16,768]{2,1,0:T(8,128)}), f32[16,16,768]{2,1,0:T(8,128)S(1)}, u32[]{:S(2)}, u32[]{:S(2)}) %all-to-all-start.2) | async-done | bytes 786464 | tf_op jit(solution)/shard_map/all_to_all | solution.py:205
  82.5 1.1 %whole_grads.1 = (f32[1,64,1536]{2,1,0:T(8,128)}, f32[1,64,1536]{2,1,0:T(8,128)}) custom-call(f32[16,16,768]{2,1,0:T(8,128)S(1)} %all-to-all-done.2.parts_ref), custom_call_target="tpu_custom_call" | custom-call | tf_op jit(solution)/shard_map/whole_grads/pallas_call | solution.py:20
  (1 shorter events, 0.0 us)
Async XLA Ops:
  0.6 3.6 %copy-start.5 = (s32[1,4]{1,0:T(1,128)S(1)}, s32[1,4]{1,0:T(1,128)}, u32[]{:S(2)}) copy-start(s32[1,4]{1,0:T(1,128)} %order_ref.3) | copy-start | bytes 52
  0.6 3.6 %copy-start.4 = (s32[128]{0:T(128)S(1)}, s32[128]{0:T(128)}, u32[]{:S(2)}) copy-start(s32[128]{0:T(128)} %param.14) | copy-start | bytes 1540
  0.7 15.4 %collective-permute-start = (bf16[1,128,1536]{2,1,0:T(8,128)(2,1)}, bf16[1,128,1536]{2,1,0:T(8,128)(2,1)S(1)}, u32[]{:S(2)}, u32[]{:S(2)}) collective-permute-start(bf16[1,128,1536]{2,1,0:T(8,128)(2,1)} %param.8), channel_id=1, source_target_pairs={{0,8},{8,16},{16,24},{1,9},{9,17},{17,25},{2,10},{10,18},{18,26},{... | collective-permute-start | bytes 1179656 | tf_op jit(solution)/shard_map/ppermute | solution.py:216
  4.2 1.0 %copy-start = (bf16[1,128,1536]{2,1,0:T(8,128)(2,1)S(1)}, bf16[1,128,1536]{2,1,0:T(8,128)(2,1)}, u32[]{:S(2)}) copy-start(bf16[1,128,1536]{2,1,0:T(8,128)(2,1)} %cot_ref.1) | copy-start | bytes 1179652
  7.3 8.8 %copy-start.2 = (bf16[1,64,1536]{2,1,0:T(8,128)(2,1)S(1)}, bf16[1,64,1536]{2,1,0:T(8,128)(2,1)}, u32[]{:S(2)}) copy-start(bf16[1,64,1536]{2,1,0:T(8,128)(2,1)} %gain_ref.3) | copy-start | bytes 589828
  7.3 8.8 %copy-start.6 = (bf16[128,1536]{1,0:T(8,128)(2,1)S(1)}, bf16[128,1536]{1,0:T(8,128)(2,1)}, u32[]{:S(2)}) copy-start(bf16[128,1536]{1,0:T(8,128)(2,1)} %emb_ref.1) | copy-start | bytes 1179652
  7.3 30.8 %all-to-all-start = ((f32[16,8,768]{2,1,0:T(8,128)}), f32[16,8,768]{2,1,0:T(8,128)S(1)}, u32[]{:S(2)}, u32[]{:S(2)}) async-start(f32[16,8,768]{2,1,0:T(8,128)} %get-tuple-element.19), calls=%async_computation | async-start | bytes 786432 | tf_op jit(solution)/shard_map/all_to_all | solution.py:205
  16.1 30.7 %copy-start.3 = (bf16[1,64,1536]{2,1,0:T(8,128)(2,1)S(1)}, bf16[1,64,1536]{2,1,0:T(8,128)(2,1)}, u32[]{:S(2)}) copy-start(bf16[1,64,1536]{2,1,0:T(8,128)(2,1)} %bias_ref.1) | copy-start | bytes 589828
  39.4 17.7 %all-to-all-start.1 = ((f32[16,8,768]{2,1,0:T(8,128)}), f32[16,8,768]{2,1,0:T(8,128)S(1)}, u32[]{:S(2)}, u32[]{:S(2)}) async-start(f32[16,8,768]{2,1,0:T(8,128)} %gain_part.1), calls=%async_computation.1 | async-start | bytes 786432 | tf_op jit(solution)/shard_map/all_to_all | solution.py:205
  46.7 1.0 %copy-start.1 = (bf16[1,128,1536]{2,1,0:T(8,128)(2,1)S(1)}, bf16[1,128,1536]{2,1,0:T(8,128)(2,1)}, u32[]{:S(2)}) copy-start(bf16[1,128,1536]{2,1,0:T(8,128)(2,1)} %res_ref.1) | copy-start | bytes 1179652
  58.2 24.3 %all-to-all-start.2 = ((f32[16,16,768]{2,1,0:T(8,128)}), f32[16,16,768]{2,1,0:T(8,128)S(1)}, u32[]{:S(2)}, u32[]{:S(2)}) async-start(f32[16,16,768]{2,1,0:T(8,128)} %add_parts.1), calls=%async_computation.2 | async-start | bytes 1572864 | tf_op jit(solution)/shard_map/all_to_all | solution.py:205
  63.3 11.1 %collective-permute-start.1 = (bf16[1,128,1536]{2,1,0:T(8,128)(2,1)S(1)}, bf16[1,128,1536]{2,1,0:T(8,128)(2,1)S(1)}, u32[]{:S(2)}, u32[]{:S(2)}) collective-permute-start(bf16[1,128,1536]{2,1,0:T(8,128)(2,1)S(1)} %get-tuple-element.26), channel_id=1, source_target_pairs={{0,24},{8,0},{16,8},{24,16},{1,25},{9,1},{17,9},{25,17},{2,26},{10... | collective-permute-start | bytes 1179656 | tf_op jit(solution)/shard_map/ppermute | solution.py:262

commit v5 on v4

--- a/solution.py
+++ b/solution.py
@@ -61,16 +61,10 @@
         out_ref[k] = sums[top : top + height, left : left + width]
 
 
-def bias_kernel(order_ref, lang_ref, cot_ref, out_ref, forward_ref, sems):
+def bias_kernel(order_ref, lang_ref, cot_ref, out_ref, forward_ref):
     rows = forward_ref.shape[0] // MB
-    run_copies(
-        [
-            pltpu.make_async_copy(
-                cot_ref.at[0, pl.ds(j * rows, rows), :], forward_ref.at[rows_of(order_ref[0, j], rows), :], sems.at[j]
-            )
-            for j in range(MB)
-        ]
-    )
+    for j in range(MB):
+        forward_ref[rows_of(order_ref[0, j], rows), :] = cot_ref[0, j * rows : (j + 1) * rows, :]
     langs = out_ref.shape[0] * out_ref.shape[1] * out_ref.shape[2] // forward_ref.shape[1]
     put_pieces(out_ref, jnp.dot(members(lang_ref, langs), forward_ref[...], preferred_element_type=f32))
 
@@ -182,14 +176,13 @@
 
 
 def whole_kernel(parts_ref, gain_ref, bias_ref, sems):
-    pieces, height, width = parts_ref.shape
+    _, halves, height, width = parts_ref.shape
     height //= 2
-    halves = gain_ref.shape[2] // width
     copies = []
     for i, out_ref in enumerate((gain_ref, bias_ref)):
-        for k in range(pieces):
-            place = out_ref.at[0, pl.ds((k // halves) * height, height), pl.ds((k % halves) * width, width)]
-            copies.append(pltpu.make_async_copy(parts_ref.at[k, pl.ds(i * height, height), :], place, sems.at[i, k]))
+        for half in range(halves):
+            place = out_ref.at[:, :, pl.ds(half * width, width)]
+            copies.append(pltpu.make_async_copy(parts_ref.at[:, half, pl.ds(i * height, height), :], place, sems.at[i, half]))
     run_copies(copies)
 
 
@@ -221,8 +214,8 @@
         bias_kernel,
         "bias_part",
         (shape(pieces, f32), forward),
-        [sems((MB,))],
-        [SMEM, VMEM, HBM],
+        [],
+        [SMEM, VMEM, VMEM],
         mb_order, lang, cot_norm,
     )
     bias_mine = exchanged(bias_part)
@@ -273,12 +266,20 @@
             out_specs=HBM,
         )
     )
-    returned = call(settle_kernel, "settle", shape(back.shape, bf16), [sems(())], [VMEM], returned, out_specs=HBM)
+    returned = call(settle_kernel, "settle", shape(back.shape, bf16), [sems(())], [VMEM], returned, out_specs=HBM, cover=10**11)
     totals, returned = lax.optimization_barrier((totals, returned))
-    grads = shape((1, langs, width), f32)
+    halves = width // pieces[2]
+    grads = shape((replicas // halves, pieces[1], width), f32)
     gain_grad, bias_grad = call(
-        whole_kernel, "whole_grads", (grads, grads), [sems((2, replicas))], [VMEM], totals, out_specs=(HBM, HBM)
-    )
+        whole_kernel,
+        "whole_grads",
+        (grads, grads),
+        [sems((2, halves))],
+        [VMEM],
+        totals.reshape(replicas // halves, halves, *both[1:]),
+        out_specs=(HBM, HBM),
+    )
+    gain_grad, bias_grad = (g.reshape(1, langs, width) for g in (gain_grad, bias_grad))
     return normed, returned, gain_grad, bias_grad
 
 

time: 84.2 us -> 83.5 us (level)
  the two profiles are of different devices: /device:TPU:32 before, /device:TPU:6 now
where the time goes in v5:
time: 83.5 us; the launch traced here: 82 us
  waiting for transfers between devices  24.6 us (29%)
  blocking collectives  23.7 us (28%)
  starting transfers between devices  23.3 us (28%)
  Pallas kernels  8.53 us (10%)
  local copies, waits for them, and re-layouts  1.02 us (1%)
    all_to_all x3, waiting for transfers between devices, exchanged(): return lax.all_to_all(pieces, 'dp', 0, 0)  24.2 us
    psum x2, blocking collectives, local(): sums = lax.psum(lax.psum(sums, 'core'), 'far')  23.7 us
    all_to_all x3, starting transfers between devices, exchanged(): return lax.all_to_all(pieces, 'dp', 0, 0)  18.8 us
    pallas_call x8, Pallas kernels, call(): pl.pallas_call(kernel, name=name, out_shape=outs, in_specs=in_specs, out_...  8.53 us
    ppermute x1, starting transfers between devices, local(): lax.ppermute(back, 'pipe', [(i, (i - 1) % stages) for i in range(stages)])  3.09 us
  transfers between devices with their start and end apart: 5, of which 3 were waited for; matrix products, arithmetic and copies ran while one was open for 0% of the time, Pallas kernels for 8%

profile of v5, /device:TPU:6, one launch (start us, length us, event | category | flops | bytes accessed | tf_op | source)
XLA Modules:
  0.0 82.0 jit_solution(2803820211844944781)
XLA Ops:
  0.6 0.0 copy-start.5
  0.6 0.0 copy-start.4
  0.7 1.4 %collective-permute-start = (bf16[1,128,1536]{2,1,0:T(8,128)(2,1)}, bf16[1,128,1536]{2,1,0:T(8,128)(2,1)S(1)}, u32[]{:S(2)}, u32[]{:S(2)}) collective-permute-start(bf16[1,128,1536]{2,1,0:T(8,128)(2,1)} %param.8), channel_id=1, source_target_pairs={{0,8},{8,16},{16,24},{1,9},{9,17},{17,25},{2,10},{10,18},{18,26},{... | collective-permute-start | bytes 1179656 | tf_op jit(solution)/shard_map/ppermute | solution.py:209
  2.1 0.0 copy-done.5
  2.1 0.0 copy-done.4
  2.1 0.0 copy-start
  2.1 1.0 %copy-done = bf16[1,128,1536]{2,1,0:T(8,128)(2,1)S(1)} copy-done((bf16[1,128,1536]{2,1,0:T(8,128)(2,1)S(1)}, bf16[1,128,1536]{2,1,0:T(8,128)(2,1)}, u32[]{:S(2)}) %copy-start) | copy-done | bytes 393240
  3.1 1.5 %bias_part.1 = (f32[16,8,768]{2,1,0:T(8,128)}, bf16[128,1536]{1,0:T(8,128)(2,1)S(1)}) custom-call(s32[1,4]{1,0:T(1,128)S(1)} %copy-done.5, s32[1,128]{1,0:T(1,128)S(1)} %bitcast.6, bf16[1,128,1536]{2,1,0:T(8,128)(2,1)S(1)} %copy-done), custom_call_target="tpu_custom_call" | custom-call | tf_op jit(solution)/shard_map/bias_part/pallas_call | solution.py:20
  4.6 0.0 copy-start.2
  4.6 0.0 copy-start.6
  4.6 8.8 %all-to-all-start = ((f32[16,8,768]{2,1,0:T(8,128)}), f32[16,8,768]{2,1,0:T(8,128)S(1)}, u32[]{:S(2)}, u32[]{:S(2)}) async-start(f32[16,8,768]{2,1,0:T(8,128)} %get-tuple-element.19), calls=%async_computation | async-start | bytes 786432 | tf_op jit(solution)/shard_map/all_to_all | solution.py:198
  13.4 0.3 collective-permute-done.recv_ref
  13.7 0.0 copy-done.2
  13.7 0.0 copy-done.6
  13.7 0.7 token_sums.1
  14.4 2.5 %psum.14 = f32[8,128]{1,0:T(8,128)S(1)} all-reduce(f32[8,128]{1,0:T(8,128)S(1)} %get-tuple-element.22), channel_id=1, replica_groups=mesh['dp'=16,'pipe'=4,'far'=4,'core'=2] {'core'}, use_global_device_ids=true, to_apply=%region_0.0 | all-reduce | flops 1024 | bytes 8192 | tf_op jit(solution)/shard_map/psum | solution.py:233
  16.9 21.3 %psum.15.sums_ref = f32[8,128]{1,0:T(8,128)S(1)} all-reduce(f32[8,128]{1,0:T(8,128)S(1)} %psum.14), channel_id=1, replica_groups=mesh['dp'=16,'pipe'=4,'far'=4,'core'=2] {'far'}, use_global_device_ids=true, to_apply=%region_1.0 | all-reduce | flops 1024 | bytes 8192 | tf_op jit(solution)/shard_map/psum | solution.py:233
  38.2 0.0 all-to-all-done.parts_ref
  38.2 1.3 %gain_part.1 = f32[16,8,768]{2,1,0:T(8,128)} custom-call(s32[1,128]{1,0:T(1,128)S(1)} %bitcast.8, f32[8,128]{1,0:T(8,128)S(1)} %psum.15.sums_ref, bf16[128,1536]{1,0:T(8,128)(2,1)S(1)} %get-tuple-element.24.x_ref, bf16[128,1536]{1,0:T(8,128)(2,1)S(1)} %get-tuple-element.21.cot_ref), custom_call_target="tpu_custom_call" | custom-call | tf_op jit(solution)/shard_map/gain_part/pallas_call | solution.py:20
  39.5 0.0 copy-start.1
  39.5 0.0 copy-start.3
  39.5 6.0 %all-to-all-start.1 = ((f32[16,8,768]{2,1,0:T(8,128)}), f32[16,8,768]{2,1,0:T(8,128)S(1)}, u32[]{:S(2)}, u32[]{:S(2)}) async-start(f32[16,8,768]{2,1,0:T(8,128)} %gain_part.1), calls=%async_computation.1 | async-start | bytes 786432 | tf_op jit(solution)/shard_map/all_to_all | solution.py:198
  45.6 0.0 copy-done.1
  45.6 0.0 copy-done.3
  45.6 2.2 %norm_and_grad.1 = (bf16[1,128,1536]{2,1,0:T(8,128)(2,1)}, bf16[1,128,1536]{2,1,0:T(8,128)(2,1)S(1)}) custom-call(s32[1,4]{1,0:T(1,128)S(1)} %copy-done.5, s32[1,128]{1,0:T(1,128)S(1)} %bitcast.9, f32[8,128]{1,0:T(8,128)S(1)} %psum.15.sums_ref, bf16[128,1536]{1,0:T(8,128)(2,1)S(1)} %get-tuple-element.24.x_ref, ...), custom_call_target="tpu_custom_call" | custom-call | tf_op jit(solution)/shard_map/norm_and_grad/pallas_call | solution.py:20
  47.8 3.1 %collective-permute-start.1 = (bf16[1,128,1536]{2,1,0:T(8,128)(2,1)S(1)}, bf16[1,128,1536]{2,1,0:T(8,128)(2,1)S(1)}, u32[]{:S(2)}, u32[]{:S(2)}) collective-permute-start(bf16[1,128,1536]{2,1,0:T(8,128)(2,1)S(1)} %get-tuple-element.26), channel_id=1, source_target_pairs={{0,24},{8,0},{16,8},{24,16},{1,25},{9,1},{17,9},{25,17},{2,26},{10... | collective-permute-start | bytes 1179656 | tf_op jit(solution)/shard_map/ppermute | solution.py:255
  51.0 6.1 %all-to-all-done.1.gain_ref = f32[16,8,768]{2,1,0:T(8,128)S(1)} async-done(((f32[16,8,768]{2,1,0:T(8,128)}), f32[16,8,768]{2,1,0:T(8,128)S(1)}, u32[]{:S(2)}, u32[]{:S(2)}) %all-to-all-start.1) | async-done | bytes 393248 | tf_op jit(solution)/shard_map/all_to_all | solution.py:198
  57.0 1.1 %add_parts.1 = f32[16,16,768]{2,1,0:T(8,128)} custom-call(f32[16,8,768]{2,1,0:T(8,128)S(1)} %all-to-all-done.1.gain_ref, f32[8,768]{1,0:T(8,128)S(1)} %bias_total.1.bias_ref), custom_call_target="tpu_custom_call" | custom-call | tf_op jit(solution)/shard_map/add_parts/pallas_call | solution.py:20
  58.1 4.0 %all-to-all-start.2 = ((f32[16,16,768]{2,1,0:T(8,128)}), f32[16,16,768]{2,1,0:T(8,128)S(1)}, u32[]{:S(2)}, u32[]{:S(2)}) async-start(f32[16,16,768]{2,1,0:T(8,128)} %add_parts.1), calls=%async_computation.2 | async-start | bytes 1572864 | tf_op jit(solution)/shard_map/all_to_all | solution.py:198
  62.1 0.0 collective-permute-done.1.value_ref
  62.2 0.8 settle.1
  62.9 18.2 %all-to-all-done.2 = f32[16,16,768]{2,1,0:T(8,128)S(1)} async-done(((f32[16,16,768]{2,1,0:T(8,128)}), f32[16,16,768]{2,1,0:T(8,128)S(1)}, u32[]{:S(2)}, u32[]{:S(2)}) %all-to-all-start.2) | async-done | bytes 786464 | tf_op jit(solution)/shard_map/all_to_all | solution.py:198
  81.1 0.9 %whole_grads.1 = (f32[8,8,1536]{2,1,0:T(8,128)}, f32[8,8,1536]{2,1,0:T(8,128)}) custom-call(f32[8,2,16,768]{3,2,1,0:T(8,128)S(1)} %bitcast.5), custom_call_target="tpu_custom_call" | custom-call | tf_op jit(solution)/shard_map/whole_grads/pallas_call | solution.py:20
  (1 shorter events, 0.0 us)
Async XLA Ops:
  0.6 1.5 %copy-start.5 = (s32[1,4]{1,0:T(1,128)S(1)}, s32[1,4]{1,0:T(1,128)}, u32[]{:S(2)}) copy-start(s32[1,4]{1,0:T(1,128)} %order_ref.3) | copy-start | bytes 52
  0.6 1.5 %copy-start.4 = (s32[128]{0:T(128)S(1)}, s32[128]{0:T(128)}, u32[]{:S(2)}) copy-start(s32[128]{0:T(128)} %param.14) | copy-start | bytes 1540
  0.7 13.1 %collective-permute-start = (bf16[1,128,1536]{2,1,0:T(8,128)(2,1)}, bf16[1,128,1536]{2,1,0:T(8,128)(2,1)S(1)}, u32[]{:S(2)}, u32[]{:S(2)}) collective-permute-start(bf16[1,128,1536]{2,1,0:T(8,128)(2,1)} %param.8), channel_id=1, source_target_pairs={{0,8},{8,16},{16,24},{1,9},{9,17},{17,25},{2,10},{10,18},{18,26},{... | collective-permute-start | bytes 1179656 | tf_op jit(solution)/shard_map/ppermute | solution.py:209
  2.1 1.0 %copy-start = (bf16[1,128,1536]{2,1,0:T(8,128)(2,1)S(1)}, bf16[1,128,1536]{2,1,0:T(8,128)(2,1)}, u32[]{:S(2)}) copy-start(bf16[1,128,1536]{2,1,0:T(8,128)(2,1)} %cot_ref.1) | copy-start | bytes 1179652
  4.6 9.1 %copy-start.2 = (bf16[1,64,1536]{2,1,0:T(8,128)(2,1)S(1)}, bf16[1,64,1536]{2,1,0:T(8,128)(2,1)}, u32[]{:S(2)}) copy-start(bf16[1,64,1536]{2,1,0:T(8,128)(2,1)} %gain_ref.3) | copy-start | bytes 589828
  4.6 9.1 %copy-start.6 = (bf16[128,1536]{1,0:T(8,128)(2,1)S(1)}, bf16[128,1536]{1,0:T(8,128)(2,1)}, u32[]{:S(2)}) copy-start(bf16[128,1536]{1,0:T(8,128)(2,1)} %emb_ref.1) | copy-start | bytes 1179652
  4.6 33.5 %all-to-all-start = ((f32[16,8,768]{2,1,0:T(8,128)}), f32[16,8,768]{2,1,0:T(8,128)S(1)}, u32[]{:S(2)}, u32[]{:S(2)}) async-start(f32[16,8,768]{2,1,0:T(8,128)} %get-tuple-element.19), calls=%async_computation | async-start | bytes 786432 | tf_op jit(solution)/shard_map/all_to_all | solution.py:198
  39.5 6.1 %copy-start.1 = (bf16[1,128,1536]{2,1,0:T(8,128)(2,1)S(1)}, bf16[1,128,1536]{2,1,0:T(8,128)(2,1)}, u32[]{:S(2)}) copy-start(bf16[1,128,1536]{2,1,0:T(8,128)(2,1)} %res_ref.1) | copy-start | bytes 1179652
  39.5 6.1 %copy-start.3 = (bf16[1,64,1536]{2,1,0:T(8,128)(2,1)S(1)}, bf16[1,64,1536]{2,1,0:T(8,128)(2,1)}, u32[]{:S(2)}) copy-start(bf16[1,64,1536]{2,1,0:T(8,128)(2,1)} %bias_ref.1) | copy-start | bytes 589828
  39.5 17.5 %all-to-all-start.1 = ((f32[16,8,768]{2,1,0:T(8,128)}), f32[16,8,768]{2,1,0:T(8,128)S(1)}, u32[]{:S(2)}, u32[]{:S(2)}) async-start(f32[16,8,768]{2,1,0:T(8,128)} %gain_part.1), calls=%async_computation.1 | async-start | bytes 786432 | tf_op jit(solution)/shard_map/all_to_all | solution.py:198
  47.8 14.3 %collective-permute-start.1 = (bf16[1,128,1536]{2,1,0:T(8,128)(2,1)S(1)}, bf16[1,128,1536]{2,1,0:T(8,128)(2,1)S(1)}, u32[]{:S(2)}, u32[]{:S(2)}) collective-permute-start(bf16[1,128,1536]{2,1,0:T(8,128)(2,1)S(1)} %get-tuple-element.26), channel_id=1, source_target_pairs={{0,24},{8,0},{16,8},{24,16},{1,25},{9,1},{17,9},{25,17},{2,26},{10... | collective-permute-start | bytes 1179656 | tf_op jit(solution)/shard_map/ppermute | solution.py:255
  58.1 23.0 %all-to-all-start.2 = ((f32[16,16,768]{2,1,0:T(8,128)}), f32[16,16,768]{2,1,0:T(8,128)S(1)}, u32[]{:S(2)}, u32[]{:S(2)}) async-start(f32[16,16,768]{2,1,0:T(8,128)} %add_parts.1), calls=%async_computation.2 | async-start | bytes 1572864 | tf_op jit(solution)/shard_map/all_to_all | solution.py:198

commit v6 on v5

--- a/solution.py
+++ b/solution.py
@@ -10,6 +10,8 @@
 eps = 1e-05
 bf16, f32 = jnp.bfloat16, jnp.float32
 CORES = 2
+NEAR = ("next", "row")
+NEAR_SIZES = (2, 4)
 
 VMEM = pl.BlockSpec(memory_space=pltpu.VMEM)
 SMEM = pl.BlockSpec(memory_space=pltpu.SMEM)
@@ -53,20 +55,13 @@
     return jnp.where(column[:, :langs] == lane, 1.0, 0.0).astype(bf16)
 
 
-def put_pieces(out_ref, sums):
-    pieces, height, width = out_ref.shape
-    halves = sums.shape[1] // width
-    for k in range(pieces):
-        top, left = (k // halves) * height, (k % halves) * width
-        out_ref[k] = sums[top : top + height, left : left + width]
-
-
 def bias_kernel(order_ref, lang_ref, cot_ref, out_ref, forward_ref):
     rows = forward_ref.shape[0] // MB
     for j in range(MB):
         forward_ref[rows_of(order_ref[0, j], rows), :] = cot_ref[0, j * rows : (j + 1) * rows, :]
-    langs = out_ref.shape[0] * out_ref.shape[1] * out_ref.shape[2] // forward_ref.shape[1]
-    put_pieces(out_ref, jnp.dot(members(lang_ref, langs), forward_ref[...], preferred_element_type=f32))
+    langs = out_ref.shape[0] * out_ref.shape[1]
+    sums = jnp.dot(members(lang_ref, langs), forward_ref[...], preferred_element_type=f32)
+    out_ref[...] = sums.reshape(out_ref.shape)
 
 
 def sums_kernel(first_ref, lang_ref, recv_ref, emb_ref, cot_ref, gain_ref, out_ref, x_ref, gain_scr, wide_scr):
@@ -105,16 +100,15 @@
     return jnp.transpose(tile)
 
 
-def gain_kernel(lang_ref, sums_ref, x_ref, cot_ref, out_ref, high_scr, low_scr, piece_scr, sems):
-    pieces, height, width = piece_scr.shape
-    halves = x_ref.shape[1] // width
-    langs = pieces // halves * height
+def gain_kernel(lang_ref, sums_ref, x_ref, cot_ref, out_ref, high_scr, low_scr, out_scr, sems):
+    pieces, height, width = out_ref.shape
     tokens, step = cot_ref.shape[0], 16
     figures = columns(sums_ref)
-    who = members(lang_ref, langs)
-    copies = [pltpu.make_async_copy(piece_scr.at[k], out_ref.at[k], sems.at[k]) for k in range(pieces)]
-    for half in range(halves):
-        wide = slice(half * width, (half + 1) * width)
+    who = members(lang_ref, pieces * height)
+    copies = []
+    chunk = width // sems.shape[0]
+    for i, left in enumerate(range(0, width, chunk)):
+        wide = slice(left, left + chunk)
         for top in range(0, tokens, step):
             rows = slice(top, top + step)
             center, inv = figures[rows, 0:1], figures[rows, 1:2]
@@ -125,10 +119,10 @@
         sums = jnp.dot(who, high_scr[:, wide], preferred_element_type=f32) + jnp.dot(
             who, low_scr[:, wide], preferred_element_type=f32
         )
-        for top in range(0, langs, height):
-            k = top // height * halves + half
-            piece_scr[k] = sums[top : top + height, :]
-            copies[k].start()
+        out_scr[:, :, wide] = sums.reshape(pieces, height, chunk)
+        here = pl.ds(left, chunk)
+        copies.append(pltpu.make_async_copy(out_scr.at[:, :, here], out_ref.at[:, :, here], sems.at[i]))
+        copies[-1].start()
     for copy in copies:
         copy.wait()
 
@@ -168,22 +162,25 @@
     out_ref[...] = added(parts_ref)
 
 
-def add_kernel(gain_ref, bias_ref, out_ref, total_scr, sems):
+def near_kernel(gain_ref, bias_ref, out_ref):
     height = bias_ref.shape[0]
-    total_scr[height:, :] = bias_ref[...]
-    total_scr[:height, :] = added(gain_ref)
+    out_ref[:height, :] = added(gain_ref)
+    out_ref[height:, :] = bias_ref[...]
+
+
+def add_kernel(near_ref, far_ref, out_ref, total_scr, sems):
+    total_scr[...] = near_ref[...] + far_ref[...]
     run_copies([pltpu.make_async_copy(total_scr, out_ref.at[k], sems.at[k]) for k in range(out_ref.shape[0])])
 
 
 def whole_kernel(parts_ref, gain_ref, bias_ref, sems):
-    _, halves, height, width = parts_ref.shape
-    height //= 2
-    copies = []
-    for i, out_ref in enumerate((gain_ref, bias_ref)):
-        for half in range(halves):
-            place = out_ref.at[:, :, pl.ds(half * width, width)]
-            copies.append(pltpu.make_async_copy(parts_ref.at[:, half, pl.ds(i * height, height), :], place, sems.at[i, half]))
-    run_copies(copies)
+    height = gain_ref.shape[1]
+    run_copies(
+        [
+            pltpu.make_async_copy(parts_ref.at[:, pl.ds(i * height, height), :], out_ref, sems.at[i])
+            for i, out_ref in enumerate((gain_ref, bias_ref))
+        ]
+    )
 
 
 def settle_kernel(value_ref, out_ref, sem):
@@ -195,14 +192,14 @@
 
 
 def exchanged(pieces):
-    return lax.all_to_all(pieces, "dp", 0, 0)
+    return lax.all_to_all(pieces, NEAR, 0, 0)
 
 
 def local(section_out, embedded, cot_norm, cot_res, gain, bias, lang_ids, mb_order):
     tokens, width = embedded.shape
     langs = gain.shape[1]
-    replicas = lax.axis_size("dp")
-    pieces = (replicas, 8, langs * width // (8 * replicas))
+    near = NEAR_SIZES[0] * NEAR_SIZES[1]
+    pieces = (near, langs // near, width)
     lang = lang_ids.reshape(1, tokens)
     first = (lax.axis_index("pipe") == 0).astype(jnp.int32).reshape(1)
     stages = lax.axis_size("pipe")
@@ -237,7 +234,7 @@
         gain_kernel,
         "gain_part",
         shape(pieces, f32),
-        [pltpu.VMEM((tokens, width), bf16), pltpu.VMEM((tokens, width), bf16), pltpu.VMEM(pieces, f32), sems((replicas,))],
+        [pltpu.VMEM((tokens, width), bf16), pltpu.VMEM((tokens, width), bf16), pltpu.VMEM(pieces, f32), sems((2,))],
         [VMEM, VMEM, VMEM, VMEM],
         lang, sums, x, cot,
         out_specs=HBM,
@@ -254,30 +251,25 @@
     )
     returned = lax.ppermute(back, "pipe", [(i, (i - 1) % stages) for i in range(stages)])
     gain_mine, back, bias_total = lax.optimization_barrier((gain_mine, back, bias_total))
-    both = (pieces[0], 2 * pieces[1], pieces[2])
+    both = (2 * pieces[1], width)
+    near_total = call(near_kernel, "near_parts", shape(both, f32), [], [VMEM, VMEM], gain_mine, bias_total)
+    far_total = lax.ppermute(near_total, "far_dp", [(0, 1), (1, 0)])
     totals = exchanged(
         call(
             add_kernel,
             "add_parts",
-            shape(both, f32),
-            [pltpu.VMEM(both[1:], f32), sems((replicas,))],
+            shape((near, *both), f32),
+            [pltpu.VMEM(both, f32), sems((near,))],
             [VMEM, VMEM],
-            gain_mine, bias_total,
+            near_total, far_total,
             out_specs=HBM,
         )
     )
     returned = call(settle_kernel, "settle", shape(back.shape, bf16), [sems(())], [VMEM], returned, out_specs=HBM, cover=10**11)
     totals, returned = lax.optimization_barrier((totals, returned))
-    halves = width // pieces[2]
-    grads = shape((replicas // halves, pieces[1], width), f32)
+    grads = shape(pieces, f32)
     gain_grad, bias_grad = call(
-        whole_kernel,
-        "whole_grads",
-        (grads, grads),
-        [sems((2, halves))],
-        [VMEM],
-        totals.reshape(replicas // halves, halves, *both[1:]),
-        out_specs=(HBM, HBM),
+        whole_kernel, "whole_grads", (grads, grads), [sems((2,))], [VMEM], totals, out_specs=(HBM, HBM)
     )
     gain_grad, bias_grad = (g.reshape(1, langs, width) for g in (gain_grad, bias_grad))
     return normed, returned, gain_grad, bias_grad
@@ -285,24 +277,26 @@
 
 def solution(mesh):
     dp, pipe, tensor = (mesh.shape[a] for a in ("dp", "pipe", "tensor"))
-    split = Mesh(mesh.devices.reshape(dp, pipe, tensor // CORES, CORES), ("dp", "pipe", "far", "core"))
-    tensor = ("far", "core")
+    names = ("far_dp", *NEAR, "pipe", "far", "core")
+    far_dp = dp // (NEAR_SIZES[0] * NEAR_SIZES[1])
+    split = Mesh(mesh.devices.reshape(far_dp, *NEAR_SIZES, pipe, tensor // CORES, CORES), names)
+    dp, tensor = ("far_dp", *NEAR), ("far", "core")
     return jax.shard_map(
         local,
         mesh=split,
         in_specs=(
-            P("pipe", "dp", tensor),
-            P("dp", tensor),
-            P("pipe", "dp", tensor),
-            P("pipe", "dp", tensor),
+            P("pipe", dp, tensor),
+            P(dp, tensor),
+            P("pipe", dp, tensor),
+            P("pipe", dp, tensor),
             P("pipe", None, tensor),
             P("pipe", None, tensor),
-            P("dp"),
-            P("dp", None),
+            P(dp),
+            P(dp, None),
         ),
         out_specs=(
-            P("pipe", "dp", tensor),
-            P("pipe", "dp", tensor),
+            P("pipe", dp, tensor),
+            P("pipe", dp, tensor),
             P("pipe", None, tensor),
             P("pipe", None, tensor),
         ),

time: 83.5 us -> 76.1 us (0.911); the launches traced: 82 us -> 75.5 us
  waiting for transfers between devices: 24.6 us -> 19.6 us
  starting transfers between devices: 23.3 us -> 22.1 us
    all_to_all x3, waiting for transfers between devices: 24.2 us -> 11.3 us  [exchanged(): return lax.all_to_all(pieces, NEAR, 0, 0)]
    ppermute x0 -> x1, waiting for transfers between devices: none -> 5.08 us  [local(): far_total = lax.ppermute(near_total, 'far_dp', [(0, 1), (1, 0)])]
    all_to_all x3, starting transfers between devices: 18.8 us -> 14.6 us  [exchanged(): return lax.all_to_all(pieces, NEAR, 0, 0)]
    ppermute x0 -> x1, starting transfers between devices: none -> 3.38 us  [local(): far_total = lax.ppermute(near_total, 'far_dp', [(0, 1), (1, 0)])]
    ppermute x1, waiting for transfers between devices: 0.34 us -> 3.16 us  [local(): lax.ppermute(section_out, 'pipe', [(i, i + 1) for i in range(stages - 1)])]
    pallas_call x8 -> x9, Pallas kernels: 8.53 us -> 8.38 us  [call(): pl.pallas_call(kernel, name=name, out_shape=outs, in_specs=in_specs, out_...]
  transfers between devices with their start and end apart: 5 -> 6, of which waited for: 3 -> 4; matrix products, arithmetic and copies ran while one was open for 0% -> 0% of each run, Pallas kernels for 8% -> 8%
where the time goes in v6:
time: 76.1 us; the launch traced here: 75.5 us
  blocking collectives  23.7 us (31%)
  starting transfers between devices  22.1 us (29%)
  waiting for transfers between devices  19.6 us (26%)
  Pallas kernels  8.38 us (11%)
  local copies, waits for them, and re-layouts  1.02 us (1%)
  between operations  0.78 us (1%)
    psum x2, blocking collectives, local(): sums = lax.psum(lax.psum(sums, 'core'), 'far')  23.7 us
    all_to_all x3, starting transfers between devices, exchanged(): return lax.all_to_all(pieces, NEAR, 0, 0)  14.6 us
    all_to_all x3, waiting for transfers between devices, exchanged(): return lax.all_to_all(pieces, NEAR, 0, 0)  11.3 us
    pallas_call x9, Pallas kernels, call(): pl.pallas_call(kernel, name=name, out_shape=outs, in_specs=in_specs, out_...  8.38 us
    ppermute x1, waiting for transfers between devices, local(): far_total = lax.ppermute(near_total, 'far_dp', [(0, 1), (1, 0)])  5.08 us
    ppermute x1, starting transfers between devices, local(): far_total = lax.ppermute(near_total, 'far_dp', [(0, 1), (1, 0)])  3.38 us
    ppermute x1, waiting for transfers between devices, local(): lax.ppermute(section_out, 'pipe', [(i, i + 1) for i in range(stages - 1)])  3.16 us
    ppermute x1, starting transfers between devices, local(): lax.ppermute(back, 'pipe', [(i, (i - 1) % stages) for i in range(stages)])  2.72 us
  transfers between devices with their start and end apart: 6, of which 4 were waited for; matrix products, arithmetic and copies ran while one was open for 0% of the time, Pallas kernels for 8%

profile of v6, /device:TPU:6, one launch (start us, length us, event | category | flops | bytes accessed | tf_op | source)
XLA Modules:
  0.0 75.5 jit_solution(6608268887704774082)
XLA Ops:
  0.6 0.0 copy-start.5
  0.6 0.0 copy-start.4
  0.7 1.4 %collective-permute-start = (bf16[1,128,1536]{2,1,0:T(8,128)(2,1)}, bf16[1,128,1536]{2,1,0:T(8,128)(2,1)S(1)}, u32[]{:S(2)}, u32[]{:S(2)}) collective-permute-start(bf16[1,128,1536]{2,1,0:T(8,128)(2,1)} %param.8), channel_id=1, source_target_pairs={{0,8},{8,16},{16,24},{1,9},{9,17},{17,25},{2,10},{10,18},{18,26},{... | collective-permute-start | bytes 1179656 | tf_op jit(solution)/shard_map/ppermute | solution.py:206
  2.1 0.0 copy-done.5
  2.1 0.0 copy-done.4
  2.1 0.0 copy-start
  2.1 1.0 %copy-done = bf16[1,128,1536]{2,1,0:T(8,128)(2,1)S(1)} copy-done((bf16[1,128,1536]{2,1,0:T(8,128)(2,1)S(1)}, bf16[1,128,1536]{2,1,0:T(8,128)(2,1)}, u32[]{:S(2)}) %copy-start) | copy-done | bytes 393240
  3.1 1.5 %bias_part.1 = (f32[8,8,1536]{2,1,0:T(8,128)}, bf16[128,1536]{1,0:T(8,128)(2,1)S(1)}) custom-call(s32[1,4]{1,0:T(1,128)S(1)} %copy-done.5, s32[1,128]{1,0:T(1,128)S(1)} %bitcast.4, bf16[1,128,1536]{2,1,0:T(8,128)(2,1)S(1)} %copy-done), custom_call_target="tpu_custom_call" | custom-call | tf_op jit(solution)/shard_map/bias_part/pallas_call | solution.py:22
  4.6 0.0 copy-start.2
  4.6 0.0 copy-start.6
  4.6 6.0 %all-to-all-start = ((f32[8,8,1536]{2,1,0:T(8,128)}), f32[8,8,1536]{2,1,0:T(8,128)S(1)}, u32[]{:S(2)}, u32[]{:S(2)}) async-start(f32[8,8,1536]{2,1,0:T(8,128)} %get-tuple-element.19), calls=%async_computation | async-start | bytes 786432 | tf_op jit(solution)/shard_map/all_to_all | solution.py:195
  10.6 3.2 %collective-permute-done.recv_ref = bf16[1,128,1536]{2,1,0:T(8,128)(2,1)S(1)} collective-permute-done((bf16[1,128,1536]{2,1,0:T(8,128)(2,1)}, bf16[1,128,1536]{2,1,0:T(8,128)(2,1)S(1)}, u32[]{:S(2)}, u32[]{:S(2)}) %collective-permute-start) | collective-permute-done | bytes 393248 | tf_op jit(solution)/shard_map/ppermute | solution.py:206
  13.7 0.0 copy-done.2
  13.7 0.0 copy-done.6
  13.7 0.7 token_sums.1
  14.4 2.5 %psum.14 = f32[8,128]{1,0:T(8,128)S(1)} all-reduce(f32[8,128]{1,0:T(8,128)S(1)} %get-tuple-element.22), channel_id=1, replica_groups=mesh['far_dp'=2,'next'=2,'row'=4,'pipe'=4,'far'=4,'core'=2] {'core'}, use_global_device_ids=true, to_apply=%region_0.0 | all-reduce | flops 1024 | bytes 8192 | tf_op jit(solution)/shard_map/psum | solution.py:230
  16.9 21.3 %psum.15.sums_ref = f32[8,128]{1,0:T(8,128)S(1)} all-reduce(f32[8,128]{1,0:T(8,128)S(1)} %psum.14), channel_id=1, replica_groups=mesh['far_dp'=2,'next'=2,'row'=4,'pipe'=4,'far'=4,'core'=2] {'far'}, use_global_device_ids=true, to_apply=%region_1.0 | all-reduce | flops 1024 | bytes 8192 | tf_op jit(solution)/shard_map/psum | solution.py:230
  38.2 0.0 all-to-all-done.parts_ref
  38.2 1.2 %gain_part.1 = f32[8,8,1536]{2,1,0:T(8,128)} custom-call(s32[1,128]{1,0:T(1,128)S(1)} %bitcast.6, f32[8,128]{1,0:T(8,128)S(1)} %psum.15.sums_ref, bf16[128,1536]{1,0:T(8,128)(2,1)S(1)} %get-tuple-element.24.x_ref, bf16[128,1536]{1,0:T(8,128)(2,1)S(1)} %get-tuple-element.21.cot_ref), custom_call_target="tpu_custom_call" | custom-call | tf_op jit(solution)/shard_map/gain_part/pallas_call | solution.py:22
  39.4 0.0 copy-start.1
  39.4 0.0 copy-start.3
  39.4 5.0 %all-to-all-start.1 = ((f32[8,8,1536]{2,1,0:T(8,128)}), f32[8,8,1536]{2,1,0:T(8,128)S(1)}, u32[]{:S(2)}, u32[]{:S(2)}) async-start(f32[8,8,1536]{2,1,0:T(8,128)} %gain_part.1), calls=%async_computation.1 | async-start | bytes 786432 | tf_op jit(solution)/shard_map/all_to_all | solution.py:195
  44.5 0.0 copy-done.1
  44.5 0.0 copy-done.3
  44.5 2.3 %norm_and_grad.1 = (bf16[1,128,1536]{2,1,0:T(8,128)(2,1)}, bf16[1,128,1536]{2,1,0:T(8,128)(2,1)S(1)}) custom-call(s32[1,4]{1,0:T(1,128)S(1)} %copy-done.5, s32[1,128]{1,0:T(1,128)S(1)} %bitcast.7, f32[8,128]{1,0:T(8,128)S(1)} %psum.15.sums_ref, bf16[128,1536]{1,0:T(8,128)(2,1)S(1)} %get-tuple-element.24.x_ref, ...), custom_call_target="tpu_custom_call" | custom-call | tf_op jit(solution)/shard_map/norm_and_grad/pallas_call | solution.py:22
  46.7 2.7 %collective-permute-start.2 = (bf16[1,128,1536]{2,1,0:T(8,128)(2,1)S(1)}, bf16[1,128,1536]{2,1,0:T(8,128)(2,1)S(1)}, u32[]{:S(2)}, u32[]{:S(2)}) collective-permute-start(bf16[1,128,1536]{2,1,0:T(8,128)(2,1)S(1)} %get-tuple-element.26), channel_id=1, source_target_pairs={{0,24},{8,0},{16,8},{24,16},{1,25},{9,1},{17,9},{25,17},{2,26},{10... | collective-permute-start | bytes 1179656 | tf_op jit(solution)/shard_map/ppermute | solution.py:252
  49.5 2.7 %all-to-all-done.1.gain_ref = f32[8,8,1536]{2,1,0:T(8,128)S(1)} async-done(((f32[8,8,1536]{2,1,0:T(8,128)}), f32[8,8,1536]{2,1,0:T(8,128)S(1)}, u32[]{:S(2)}, u32[]{:S(2)}) %all-to-all-start.1) | async-done | bytes 393248 | tf_op jit(solution)/shard_map/all_to_all | solution.py:195
  52.2 3.4 %collective-permute-start.1 = (f32[16,1536]{1,0:T(8,128)S(1)}, f32[16,1536]{1,0:T(8,128)S(1)}, u32[]{:S(2)}, u32[]{:S(2)}) collective-permute-start(f32[16,1536]{1,0:T(8,128)S(1)} %near_parts.1.near_ref), channel_id=1, source_target_pairs={{0,256},{256,0},{1,257},{257,1},{2,258},{258,2},{3,259},{259,3},{4... | collective-permute-start | bytes 294920 | tf_op jit(solution)/shard_map/ppermute | solution.py:256
  55.6 5.1 %collective-permute-done.1.far_ref = f32[16,1536]{1,0:T(8,128)S(1)} collective-permute-done((f32[16,1536]{1,0:T(8,128)S(1)}, f32[16,1536]{1,0:T(8,128)S(1)}, u32[]{:S(2)}, u32[]{:S(2)}) %collective-permute-start.1) | collective-permute-done | bytes 98336 | tf_op jit(solution)/shard_map/ppermute | solution.py:256
  60.7 1.0 %add_parts.1 = f32[8,16,1536]{2,1,0:T(8,128)} custom-call(f32[16,1536]{1,0:T(8,128)S(1)} %near_parts.1.near_ref, f32[16,1536]{1,0:T(8,128)S(1)} %collective-permute-done.1.far_ref), custom_call_target="tpu_custom_call" | custom-call | tf_op jit(solution)/shard_map/add_parts/pallas_call | solution.py:22
  61.7 3.6 %all-to-all-start.2 = ((f32[8,16,1536]{2,1,0:T(8,128)}), f32[8,16,1536]{2,1,0:T(8,128)S(1)}, u32[]{:S(2)}, u32[]{:S(2)}) async-start(f32[8,16,1536]{2,1,0:T(8,128)} %add_parts.1), calls=%async_computation.2 | async-start | bytes 1572864 | tf_op jit(solution)/shard_map/all_to_all | solution.py:195
  65.3 0.0 collective-permute-done.2.value_ref
  65.3 0.8 %settle.1 = bf16[1,128,1536]{2,1,0:T(8,128)(2,1)} custom-call(bf16[1,128,1536]{2,1,0:T(8,128)(2,1)S(1)} %collective-permute-done.2.value_ref), custom_call_target="tpu_custom_call" | custom-call | flops 99999997952 | tf_op jit(solution)/shard_map/settle/pallas_call | solution.py:22
  66.0 8.6 %all-to-all-done.2.parts_ref = f32[8,16,1536]{2,1,0:T(8,128)S(1)} async-done(((f32[8,16,1536]{2,1,0:T(8,128)}), f32[8,16,1536]{2,1,0:T(8,128)S(1)}, u32[]{:S(2)}, u32[]{:S(2)}) %all-to-all-start.2) | async-done | bytes 786464 | tf_op jit(solution)/shard_map/all_to_all | solution.py:195
  74.7 0.9 %whole_grads.1 = (f32[8,8,1536]{2,1,0:T(8,128)}, f32[8,8,1536]{2,1,0:T(8,128)}) custom-call(f32[8,16,1536]{2,1,0:T(8,128)S(1)} %all-to-all-done.2.parts_ref), custom_call_target="tpu_custom_call" | custom-call | tf_op jit(solution)/shard_map/whole_grads/pallas_call | solution.py:22
  (2 shorter events, 0.0 us)
Async XLA Ops:
  0.6 1.5 %copy-start.5 = (s32[1,4]{1,0:T(1,128)S(1)}, s32[1,4]{1,0:T(1,128)}, u32[]{:S(2)}) copy-start(s32[1,4]{1,0:T(1,128)} %order_ref.3) | copy-start | bytes 52
  0.6 1.5 %copy-start.4 = (s32[128]{0:T(128)S(1)}, s32[128]{0:T(128)}, u32[]{:S(2)}) copy-start(s32[128]{0:T(128)} %param.14) | copy-start | bytes 1540
  0.7 13.1 %collective-permute-start = (bf16[1,128,1536]{2,1,0:T(8,128)(2,1)}, bf16[1,128,1536]{2,1,0:T(8,128)(2,1)S(1)}, u32[]{:S(2)}, u32[]{:S(2)}) collective-permute-start(bf16[1,128,1536]{2,1,0:T(8,128)(2,1)} %param.8), channel_id=1, source_target_pairs={{0,8},{8,16},{16,24},{1,9},{9,17},{17,25},{2,10},{10,18},{18,26},{... | collective-permute-start | bytes 1179656 | tf_op jit(solution)/shard_map/ppermute | solution.py:206
  2.1 1.0 %copy-start = (bf16[1,128,1536]{2,1,0:T(8,128)(2,1)S(1)}, bf16[1,128,1536]{2,1,0:T(8,128)(2,1)}, u32[]{:S(2)}) copy-start(bf16[1,128,1536]{2,1,0:T(8,128)(2,1)} %cot_ref.1) | copy-start | bytes 1179652
  4.6 9.1 %copy-start.2 = (bf16[1,64,1536]{2,1,0:T(8,128)(2,1)S(1)}, bf16[1,64,1536]{2,1,0:T(8,128)(2,1)}, u32[]{:S(2)}) copy-start(bf16[1,64,1536]{2,1,0:T(8,128)(2,1)} %gain_ref.3) | copy-start | bytes 589828
  4.6 9.1 %copy-start.6 = (bf16[128,1536]{1,0:T(8,128)(2,1)S(1)}, bf16[128,1536]{1,0:T(8,128)(2,1)}, u32[]{:S(2)}) copy-start(bf16[128,1536]{1,0:T(8,128)(2,1)} %emb_ref.1) | copy-start | bytes 1179652
  4.6 33.5 %all-to-all-start = ((f32[8,8,1536]{2,1,0:T(8,128)}), f32[8,8,1536]{2,1,0:T(8,128)S(1)}, u32[]{:S(2)}, u32[]{:S(2)}) async-start(f32[8,8,1536]{2,1,0:T(8,128)} %get-tuple-element.19), calls=%async_computation | async-start | bytes 786432 | tf_op jit(solution)/shard_map/all_to_all | solution.py:195
  39.4 5.1 %copy-start.1 = (bf16[1,128,1536]{2,1,0:T(8,128)(2,1)S(1)}, bf16[1,128,1536]{2,1,0:T(8,128)(2,1)}, u32[]{:S(2)}) copy-start(bf16[1,128,1536]{2,1,0:T(8,128)(2,1)} %res_ref.1) | copy-start | bytes 1179652
  39.4 5.1 %copy-start.3 = (bf16[1,64,1536]{2,1,0:T(8,128)(2,1)S(1)}, bf16[1,64,1536]{2,1,0:T(8,128)(2,1)}, u32[]{:S(2)}) copy-start(bf16[1,64,1536]{2,1,0:T(8,128)(2,1)} %bias_ref.1) | copy-start | bytes 589828
  39.4 12.8 %all-to-all-start.1 = ((f32[8,8,1536]{2,1,0:T(8,128)}), f32[8,8,1536]{2,1,0:T(8,128)S(1)}, u32[]{:S(2)}, u32[]{:S(2)}) async-start(f32[8,8,1536]{2,1,0:T(8,128)} %gain_part.1), calls=%async_computation.1 | async-start | bytes 786432 | tf_op jit(solution)/shard_map/all_to_all | solution.py:195
  46.7 18.5 %collective-permute-start.2 = (bf16[1,128,1536]{2,1,0:T(8,128)(2,1)S(1)}, bf16[1,128,1536]{2,1,0:T(8,128)(2,1)S(1)}, u32[]{:S(2)}, u32[]{:S(2)}) collective-permute-start(bf16[1,128,1536]{2,1,0:T(8,128)(2,1)S(1)} %get-tuple-element.26), channel_id=1, source_target_pairs={{0,24},{8,0},{16,8},{24,16},{1,25},{9,1},{17,9},{25,17},{2,26},{10... | collective-permute-start | bytes 1179656 | tf_op jit(solution)/shard_map/ppermute | solution.py:252
  52.2 8.5 %collective-permute-start.1 = (f32[16,1536]{1,0:T(8,128)S(1)}, f32[16,1536]{1,0:T(8,128)S(1)}, u32[]{:S(2)}, u32[]{:S(2)}) collective-permute-start(f32[16,1536]{1,0:T(8,128)S(1)} %near_parts.1.near_ref), channel_id=1, source_target_pairs={{0,256},{256,0},{1,257},{257,1},{2,258},{258,2},{3,259},{259,3},{4... | collective-permute-start | bytes 294920 | tf_op jit(solution)/shard_map/ppermute | solution.py:256
  61.7 13.0 %all-to-all-start.2 = ((f32[8,16,1536]{2,1,0:T(8,128)}), f32[8,16,1536]{2,1,0:T(8,128)S(1)}, u32[]{:S(2)}, u32[]{:S(2)}) async-start(f32[8,16,1536]{2,1,0:T(8,128)} %add_parts.1), calls=%async_computation.2 | async-start | bytes 1572864 | tf_op jit(solution)/shard_map/all_to_all | solution.py:195

commit v7 on v6

--- a/solution.py
+++ b/solution.py
@@ -162,14 +162,10 @@
     out_ref[...] = added(parts_ref)
 
 
-def near_kernel(gain_ref, bias_ref, out_ref):
-    height = bias_ref.shape[0]
-    out_ref[:height, :] = added(gain_ref)
-    out_ref[height:, :] = bias_ref[...]
-
-
-def add_kernel(near_ref, far_ref, out_ref, total_scr, sems):
-    total_scr[...] = near_ref[...] + far_ref[...]
+def add_kernel(gain_ref, gain_far_ref, bias_ref, bias_far_ref, out_ref, total_scr, sems):
+    height = gain_ref.shape[0]
+    total_scr[:height, :] = gain_ref[...] + gain_far_ref[...]
+    total_scr[height:, :] = bias_ref[...] + bias_far_ref[...]
     run_copies([pltpu.make_async_copy(total_scr, out_ref.at[k], sems.at[k]) for k in range(out_ref.shape[0])])
 
 
@@ -193,6 +189,10 @@
 
 def exchanged(pieces):
     return lax.all_to_all(pieces, NEAR, 0, 0)
+
+
+def from_far(total):
+    return lax.ppermute(total, "far_dp", [(0, 1), (1, 0)])
 
 
 def local(section_out, embedded, cot_norm, cot_res, gain, bias, lang_ids, mb_order):
@@ -240,7 +240,8 @@
         out_specs=HBM,
     )
     gain_mine = exchanged(gain_part)
-    bias_total = call(total_kernel, "bias_total", shape(pieces[1:], f32), [], [VMEM], bias_mine)
+    bias_near = call(total_kernel, "bias_near", shape(pieces[1:], f32), [], [VMEM], bias_mine)
+    bias_far = from_far(bias_near)
     normed, back = call(
         outs_kernel,
         "norm_and_grad",
@@ -249,20 +250,22 @@
         [SMEM, VMEM, VMEM, VMEM, VMEM, VMEM, VMEM, VMEM],
         mb_order, lang, sums, x, cot, cot_res, gain, bias,
     )
+    gain_mine, back, bias_far = lax.optimization_barrier((gain_mine, back, bias_far))
+    gain_near = call(total_kernel, "gain_near", shape(pieces[1:], f32), [], [VMEM], gain_mine)
+    gain_far = from_far(gain_near)
+    gain_near, back = lax.optimization_barrier((gain_near, back))
     returned = lax.ppermute(back, "pipe", [(i, (i - 1) % stages) for i in range(stages)])
-    gain_mine, back, bias_total = lax.optimization_barrier((gain_mine, back, bias_total))
     both = (2 * pieces[1], width)
-    near_total = call(near_kernel, "near_parts", shape(both, f32), [], [VMEM, VMEM], gain_mine, bias_total)
-    far_total = lax.ppermute(near_total, "far_dp", [(0, 1), (1, 0)])
     totals = exchanged(
         call(
             add_kernel,
             "add_parts",
             shape((near, *both), f32),
             [pltpu.VMEM(both, f32), sems((near,))],
-            [VMEM, VMEM],
-            near_total, far_total,
+            [VMEM, VMEM, VMEM, VMEM],
+            gain_near, gain_far, bias_near, bias_far,
             out_specs=HBM,
+            cover=10**11,
         )
     )
     returned = call(settle_kernel, "settle", shape(back.shape, bf16), [sems(())], [VMEM], returned, out_specs=HBM, cover=10**11)

time: 76.1 us -> 76.9 us (1.011); the launches traced: 75.5 us -> 75.3 us
  waiting for transfers between devices: 19.6 us -> 15.5 us
  starting transfers between devices: 22.1 us -> 26 us
    ppermute x1 -> x2, starting transfers between devices: 3.38 us -> 6.89 us  [from_far(): return lax.ppermute(total, 'far_dp', [(0, 1), (1, 0)])]
    all_to_all x3, waiting for transfers between devices: 11.3 us -> 8.05 us  [exchanged(): return lax.all_to_all(pieces, NEAR, 0, 0)]
    ppermute x1 -> x2, waiting for transfers between devices: 5.08 us -> 2.49 us  [from_far(): return lax.ppermute(total, 'far_dp', [(0, 1), (1, 0)])]
    ppermute x1, waiting for transfers between devices: 0.01 us -> 1.82 us  [local(): lax.ppermute(back, 'pipe', [(i, (i - 1) % stages) for i in range(stages)])]
  transfers between devices with their start and end apart: 6 -> 7, of which waited for: 4 -> 6; matrix products, arithmetic and copies ran while one was open for 0% -> 0% of each run, Pallas kernels for 8% -> 8%
where the time goes in v7:
time: 76.9 us; the launch traced here: 75.3 us
  starting transfers between devices  26 us (34%)
  blocking collectives  23.7 us (31%)
  waiting for transfers between devices  15.5 us (20%)
  Pallas kernels  8.37 us (11%)
  local copies, waits for them, and re-layouts  1.01 us (1%)
  between operations  0.77 us (1%)
    psum x2, blocking collectives, local(): sums = lax.psum(lax.psum(sums, 'core'), 'far')  23.7 us
    all_to_all x3, starting transfers between devices, exchanged(): return lax.all_to_all(pieces, NEAR, 0, 0)  14.9 us
    pallas_call x9, Pallas kernels, call(): pl.pallas_call(kernel, name=name, out_shape=outs, in_specs=in_specs, out_...  8.37 us
    all_to_all x3, waiting for transfers between devices, exchanged(): return lax.all_to_all(pieces, NEAR, 0, 0)  8.05 us
    ppermute x2, starting transfers between devices, from_far(): return lax.ppermute(total, 'far_dp', [(0, 1), (1, 0)])  6.89 us
    ppermute x1, waiting for transfers between devices, local(): lax.ppermute(section_out, 'pipe', [(i, i + 1) for i in range(stages - 1)])  3.16 us
    ppermute x1, starting transfers between devices, local(): lax.ppermute(back, 'pipe', [(i, (i - 1) % stages) for i in range(stages)])  2.75 us
    ppermute x2, waiting for transfers between devices, from_far(): return lax.ppermute(total, 'far_dp', [(0, 1), (1, 0)])  2.49 us
  transfers between devices with their start and end apart: 7, of which 6 were waited for; matrix products, arithmetic and copies ran while one was open for 0% of the time, Pallas kernels for 8%

profile of v7, /device:TPU:6, one launch (start us, length us, event | category | flops | bytes accessed | tf_op | source)
XLA Modules:
  0.0 75.3 jit_solution(7708165163931460570)
XLA Ops:
  0.6 0.0 copy-start.5
  0.6 0.0 copy-start.4
  0.7 1.4 %collective-permute-start = (bf16[1,128,1536]{2,1,0:T(8,128)(2,1)}, bf16[1,128,1536]{2,1,0:T(8,128)(2,1)S(1)}, u32[]{:S(2)}, u32[]{:S(2)}) collective-permute-start(bf16[1,128,1536]{2,1,0:T(8,128)(2,1)} %param.8), channel_id=1, source_target_pairs={{0,8},{8,16},{16,24},{1,9},{9,17},{17,25},{2,10},{10,18},{18,26},{... | collective-permute-start | bytes 1179656 | tf_op jit(solution)/shard_map/ppermute | solution.py:206
  2.1 0.0 copy-done.5
  2.1 0.0 copy-done.4
  2.1 0.0 copy-start
  2.1 1.0 %copy-done = bf16[1,128,1536]{2,1,0:T(8,128)(2,1)S(1)} copy-done((bf16[1,128,1536]{2,1,0:T(8,128)(2,1)S(1)}, bf16[1,128,1536]{2,1,0:T(8,128)(2,1)}, u32[]{:S(2)}) %copy-start) | copy-done | bytes 393240
  3.1 1.5 %bias_part.1 = (f32[8,8,1536]{2,1,0:T(8,128)}, bf16[128,1536]{1,0:T(8,128)(2,1)S(1)}) custom-call(s32[1,4]{1,0:T(1,128)S(1)} %copy-done.5, s32[1,128]{1,0:T(1,128)S(1)} %bitcast.4, bf16[1,128,1536]{2,1,0:T(8,128)(2,1)S(1)} %copy-done), custom_call_target="tpu_custom_call" | custom-call | tf_op jit(solution)/shard_map/bias_part/pallas_call | solution.py:22
  4.6 0.0 copy-start.2
  4.6 0.0 copy-start.6
  4.6 6.0 %all-to-all-start = ((f32[8,8,1536]{2,1,0:T(8,128)}), f32[8,8,1536]{2,1,0:T(8,128)S(1)}, u32[]{:S(2)}, u32[]{:S(2)}) async-start(f32[8,8,1536]{2,1,0:T(8,128)} %get-tuple-element.22), calls=%async_computation | async-start | bytes 786432 | tf_op jit(solution)/shard_map/all_to_all | solution.py:191
  10.6 3.2 %collective-permute-done.recv_ref = bf16[1,128,1536]{2,1,0:T(8,128)(2,1)S(1)} collective-permute-done((bf16[1,128,1536]{2,1,0:T(8,128)(2,1)}, bf16[1,128,1536]{2,1,0:T(8,128)(2,1)S(1)}, u32[]{:S(2)}, u32[]{:S(2)}) %collective-permute-start) | collective-permute-done | bytes 393248 | tf_op jit(solution)/shard_map/ppermute | solution.py:206
  13.7 0.0 copy-done.2
  13.7 0.0 copy-done.6
  13.7 0.0 copy-start.3
  13.7 0.7 token_sums.1
  14.4 2.5 %psum.14 = f32[8,128]{1,0:T(8,128)S(1)} all-reduce(f32[8,128]{1,0:T(8,128)S(1)} %get-tuple-element.25), channel_id=1, replica_groups=mesh['far_dp'=2,'next'=2,'row'=4,'pipe'=4,'far'=4,'core'=2] {'core'}, use_global_device_ids=true, to_apply=%region_0.0 | all-reduce | flops 1024 | bytes 8192 | tf_op jit(solution)/shard_map/psum | solution.py:230
  16.9 21.2 %psum.15.sums_ref = f32[8,128]{1,0:T(8,128)S(1)} all-reduce(f32[8,128]{1,0:T(8,128)S(1)} %psum.14), channel_id=1, replica_groups=mesh['far_dp'=2,'next'=2,'row'=4,'pipe'=4,'far'=4,'core'=2] {'far'}, use_global_device_ids=true, to_apply=%region_1.0 | all-reduce | flops 1024 | bytes 8192 | tf_op jit(solution)/shard_map/psum | solution.py:230
  38.1 0.0 all-to-all-done.parts_ref
  38.1 1.2 %gain_part.1 = f32[8,8,1536]{2,1,0:T(8,128)} custom-call(s32[1,128]{1,0:T(1,128)S(1)} %bitcast.6, f32[8,128]{1,0:T(8,128)S(1)} %psum.15.sums_ref, bf16[128,1536]{1,0:T(8,128)(2,1)S(1)} %get-tuple-element.27.x_ref, bf16[128,1536]{1,0:T(8,128)(2,1)S(1)} %get-tuple-element.24.cot_ref), custom_call_target="tpu_custom_call" | custom-call | tf_op jit(solution)/shard_map/gain_part/pallas_call | solution.py:22
  39.4 4.9 %all-to-all-start.1 = ((f32[8,8,1536]{2,1,0:T(8,128)}), f32[8,8,1536]{2,1,0:T(8,128)S(1)}, u32[]{:S(2)}, u32[]{:S(2)}) async-start(f32[8,8,1536]{2,1,0:T(8,128)} %gain_part.1), calls=%async_computation.1 | async-start | bytes 786432 | tf_op jit(solution)/shard_map/all_to_all | solution.py:191
  44.3 0.0 copy-start.1
  44.3 3.5 %collective-permute-start.1 = (f32[8,1536]{1,0:T(8,128)S(1)}, f32[8,1536]{1,0:T(8,128)S(1)}, u32[]{:S(2)}, u32[]{:S(2)}) collective-permute-start(f32[8,1536]{1,0:T(8,128)S(1)} %bias_near.1.bias_ref), channel_id=1, source_target_pairs={{0,256},{256,0},{1,257},{257,1},{2,258},{258,2},{3,259},{259,3},{4... | collective-permute-start | bytes 147464 | tf_op jit(solution)/shard_map/ppermute | solution.py:195
  47.9 0.0 copy-done.3
  47.9 0.0 copy-done.1
  47.9 2.3 %norm_and_grad.1 = (bf16[1,128,1536]{2,1,0:T(8,128)(2,1)}, bf16[1,128,1536]{2,1,0:T(8,128)(2,1)S(1)}) custom-call(s32[1,4]{1,0:T(1,128)S(1)} %copy-done.5, s32[1,128]{1,0:T(1,128)S(1)} %bitcast.7, f32[8,128]{1,0:T(8,128)S(1)} %psum.15.sums_ref, bf16[128,1536]{1,0:T(8,128)(2,1)S(1)} %get-tuple-element.27.x_ref, ...), custom_call_target="tpu_custom_call" | custom-call | tf_op jit(solution)/shard_map/norm_and_grad/pallas_call | solution.py:22
  50.1 1.2 %collective-permute-done.1.bias_far_ref = f32[8,1536]{1,0:T(8,128)S(1)} collective-permute-done((f32[8,1536]{1,0:T(8,128)S(1)}, f32[8,1536]{1,0:T(8,128)S(1)}, u32[]{:S(2)}, u32[]{:S(2)}) %collective-permute-start.1) | collective-permute-done | bytes 49184 | tf_op jit(solution)/shard_map/ppermute | solution.py:195
  51.3 1.2 %all-to-all-done.1.parts_ref = f32[8,8,1536]{2,1,0:T(8,128)S(1)} async-done(((f32[8,8,1536]{2,1,0:T(8,128)}), f32[8,8,1536]{2,1,0:T(8,128)S(1)}, u32[]{:S(2)}, u32[]{:S(2)}) %all-to-all-start.1) | async-done | bytes 393248 | tf_op jit(solution)/shard_map/all_to_all | solution.py:191
  52.5 3.4 %collective-permute-start.2 = (f32[8,1536]{1,0:T(8,128)S(1)}, f32[8,1536]{1,0:T(8,128)S(1)}, u32[]{:S(2)}, u32[]{:S(2)}) collective-permute-start(f32[8,1536]{1,0:T(8,128)S(1)} %gain_near.1.gain_ref), channel_id=1, source_target_pairs={{0,256},{256,0},{1,257},{257,1},{2,258},{258,2},{3,259},{259,3},{4... | collective-permute-start | bytes 147464 | tf_op jit(solution)/shard_map/ppermute | solution.py:195
  55.9 2.7 %collective-permute-start.3 = (bf16[1,128,1536]{2,1,0:T(8,128)(2,1)S(1)}, bf16[1,128,1536]{2,1,0:T(8,128)(2,1)S(1)}, u32[]{:S(2)}, u32[]{:S(2)}) collective-permute-start(bf16[1,128,1536]{2,1,0:T(8,128)(2,1)S(1)} %get-tuple-element.35), channel_id=1, source_target_pairs={{0,24},{8,0},{16,8},{24,16},{1,25},{9,1},{17,9},{25,17},{2,26},{10... | collective-permute-start | bytes 1179656 | tf_op jit(solution)/shard_map/ppermute | solution.py:257
  58.7 1.3 %collective-permute-done.2.gain_far_ref = f32[8,1536]{1,0:T(8,128)S(1)} collective-permute-done((f32[8,1536]{1,0:T(8,128)S(1)}, f32[8,1536]{1,0:T(8,128)S(1)}, u32[]{:S(2)}, u32[]{:S(2)}) %collective-permute-start.2) | collective-permute-done | bytes 49184 | tf_op jit(solution)/shard_map/ppermute | solution.py:195
  59.9 1.0 %add_parts.1 = f32[8,16,1536]{2,1,0:T(8,128)} custom-call(f32[8,1536]{1,0:T(8,128)S(1)} %gain_near.1.gain_ref, f32[8,1536]{1,0:T(8,128)S(1)} %collective-permute-done.2.gain_far_ref, f32[8,1536]{1,0:T(8,128)S(1)} %bias_near.1.bias_ref, f32[8,1536]{1,0:T(8,128)S(1)} %collective-permute-done.1.bias_far_ref), custom_call_target="tpu_custom_call" | custom-call | flops 99999997952 | tf_op jit(solution)/shard_map/add_parts/pallas_call | solution.py:22
  60.9 4.0 %all-to-all-start.2 = ((f32[8,16,1536]{2,1,0:T(8,128)}), f32[8,16,1536]{2,1,0:T(8,128)S(1)}, u32[]{:S(2)}, u32[]{:S(2)}) async-start(f32[8,16,1536]{2,1,0:T(8,128)} %add_parts.1), calls=%async_computation.2 | async-start | bytes 1572864 | tf_op jit(solution)/shard_map/all_to_all | solution.py:191
  65.0 1.8 %collective-permute-done.3.value_ref = bf16[1,128,1536]{2,1,0:T(8,128)(2,1)S(1)} collective-permute-done((bf16[1,128,1536]{2,1,0:T(8,128)(2,1)S(1)}, bf16[1,128,1536]{2,1,0:T(8,128)(2,1)S(1)}, u32[]{:S(2)}, u32[]{:S(2)}) %collective-permute-start.3) | collective-permute-done | bytes 393248 | tf_op jit(solution)/shard_map/ppermute | solution.py:257
  66.8 0.8 settle.1
  67.6 6.9 %all-to-all-done.2.parts_ref = f32[8,16,1536]{2,1,0:T(8,128)S(1)} async-done(((f32[8,16,1536]{2,1,0:T(8,128)}), f32[8,16,1536]{2,1,0:T(8,128)S(1)}, u32[]{:S(2)}, u32[]{:S(2)}) %all-to-all-start.2) | async-done | bytes 786464 | tf_op jit(solution)/shard_map/all_to_all | solution.py:191
  74.4 0.9 %whole_grads.1 = (f32[8,8,1536]{2,1,0:T(8,128)}, f32[8,8,1536]{2,1,0:T(8,128)}) custom-call(f32[8,16,1536]{2,1,0:T(8,128)S(1)} %all-to-all-done.2.parts_ref), custom_call_target="tpu_custom_call" | custom-call | tf_op jit(solution)/shard_map/whole_grads/pallas_call | solution.py:22
  (2 shorter events, 0.0 us)
Async XLA Ops:
  0.6 1.5 %copy-start.5 = (s32[1,4]{1,0:T(1,128)S(1)}, s32[1,4]{1,0:T(1,128)}, u32[]{:S(2)}) copy-start(s32[1,4]{1,0:T(1,128)} %order_ref.3) | copy-start | bytes 52
  0.6 1.5 %copy-start.4 = (s32[128]{0:T(128)S(1)}, s32[128]{0:T(128)}, u32[]{:S(2)}) copy-start(s32[128]{0:T(128)} %param.14) | copy-start | bytes 1540
  0.7 13.1 %collective-permute-start = (bf16[1,128,1536]{2,1,0:T(8,128)(2,1)}, bf16[1,128,1536]{2,1,0:T(8,128)(2,1)S(1)}, u32[]{:S(2)}, u32[]{:S(2)}) collective-permute-start(bf16[1,128,1536]{2,1,0:T(8,128)(2,1)} %param.8), channel_id=1, source_target_pairs={{0,8},{8,16},{16,24},{1,9},{9,17},{17,25},{2,10},{10,18},{18,26},{... | collective-permute-start | bytes 1179656 | tf_op jit(solution)/shard_map/ppermute | solution.py:206
  2.1 1.0 %copy-start = (bf16[1,128,1536]{2,1,0:T(8,128)(2,1)S(1)}, bf16[1,128,1536]{2,1,0:T(8,128)(2,1)}, u32[]{:S(2)}) copy-start(bf16[1,128,1536]{2,1,0:T(8,128)(2,1)} %cot_ref.1) | copy-start | bytes 1179652
  4.6 9.1 %copy-start.2 = (bf16[1,64,1536]{2,1,0:T(8,128)(2,1)S(1)}, bf16[1,64,1536]{2,1,0:T(8,128)(2,1)}, u32[]{:S(2)}) copy-start(bf16[1,64,1536]{2,1,0:T(8,128)(2,1)} %gain_ref.3) | copy-start | bytes 589828
  4.6 9.1 %copy-start.6 = (bf16[128,1536]{1,0:T(8,128)(2,1)S(1)}, bf16[128,1536]{1,0:T(8,128)(2,1)}, u32[]{:S(2)}) copy-start(bf16[128,1536]{1,0:T(8,128)(2,1)} %emb_ref.1) | copy-start | bytes 1179652
  4.6 33.5 %all-to-all-start = ((f32[8,8,1536]{2,1,0:T(8,128)}), f32[8,8,1536]{2,1,0:T(8,128)S(1)}, u32[]{:S(2)}, u32[]{:S(2)}) async-start(f32[8,8,1536]{2,1,0:T(8,128)} %get-tuple-element.22), calls=%async_computation | async-start | bytes 786432 | tf_op jit(solution)/shard_map/all_to_all | solution.py:191
  13.7 34.1 %copy-start.3 = (bf16[1,64,1536]{2,1,0:T(8,128)(2,1)S(1)}, bf16[1,64,1536]{2,1,0:T(8,128)(2,1)}, u32[]{:S(2)}) copy-start(bf16[1,64,1536]{2,1,0:T(8,128)(2,1)} %bias_ref.1) | copy-start | bytes 589828
  39.4 13.1 %all-to-all-start.1 = ((f32[8,8,1536]{2,1,0:T(8,128)}), f32[8,8,1536]{2,1,0:T(8,128)S(1)}, u32[]{:S(2)}, u32[]{:S(2)}) async-start(f32[8,8,1536]{2,1,0:T(8,128)} %gain_part.1), calls=%async_computation.1 | async-start | bytes 786432 | tf_op jit(solution)/shard_map/all_to_all | solution.py:191
  44.3 3.6 %copy-start.1 = (bf16[1,128,1536]{2,1,0:T(8,128)(2,1)S(1)}, bf16[1,128,1536]{2,1,0:T(8,128)(2,1)}, u32[]{:S(2)}) copy-start(bf16[1,128,1536]{2,1,0:T(8,128)(2,1)} %res_ref.1) | copy-start | bytes 1179652
  44.3 7.0 %collective-permute-start.1 = (f32[8,1536]{1,0:T(8,128)S(1)}, f32[8,1536]{1,0:T(8,128)S(1)}, u32[]{:S(2)}, u32[]{:S(2)}) collective-permute-start(f32[8,1536]{1,0:T(8,128)S(1)} %bias_near.1.bias_ref), channel_id=1, source_target_pairs={{0,256},{256,0},{1,257},{257,1},{2,258},{258,2},{3,259},{259,3},{4... | collective-permute-start | bytes 147464 | tf_op jit(solution)/shard_map/ppermute | solution.py:195
  52.5 7.4 %collective-permute-start.2 = (f32[8,1536]{1,0:T(8,128)S(1)}, f32[8,1536]{1,0:T(8,128)S(1)}, u32[]{:S(2)}, u32[]{:S(2)}) collective-permute-start(f32[8,1536]{1,0:T(8,128)S(1)} %gain_near.1.gain_ref), channel_id=1, source_target_pairs={{0,256},{256,0},{1,257},{257,1},{2,258},{258,2},{3,259},{259,3},{4... | collective-permute-start | bytes 147464 | tf_op jit(solution)/shard_map/ppermute | solution.py:195
  55.9 10.9 %collective-permute-start.3 = (bf16[1,128,1536]{2,1,0:T(8,128)(2,1)S(1)}, bf16[1,128,1536]{2,1,0:T(8,128)(2,1)S(1)}, u32[]{:S(2)}, u32[]{:S(2)}) collective-permute-start(bf16[1,128,1536]{2,1,0:T(8,128)(2,1)S(1)} %get-tuple-element.35), channel_id=1, source_target_pairs={{0,24},{8,0},{16,8},{24,16},{1,25},{9,1},{17,9},{25,17},{2,26},{10... | collective-permute-start | bytes 1179656 | tf_op jit(solution)/shard_map/ppermute | solution.py:257
  60.9 13.5 %all-to-all-start.2 = ((f32[8,16,1536]{2,1,0:T(8,128)}), f32[8,16,1536]{2,1,0:T(8,128)S(1)}, u32[]{:S(2)}, u32[]{:S(2)}) async-start(f32[8,16,1536]{2,1,0:T(8,128)} %add_parts.1), calls=%async_computation.2 | async-start | bytes 1572864 | tf_op jit(solution)/shard_map/all_to_all | solution.py:191

commit v8 on v6

--- a/solution.py
+++ b/solution.py
@@ -64,9 +64,13 @@
     out_ref[...] = sums.reshape(out_ref.shape)
 
 
-def sums_kernel(first_ref, lang_ref, recv_ref, emb_ref, cot_ref, gain_ref, out_ref, x_ref, gain_scr, wide_scr):
+def rows_kernel(lang_ref, table_ref, out_ref):
+    pick = selector(lang_ref, table_ref.shape[1])
+    out_ref[...] = jnp.dot(pick, table_ref[0], preferred_element_type=f32).astype(bf16)
+
+
+def sums_kernel(first_ref, recv_ref, emb_ref, cot_ref, gain_ref, out_ref, x_ref, wide_scr):
     tokens = cot_ref.shape[0]
-    gain_scr[...] = jnp.dot(selector(lang_ref, gain_ref.shape[1]), gain_ref[0], preferred_element_type=f32).astype(bf16)
 
     @pl.when(first_ref[0] == 1)
     def _():
@@ -80,7 +84,7 @@
     for top in range(0, tokens, step):
         rows = slice(top, top + step)
         x = x_ref[rows, :].astype(f32)
-        scaled = cot_ref[rows, :].astype(f32) * gain_scr[rows, :].astype(f32)
+        scaled = cot_ref[rows, :].astype(f32) * gain_ref[rows, :].astype(f32)
         lane = lax.broadcasted_iota(jnp.int32, (step, tokens), 1)
         tile = jnp.zeros((step, tokens), f32)
         for i, term in enumerate((x, x * x, scaled, scaled * x)):
@@ -127,15 +131,9 @@
         copy.wait()
 
 
-def outs_kernel(
-    order_ref, lang_ref, sums_ref, x_ref, cot_ref, res_ref, gain_ref, bias_ref, normed_ref, back_ref, fig_scr, gain_scr, bias_scr
-):
-    pick = selector(lang_ref, gain_ref.shape[1])
-    gain_scr[...] = jnp.dot(pick, gain_ref[0], preferred_element_type=f32).astype(bf16)
-    bias_scr[...] = jnp.dot(pick, bias_ref[0], preferred_element_type=f32).astype(bf16)
+def grad_kernel(order_ref, sums_ref, x_ref, cot_ref, res_ref, gain_ref, back_ref, fig_scr):
     fig_scr[...] = columns(sums_ref)
-    tokens = x_ref.shape[0]
-    rows, step = tokens // MB, 16
+    rows, step = x_ref.shape[0] // MB, 16
     for j in range(MB):
         for part in range(0, rows, step):
             here = pl.ds(pl.multiple_of(order_ref[0, j] * rows + part, step), step)
@@ -143,12 +141,23 @@
             fig = fig_scr[here, :]
             center, inv, mean_cot, mean_cross = (fig[:, i : i + 1] for i in range(4))
             normalized = (x_ref[here, :].astype(f32) - center) * inv
-            gains = gain_scr[here, :].astype(f32)
-            scaled = cot_ref[here, :].astype(f32) * gains
+            scaled = cot_ref[here, :].astype(f32) * gain_ref[here, :].astype(f32)
             back_ref[0, slot, :] = (
                 res_ref[0, slot, :].astype(f32) + inv * (scaled - mean_cot - normalized * mean_cross)
             ).astype(bf16)
-            normed_ref[0, here, :] = (normalized * gains + bias_scr[here, :].astype(f32)).astype(bf16)
+
+
+def norm_kernel(lang_ref, sums_ref, x_ref, gain_ref, bias_ref, normed_ref, bias_scr):
+    pick = selector(lang_ref, bias_ref.shape[1])
+    bias_scr[...] = jnp.dot(pick, bias_ref[0], preferred_element_type=f32).astype(bf16)
+    figures = columns(sums_ref)
+    step = 16
+    for top in range(0, x_ref.shape[0], step):
+        rows = slice(top, top + step)
+        normalized = (x_ref[rows, :].astype(f32) - figures[rows, 0:1]) * figures[rows, 1:2]
+        normed_ref[0, rows, :] = (
+            normalized * gain_ref[rows, :].astype(f32) + bias_scr[rows, :].astype(f32)
+        ).astype(bf16)
 
 
 def added(parts_ref):
@@ -216,15 +225,16 @@
         mb_order, lang, cot_norm,
     )
     bias_mine = exchanged(bias_part)
-    received, bias_part = lax.optimization_barrier((received, bias_part))
+    gain_rows = call(rows_kernel, "gain_rows", forward, [], [VMEM, VMEM], lang, gain)
+    received, bias_part, gain_rows = lax.optimization_barrier((received, bias_part, gain_rows))
 
     sums, x = call(
         sums_kernel,
         "token_sums",
         (shape((8, tokens), f32), forward),
-        [pltpu.VMEM((tokens, width), bf16), pltpu.VMEM((tokens, tokens), f32)],
-        [SMEM, VMEM, VMEM, VMEM, VMEM, VMEM],
-        first, lang, received, embedded, cot, gain,
+        [pltpu.VMEM((tokens, tokens), f32)],
+        [SMEM, VMEM, VMEM, VMEM, VMEM],
+        first, received, embedded, cot, gain_rows,
         cover=10**11,
     )
     sums = lax.psum(lax.psum(sums, "core"), "far")
@@ -234,39 +244,47 @@
         gain_kernel,
         "gain_part",
         shape(pieces, f32),
-        [pltpu.VMEM((tokens, width), bf16), pltpu.VMEM((tokens, width), bf16), pltpu.VMEM(pieces, f32), sems((2,))],
+        [pltpu.VMEM((tokens, width), bf16), pltpu.VMEM((tokens, width), bf16), pltpu.VMEM(pieces, f32), sems((3,))],
         [VMEM, VMEM, VMEM, VMEM],
         lang, sums, x, cot,
         out_specs=HBM,
     )
     gain_mine = exchanged(gain_part)
     bias_total = call(total_kernel, "bias_total", shape(pieces[1:], f32), [], [VMEM], bias_mine)
-    normed, back = call(
-        outs_kernel,
-        "norm_and_grad",
-        (shape((1, tokens, width), bf16), shape((1, tokens, width), bf16)),
-        [pltpu.VMEM((tokens, tokens), f32), pltpu.VMEM((tokens, width), bf16), pltpu.VMEM((tokens, width), bf16)],
-        [SMEM, VMEM, VMEM, VMEM, VMEM, VMEM, VMEM, VMEM],
-        mb_order, lang, sums, x, cot, cot_res, gain, bias,
+    back = call(
+        grad_kernel,
+        "input_grad",
+        shape((1, tokens, width), bf16),
+        [pltpu.VMEM((tokens, tokens), f32)],
+        [SMEM, VMEM, VMEM, VMEM, VMEM, VMEM],
+        mb_order, sums, x, cot, cot_res, gain_rows,
     )
     returned = lax.ppermute(back, "pipe", [(i, (i - 1) % stages) for i in range(stages)])
     gain_mine, back, bias_total = lax.optimization_barrier((gain_mine, back, bias_total))
     both = (2 * pieces[1], width)
     near_total = call(near_kernel, "near_parts", shape(both, f32), [], [VMEM, VMEM], gain_mine, bias_total)
     far_total = lax.ppermute(near_total, "far_dp", [(0, 1), (1, 0)])
-    totals = exchanged(
-        call(
-            add_kernel,
-            "add_parts",
-            shape((near, *both), f32),
-            [pltpu.VMEM(both, f32), sems((near,))],
-            [VMEM, VMEM],
-            near_total, far_total,
-            out_specs=HBM,
-        )
+    total = call(
+        add_kernel,
+        "add_parts",
+        shape((near, *both), f32),
+        [pltpu.VMEM(both, f32), sems((near,))],
+        [VMEM, VMEM],
+        near_total, far_total,
+        out_specs=HBM,
+    )
+    totals = exchanged(total)
+    sums, total = lax.optimization_barrier((sums, total))
+    normed = call(
+        norm_kernel,
+        "normed",
+        shape((1, tokens, width), bf16),
+        [pltpu.VMEM((tokens, width), bf16)],
+        [VMEM, VMEM, VMEM, VMEM, VMEM],
+        lang, sums, x, gain_rows, bias,
     )
     returned = call(settle_kernel, "settle", shape(back.shape, bf16), [sems(())], [VMEM], returned, out_specs=HBM, cover=10**11)
-    totals, returned = lax.optimization_barrier((totals, returned))
+    totals, returned, normed = lax.optimization_barrier((totals, returned, normed))
     grads = shape(pieces, f32)
     gain_grad, bias_grad = call(
         whole_kernel, "whole_grads", (grads, grads), [sems((2,))], [VMEM], totals, out_specs=(HBM, HBM)

time: 76.1 us -> 75.8 us (level)
    pallas_call x9 -> x11, Pallas kernels: 8.38 us -> 8.24 us  [call(): pl.pallas_call(kernel, name=name, out_shape=outs, in_specs=in_specs, out_...]
where the time goes in v8:
time: 75.8 us; the launch traced here: 75.2 us
  blocking collectives  23.7 us (31%)
  starting transfers between devices  22.1 us (29%)
  waiting for transfers between devices  19.1 us (25%)
  Pallas kernels  8.24 us (11%)
  local copies, waits for them, and re-layouts  1.3 us (2%)
  between operations  0.81 us (1%)
    psum x2, blocking collectives, local(): sums = lax.psum(lax.psum(sums, 'core'), 'far')  23.7 us
    all_to_all x3, starting transfers between devices, exchanged(): return lax.all_to_all(pieces, NEAR, 0, 0)  14.6 us
    all_to_all x3, waiting for transfers between devices, exchanged(): return lax.all_to_all(pieces, NEAR, 0, 0)  11.2 us
    pallas_call x11, Pallas kernels, call(): pl.pallas_call(kernel, name=name, out_shape=outs, in_specs=in_specs, out_...  8.24 us
    ppermute x1, waiting for transfers between devices, local(): far_total = lax.ppermute(near_total, 'far_dp', [(0, 1), (1, 0)])  5.07 us
    ppermute x1, starting transfers between devices, local(): far_total = lax.ppermute(near_total, 'far_dp', [(0, 1), (1, 0)])  3.38 us
    ppermute x1, waiting for transfers between devices, local(): lax.ppermute(section_out, 'pipe', [(i, i + 1) for i in range(stages - 1)])  2.84 us
    ppermute x1, starting transfers between devices, local(): lax.ppermute(back, 'pipe', [(i, (i - 1) % stages) for i in range(stages)])  2.74 us
  transfers between devices with their start and end apart: 6, of which 4 were waited for; matrix products, arithmetic and copies ran while one was open for 0% of the time, Pallas kernels for 8%

profile of v8, /device:TPU:6, one launch (start us, length us, event | category | flops | bytes accessed | tf_op | source)
XLA Modules:
  0.0 75.2 jit_solution(12114692992030446056)
XLA Ops:
  0.6 0.0 copy-start.5
  0.6 0.0 copy-start.4
  0.7 1.4 %collective-permute-start = (bf16[1,128,1536]{2,1,0:T(8,128)(2,1)}, bf16[1,128,1536]{2,1,0:T(8,128)(2,1)S(1)}, u32[]{:S(2)}, u32[]{:S(2)}) collective-permute-start(bf16[1,128,1536]{2,1,0:T(8,128)(2,1)} %param.8), channel_id=1, source_target_pairs={{0,8},{8,16},{16,24},{1,9},{9,17},{17,25},{2,10},{10,18},{18,26},{... | collective-permute-start | bytes 1179656 | tf_op jit(solution)/shard_map/ppermute | solution.py:215
  2.1 0.0 copy-done.5
  2.1 0.0 copy-done.4
  2.1 0.0 copy-start
  2.1 1.0 %copy-done = bf16[1,128,1536]{2,1,0:T(8,128)(2,1)S(1)} copy-done((bf16[1,128,1536]{2,1,0:T(8,128)(2,1)S(1)}, bf16[1,128,1536]{2,1,0:T(8,128)(2,1)}, u32[]{:S(2)}) %copy-start) | copy-done | bytes 393240
  3.1 1.5 %bias_part.1 = (f32[8,8,1536]{2,1,0:T(8,128)}, bf16[128,1536]{1,0:T(8,128)(2,1)S(1)}) custom-call(s32[1,4]{1,0:T(1,128)S(1)} %copy-done.5, s32[1,128]{1,0:T(1,128)S(1)} %bitcast.4, bf16[1,128,1536]{2,1,0:T(8,128)(2,1)S(1)} %copy-done), custom_call_target="tpu_custom_call" | custom-call | tf_op jit(solution)/shard_map/bias_part/pallas_call | solution.py:22
  4.6 0.0 copy-start.3
  4.6 6.0 %all-to-all-start = ((f32[8,8,1536]{2,1,0:T(8,128)}), f32[8,8,1536]{2,1,0:T(8,128)S(1)}, u32[]{:S(2)}, u32[]{:S(2)}) async-start(f32[8,8,1536]{2,1,0:T(8,128)} %get-tuple-element.20), calls=%async_computation | async-start | bytes 786432 | tf_op jit(solution)/shard_map/all_to_all | solution.py:204
  10.6 0.0 copy-start.6
  10.6 0.0 copy-done.3
  10.6 0.3 gain_rows.1.gain_ref
  10.9 2.8 %collective-permute-done.recv_ref = bf16[1,128,1536]{2,1,0:T(8,128)(2,1)S(1)} collective-permute-done((bf16[1,128,1536]{2,1,0:T(8,128)(2,1)}, bf16[1,128,1536]{2,1,0:T(8,128)(2,1)S(1)}, u32[]{:S(2)}, u32[]{:S(2)}) %collective-permute-start) | collective-permute-done | bytes 393248 | tf_op jit(solution)/shard_map/ppermute | solution.py:215
  13.7 0.0 copy-done.6
  13.7 0.4 token_sums.1
  14.1 2.5 %psum.14 = f32[8,128]{1,0:T(8,128)S(1)} all-reduce(f32[8,128]{1,0:T(8,128)S(1)} %get-tuple-element.24), channel_id=1, replica_groups=mesh['far_dp'=2,'next'=2,'row'=4,'pipe'=4,'far'=4,'core'=2] {'core'}, use_global_device_ids=true, to_apply=%region_0.0 | all-reduce | flops 1024 | bytes 8192 | tf_op jit(solution)/shard_map/psum | solution.py:240
  16.6 21.3 %psum.15.sums_ref = f32[8,128]{1,0:T(8,128)S(1)} all-reduce(f32[8,128]{1,0:T(8,128)S(1)} %psum.14), channel_id=1, replica_groups=mesh['far_dp'=2,'next'=2,'row'=4,'pipe'=4,'far'=4,'core'=2] {'far'}, use_global_device_ids=true, to_apply=%region_1.0 | all-reduce | flops 1024 | bytes 8192 | tf_op jit(solution)/shard_map/psum | solution.py:240
  37.8 0.0 all-to-all-done.parts_ref
  37.8 1.2 %gain_part.1 = f32[8,8,1536]{2,1,0:T(8,128)} custom-call(s32[1,128]{1,0:T(1,128)S(1)} %bitcast.6, f32[8,128]{1,0:T(8,128)S(1)} %psum.15.sums_ref, bf16[128,1536]{1,0:T(8,128)(2,1)S(1)} %get-tuple-element.26.x_ref, bf16[128,1536]{1,0:T(8,128)(2,1)S(1)} %get-tuple-element.22.cot_ref), custom_call_target="tpu_custom_call" | custom-call | tf_op jit(solution)/shard_map/gain_part/pallas_call | solution.py:22
  39.1 0.0 copy-start.1
  39.1 5.0 %all-to-all-start.1 = ((f32[8,8,1536]{2,1,0:T(8,128)}), f32[8,8,1536]{2,1,0:T(8,128)S(1)}, u32[]{:S(2)}, u32[]{:S(2)}) async-start(f32[8,8,1536]{2,1,0:T(8,128)} %gain_part.1), calls=%async_computation.1 | async-start | bytes 786432 | tf_op jit(solution)/shard_map/all_to_all | solution.py:204
  44.1 0.0 copy-done.1
  44.1 1.0 %input_grad.1 = bf16[1,128,1536]{2,1,0:T(8,128)(2,1)S(1)} custom-call(s32[1,4]{1,0:T(1,128)S(1)} %copy-done.5, f32[8,128]{1,0:T(8,128)S(1)} %psum.15.sums_ref, bf16[128,1536]{1,0:T(8,128)(2,1)S(1)} %get-tuple-element.26.x_ref, bf16[128,1536]{1,0:T(8,128)(2,1)S(1)} %get-tuple-element.22.cot_ref, bf16[1,128,1536]{2,1,0:T(8,128)(2,1)S(1)} %copy-done.1, ...), custom_call_target="tpu_custom_call" | custom-call | tf_op jit(solution)/shard_map/input_grad/pallas_call | solution.py:22
  45.1 2.7 %collective-permute-start.2 = (bf16[1,128,1536]{2,1,0:T(8,128)(2,1)S(1)}, bf16[1,128,1536]{2,1,0:T(8,128)(2,1)S(1)}, u32[]{:S(2)}, u32[]{:S(2)}) collective-permute-start(bf16[1,128,1536]{2,1,0:T(8,128)(2,1)S(1)} %input_grad.1), channel_id=1, source_target_pairs={{0,24},{8,0},{16,8},{24,16},{1,25},{9,1},{17,9},{25,17},{2,26},{10... | collective-permute-start | bytes 1179656 | tf_op jit(solution)/shard_map/ppermute | solution.py:262
  47.9 4.0 %all-to-all-done.1.gain_ref = f32[8,8,1536]{2,1,0:T(8,128)S(1)} async-done(((f32[8,8,1536]{2,1,0:T(8,128)}), f32[8,8,1536]{2,1,0:T(8,128)S(1)}, u32[]{:S(2)}, u32[]{:S(2)}) %all-to-all-start.1) | async-done | bytes 393248 | tf_op jit(solution)/shard_map/all_to_all | solution.py:204
  51.9 3.4 %collective-permute-start.1 = (f32[16,1536]{1,0:T(8,128)S(1)}, f32[16,1536]{1,0:T(8,128)S(1)}, u32[]{:S(2)}, u32[]{:S(2)}) collective-permute-start(f32[16,1536]{1,0:T(8,128)S(1)} %near_parts.1.near_ref), channel_id=1, source_target_pairs={{0,256},{256,0},{1,257},{257,1},{2,258},{258,2},{3,259},{259,3},{4... | collective-permute-start | bytes 294920 | tf_op jit(solution)/shard_map/ppermute | solution.py:266
  55.3 5.1 %collective-permute-done.1.far_ref = f32[16,1536]{1,0:T(8,128)S(1)} collective-permute-done((f32[16,1536]{1,0:T(8,128)S(1)}, f32[16,1536]{1,0:T(8,128)S(1)}, u32[]{:S(2)}, u32[]{:S(2)}) %collective-permute-start.1) | collective-permute-done | bytes 98336 | tf_op jit(solution)/shard_map/ppermute | solution.py:266
  60.4 1.0 %add_parts.1 = f32[8,16,1536]{2,1,0:T(8,128)} custom-call(f32[16,1536]{1,0:T(8,128)S(1)} %near_parts.1.near_ref, f32[16,1536]{1,0:T(8,128)S(1)} %collective-permute-done.1.far_ref), custom_call_target="tpu_custom_call" | custom-call | tf_op jit(solution)/shard_map/add_parts/pallas_call | solution.py:22
  61.4 3.6 %all-to-all-start.2 = ((f32[8,16,1536]{2,1,0:T(8,128)}), f32[8,16,1536]{2,1,0:T(8,128)S(1)}, u32[]{:S(2)}, u32[]{:S(2)}) async-start(f32[8,16,1536]{2,1,0:T(8,128)} %add_parts.1), calls=%async_computation.2 | async-start | bytes 1572864 | tf_op jit(solution)/shard_map/all_to_all | solution.py:204
  64.9 0.0 copy-start.2
  64.9 0.0 collective-permute-done.2.value_ref
  65.0 0.8 %settle.1 = bf16[1,128,1536]{2,1,0:T(8,128)(2,1)} custom-call(bf16[1,128,1536]{2,1,0:T(8,128)(2,1)S(1)} %collective-permute-done.2.value_ref), custom_call_target="tpu_custom_call" | custom-call | flops 99999997952 | tf_op jit(solution)/shard_map/settle/pallas_call | solution.py:22
  65.7 0.3 copy-done.2
  66.0 1.1 %normed.1 = bf16[1,128,1536]{2,1,0:T(8,128)(2,1)} custom-call(s32[1,128]{1,0:T(1,128)S(1)} %bitcast.7, f32[8,128]{1,0:T(8,128)S(1)} %psum.15.sums_ref, bf16[128,1536]{1,0:T(8,128)(2,1)S(1)} %get-tuple-element.26.x_ref, bf16[128,1536]{1,0:T(8,128)(2,1)S(1)} %gain_rows.1.gain_ref, bf16[1,64,1536]{2,1,0:T(8,128)(2,1)S(1)} %copy-done.2), custom_call_target="tpu_custom_call" | custom-call | tf_op jit(solution)/shard_map/normed/pallas_call | solution.py:22
  67.1 7.2 %all-to-all-done.2.parts_ref = f32[8,16,1536]{2,1,0:T(8,128)S(1)} async-done(((f32[8,16,1536]{2,1,0:T(8,128)}), f32[8,16,1536]{2,1,0:T(8,128)S(1)}, u32[]{:S(2)}, u32[]{:S(2)}) %all-to-all-start.2) | async-done | bytes 786464 | tf_op jit(solution)/shard_map/all_to_all | solution.py:204
  74.3 0.9 %whole_grads.1 = (f32[8,8,1536]{2,1,0:T(8,128)}, f32[8,8,1536]{2,1,0:T(8,128)}) custom-call(f32[8,16,1536]{2,1,0:T(8,128)S(1)} %all-to-all-done.2.parts_ref), custom_call_target="tpu_custom_call" | custom-call | tf_op jit(solution)/shard_map/whole_grads/pallas_call | solution.py:22
  (2 shorter events, 0.0 us)
Async XLA Ops:
  0.6 1.5 %copy-start.5 = (s32[1,4]{1,0:T(1,128)S(1)}, s32[1,4]{1,0:T(1,128)}, u32[]{:S(2)}) copy-start(s32[1,4]{1,0:T(1,128)} %order_ref.3) | copy-start | bytes 52
  0.6 1.5 %copy-start.4 = (s32[128]{0:T(128)S(1)}, s32[128]{0:T(128)}, u32[]{:S(2)}) copy-start(s32[128]{0:T(128)} %param.14) | copy-start | bytes 1540
  0.7 13.1 %collective-permute-start = (bf16[1,128,1536]{2,1,0:T(8,128)(2,1)}, bf16[1,128,1536]{2,1,0:T(8,128)(2,1)S(1)}, u32[]{:S(2)}, u32[]{:S(2)}) collective-permute-start(bf16[1,128,1536]{2,1,0:T(8,128)(2,1)} %param.8), channel_id=1, source_target_pairs={{0,8},{8,16},{16,24},{1,9},{9,17},{17,25},{2,10},{10,18},{18,26},{... | collective-permute-start | bytes 1179656 | tf_op jit(solution)/shard_map/ppermute | solution.py:215
  2.1 1.0 %copy-start = (bf16[1,128,1536]{2,1,0:T(8,128)(2,1)S(1)}, bf16[1,128,1536]{2,1,0:T(8,128)(2,1)}, u32[]{:S(2)}) copy-start(bf16[1,128,1536]{2,1,0:T(8,128)(2,1)} %cot_ref.1) | copy-start | bytes 1179652
  4.6 6.0 %copy-start.3 = (bf16[1,64,1536]{2,1,0:T(8,128)(2,1)S(1)}, bf16[1,64,1536]{2,1,0:T(8,128)(2,1)}, u32[]{:S(2)}) copy-start(bf16[1,64,1536]{2,1,0:T(8,128)(2,1)} %table_ref.1) | copy-start | bytes 589828
  4.6 33.2 %all-to-all-start = ((f32[8,8,1536]{2,1,0:T(8,128)}), f32[8,8,1536]{2,1,0:T(8,128)S(1)}, u32[]{:S(2)}, u32[]{:S(2)}) async-start(f32[8,8,1536]{2,1,0:T(8,128)} %get-tuple-element.20), calls=%async_computation | async-start | bytes 786432 | tf_op jit(solution)/shard_map/all_to_all | solution.py:204
  10.6 3.2 %copy-start.6 = (bf16[128,1536]{1,0:T(8,128)(2,1)S(1)}, bf16[128,1536]{1,0:T(8,128)(2,1)}, u32[]{:S(2)}) copy-start(bf16[128,1536]{1,0:T(8,128)(2,1)} %emb_ref.1) | copy-start | bytes 1179652
  39.1 5.1 %copy-start.1 = (bf16[1,128,1536]{2,1,0:T(8,128)(2,1)S(1)}, bf16[1,128,1536]{2,1,0:T(8,128)(2,1)}, u32[]{:S(2)}) copy-start(bf16[1,128,1536]{2,1,0:T(8,128)(2,1)} %res_ref.1) | copy-start | bytes 1179652
  39.1 12.8 %all-to-all-start.1 = ((f32[8,8,1536]{2,1,0:T(8,128)}), f32[8,8,1536]{2,1,0:T(8,128)S(1)}, u32[]{:S(2)}, u32[]{:S(2)}) async-start(f32[8,8,1536]{2,1,0:T(8,128)} %gain_part.1), calls=%async_computation.1 | async-start | bytes 786432 | tf_op jit(solution)/shard_map/all_to_all | solution.py:204
  45.1 19.8 %collective-permute-start.2 = (bf16[1,128,1536]{2,1,0:T(8,128)(2,1)S(1)}, bf16[1,128,1536]{2,1,0:T(8,128)(2,1)S(1)}, u32[]{:S(2)}, u32[]{:S(2)}) collective-permute-start(bf16[1,128,1536]{2,1,0:T(8,128)(2,1)S(1)} %input_grad.1), channel_id=1, source_target_pairs={{0,24},{8,0},{16,8},{24,16},{1,25},{9,1},{17,9},{25,17},{2,26},{10... | collective-permute-start | bytes 1179656 | tf_op jit(solution)/shard_map/ppermute | solution.py:262
  51.9 8.5 %collective-permute-start.1 = (f32[16,1536]{1,0:T(8,128)S(1)}, f32[16,1536]{1,0:T(8,128)S(1)}, u32[]{:S(2)}, u32[]{:S(2)}) collective-permute-start(f32[16,1536]{1,0:T(8,128)S(1)} %near_parts.1.near_ref), channel_id=1, source_target_pairs={{0,256},{256,0},{1,257},{257,1},{2,258},{258,2},{3,259},{259,3},{4... | collective-permute-start | bytes 294920 | tf_op jit(solution)/shard_map/ppermute | solution.py:266
  61.4 13.0 %all-to-all-start.2 = ((f32[8,16,1536]{2,1,0:T(8,128)}), f32[8,16,1536]{2,1,0:T(8,128)S(1)}, u32[]{:S(2)}, u32[]{:S(2)}) async-start(f32[8,16,1536]{2,1,0:T(8,128)} %add_parts.1), calls=%async_computation.2 | async-start | bytes 1572864 | tf_op jit(solution)/shard_map/all_to_all | solution.py:204
  64.9 1.1 %copy-start.2 = (bf16[1,64,1536]{2,1,0:T(8,128)(2,1)S(1)}, bf16[1,64,1536]{2,1,0:T(8,128)(2,1)}, u32[]{:S(2)}) copy-start(bf16[1,64,1536]{2,1,0:T(8,128)(2,1)} %bias_ref.1) | copy-start | bytes 589828

commit v9 on v8

--- a/solution.py
+++ b/solution.py
@@ -64,7 +64,7 @@
     out_ref[...] = sums.reshape(out_ref.shape)
 
 
-def rows_kernel(lang_ref, table_ref, out_ref):
+def rows_kernel(lang_ref, table_ref, ahead_ref, out_ref):
     pick = selector(lang_ref, table_ref.shape[1])
     out_ref[...] = jnp.dot(pick, table_ref[0], preferred_element_type=f32).astype(bf16)
 
@@ -104,11 +104,12 @@
     return jnp.transpose(tile)
 
 
-def gain_kernel(lang_ref, sums_ref, x_ref, cot_ref, out_ref, high_scr, low_scr, out_scr, sems):
+def gain_kernel(lang_ref, sums_ref, x_ref, cot_ref, out_ref, parts_scr, out_scr, sems):
     pieces, height, width = out_ref.shape
     tokens, step = cot_ref.shape[0], 16
     figures = columns(sums_ref)
     who = members(lang_ref, pieces * height)
+    who = jnp.concatenate([who, who], axis=1)
     copies = []
     chunk = width // sems.shape[0]
     for i, left in enumerate(range(0, width, chunk)):
@@ -118,11 +119,9 @@
             center, inv = figures[rows, 0:1], figures[rows, 1:2]
             product = cot_ref[rows, wide].astype(f32) * ((x_ref[rows, wide].astype(f32) - center) * inv)
             high = product.astype(bf16)
-            high_scr[rows, wide] = high
-            low_scr[rows, wide] = (product - high.astype(f32)).astype(bf16)
-        sums = jnp.dot(who, high_scr[:, wide], preferred_element_type=f32) + jnp.dot(
-            who, low_scr[:, wide], preferred_element_type=f32
-        )
+            parts_scr[rows, wide] = high
+            parts_scr[tokens + top : tokens + top + step, wide] = (product - high.astype(f32)).astype(bf16)
+        sums = jnp.dot(who, parts_scr[:, wide], preferred_element_type=f32)
         out_scr[:, :, wide] = sums.reshape(pieces, height, chunk)
         here = pl.ds(left, chunk)
         copies.append(pltpu.make_async_copy(out_scr.at[:, :, here], out_ref.at[:, :, here], sems.at[i]))
@@ -171,14 +170,10 @@
     out_ref[...] = added(parts_ref)
 
 
-def near_kernel(gain_ref, bias_ref, out_ref):
-    height = bias_ref.shape[0]
-    out_ref[:height, :] = added(gain_ref)
-    out_ref[height:, :] = bias_ref[...]
-
-
-def add_kernel(near_ref, far_ref, out_ref, total_scr, sems):
-    total_scr[...] = near_ref[...] + far_ref[...]
+def add_kernel(gain_ref, gain_far_ref, bias_ref, bias_far_ref, out_ref, total_scr, sems):
+    height = gain_ref.shape[0]
+    total_scr[:height, :] = gain_ref[...] + gain_far_ref[...]
+    total_scr[height:, :] = bias_ref[...] + bias_far_ref[...]
     run_copies([pltpu.make_async_copy(total_scr, out_ref.at[k], sems.at[k]) for k in range(out_ref.shape[0])])
 
 
@@ -202,6 +197,10 @@
 
 def exchanged(pieces):
     return lax.all_to_all(pieces, NEAR, 0, 0)
+
+
+def from_far(total):
+    return lax.ppermute(total, "far_dp", [(0, 1), (1, 0)])
 
 
 def local(section_out, embedded, cot_norm, cot_res, gain, bias, lang_ids, mb_order):
@@ -225,7 +224,7 @@
         mb_order, lang, cot_norm,
     )
     bias_mine = exchanged(bias_part)
-    gain_rows = call(rows_kernel, "gain_rows", forward, [], [VMEM, VMEM], lang, gain)
+    gain_rows = call(rows_kernel, "gain_rows", forward, [], [VMEM, VMEM, VMEM], lang, gain, embedded)
     received, bias_part, gain_rows = lax.optimization_barrier((received, bias_part, gain_rows))
 
     sums, x = call(
@@ -244,13 +243,14 @@
         gain_kernel,
         "gain_part",
         shape(pieces, f32),
-        [pltpu.VMEM((tokens, width), bf16), pltpu.VMEM((tokens, width), bf16), pltpu.VMEM(pieces, f32), sems((3,))],
+        [pltpu.VMEM((2 * tokens, width), bf16), pltpu.VMEM(pieces, f32), sems((3,))],
         [VMEM, VMEM, VMEM, VMEM],
         lang, sums, x, cot,
         out_specs=HBM,
     )
     gain_mine = exchanged(gain_part)
-    bias_total = call(total_kernel, "bias_total", shape(pieces[1:], f32), [], [VMEM], bias_mine)
+    bias_near = call(total_kernel, "bias_near", shape(pieces[1:], f32), [], [VMEM], bias_mine)
+    bias_far = from_far(bias_near)
     back = call(
         grad_kernel,
         "input_grad",
@@ -259,19 +259,21 @@
         [SMEM, VMEM, VMEM, VMEM, VMEM, VMEM],
         mb_order, sums, x, cot, cot_res, gain_rows,
     )
+    gain_mine, back, bias_near = lax.optimization_barrier((gain_mine, back, bias_near))
+    gain_near = call(total_kernel, "gain_near", shape(pieces[1:], f32), [], [VMEM], gain_mine)
+    gain_far = from_far(gain_near)
+    gain_near, back = lax.optimization_barrier((gain_near, back))
     returned = lax.ppermute(back, "pipe", [(i, (i - 1) % stages) for i in range(stages)])
-    gain_mine, back, bias_total = lax.optimization_barrier((gain_mine, back, bias_total))
     both = (2 * pieces[1], width)
-    near_total = call(near_kernel, "near_parts", shape(both, f32), [], [VMEM, VMEM], gain_mine, bias_total)
-    far_total = lax.ppermute(near_total, "far_dp", [(0, 1), (1, 0)])
     total = call(
         add_kernel,
         "add_parts",
         shape((near, *both), f32),
         [pltpu.VMEM(both, f32), sems((near,))],
-        [VMEM, VMEM],
-        near_total, far_total,
+        [VMEM, VMEM, VMEM, VMEM],
+        gain_near, gain_far, bias_near, bias_far,
         out_specs=HBM,
+        cover=10**11,
     )
     totals = exchanged(total)
     sums, total = lax.optimization_barrier((sums, total))

time: 75.8 us -> 75.1 us (level)
  waiting for transfers between devices: 19.1 us -> 15.2 us
  starting transfers between devices: 22.1 us -> 25.6 us
    ppermute x1 -> x2, waiting for transfers between devices: 5.07 us -> 1.28 us  [from_far(): return lax.ppermute(total, 'far_dp', [(0, 1), (1, 0)])]
    ppermute x1 -> x2, starting transfers between devices: 3.38 us -> 6.89 us  [from_far(): return lax.ppermute(total, 'far_dp', [(0, 1), (1, 0)])]
    all_to_all x3, waiting for transfers between devices: 11.2 us -> 10.1 us  [exchanged(): return lax.all_to_all(pieces, NEAR, 0, 0)]
    ppermute x1, waiting for transfers between devices: 0.01 us -> 1 us  [local(): lax.ppermute(back, 'pipe', [(i, (i - 1) % stages) for i in range(stages)])]
  transfers between devices with their start and end apart: 6 -> 7, of which waited for: 4 -> 5; matrix products, arithmetic and copies ran while one was open for 0% -> 0% of each run, Pallas kernels for 8% -> 8%
where the time goes in v9:
time: 75.1 us; the launch traced here: 74.6 us
  starting transfers between devices  25.6 us (34%)
  blocking collectives  23.7 us (32%)
  waiting for transfers between devices  15.2 us (20%)
  Pallas kernels  8.23 us (11%)
  local copies, waits for them, and re-layouts  1.01 us (1%)
  between operations  0.81 us (1%)
    psum x2, blocking collectives, local(): sums = lax.psum(lax.psum(sums, 'core'), 'far')  23.7 us
    all_to_all x3, starting transfers between devices, exchanged(): return lax.all_to_all(pieces, NEAR, 0, 0)  14.6 us
    all_to_all x3, waiting for transfers between devices, exchanged(): return lax.all_to_all(pieces, NEAR, 0, 0)  10.1 us
    pallas_call x11, Pallas kernels, call(): pl.pallas_call(kernel, name=name, out_shape=outs, in_specs=in_specs, out_...  8.23 us
    ppermute x2, starting transfers between devices, from_far(): return lax.ppermute(total, 'far_dp', [(0, 1), (1, 0)])  6.89 us
    ppermute x1, waiting for transfers between devices, local(): lax.ppermute(section_out, 'pipe', [(i, i + 1) for i in range(stages - 1)])  2.84 us
    ppermute x1, starting transfers between devices, local(): lax.ppermute(back, 'pipe', [(i, (i - 1) % stages) for i in range(stages)])  2.73 us
  transfers between devices with their start and end apart: 7, of which 5 were waited for; matrix products, arithmetic and copies ran while one was open for 0% of the time, Pallas kernels for 8%

profile of v9, /device:TPU:6, one launch (start us, length us, event | category | flops | bytes accessed | tf_op | source)
XLA Modules:
  0.0 74.6 jit_solution(1813050624153744476)
XLA Ops:
  0.6 0.0 copy-start.6
  0.6 0.0 copy-start.5
  0.7 1.4 %collective-permute-start = (bf16[1,128,1536]{2,1,0:T(8,128)(2,1)}, bf16[1,128,1536]{2,1,0:T(8,128)(2,1)S(1)}, u32[]{:S(2)}, u32[]{:S(2)}) collective-permute-start(bf16[1,128,1536]{2,1,0:T(8,128)(2,1)} %param.8), channel_id=1, source_target_pairs={{0,8},{8,16},{16,24},{1,9},{9,17},{17,25},{2,10},{10,18},{18,26},{... | collective-permute-start | bytes 1179656 | tf_op jit(solution)/shard_map/ppermute | solution.py:214
  2.1 0.0 copy-done.6
  2.1 0.0 copy-done.5
  2.1 0.0 copy-start.1
  2.1 1.0 %copy-done.1 = bf16[1,128,1536]{2,1,0:T(8,128)(2,1)S(1)} copy-done((bf16[1,128,1536]{2,1,0:T(8,128)(2,1)S(1)}, bf16[1,128,1536]{2,1,0:T(8,128)(2,1)}, u32[]{:S(2)}) %copy-start.1) | copy-done | bytes 393240
  3.1 1.5 %bias_part.1 = (f32[8,8,1536]{2,1,0:T(8,128)}, bf16[128,1536]{1,0:T(8,128)(2,1)S(1)}) custom-call(s32[1,4]{1,0:T(1,128)S(1)} %copy-done.6, s32[1,128]{1,0:T(1,128)S(1)} %bitcast.4, bf16[1,128,1536]{2,1,0:T(8,128)(2,1)S(1)} %copy-done.1), custom_call_target="tpu_custom_call" | custom-call | tf_op jit(solution)/shard_map/bias_part/pallas_call | solution.py:22
  4.6 0.0 copy-start
  4.6 0.0 copy-start.3
  4.6 6.0 %all-to-all-start = ((f32[8,8,1536]{2,1,0:T(8,128)}), f32[8,8,1536]{2,1,0:T(8,128)S(1)}, u32[]{:S(2)}, u32[]{:S(2)}) async-start(f32[8,8,1536]{2,1,0:T(8,128)} %get-tuple-element.23), calls=%async_computation | async-start | bytes 786432 | tf_op jit(solution)/shard_map/all_to_all | solution.py:199
  10.6 0.0 copy-done
  10.6 0.0 copy-done.3
  10.6 0.3 gain_rows.1.gain_ref
  10.9 2.8 %collective-permute-done.recv_ref = bf16[1,128,1536]{2,1,0:T(8,128)(2,1)S(1)} collective-permute-done((bf16[1,128,1536]{2,1,0:T(8,128)(2,1)}, bf16[1,128,1536]{2,1,0:T(8,128)(2,1)S(1)}, u32[]{:S(2)}, u32[]{:S(2)}) %collective-permute-start) | collective-permute-done | bytes 393248 | tf_op jit(solution)/shard_map/ppermute | solution.py:214
  13.7 0.4 token_sums.1
  14.1 2.5 %psum.14 = f32[8,128]{1,0:T(8,128)S(1)} all-reduce(f32[8,128]{1,0:T(8,128)S(1)} %get-tuple-element.27), channel_id=1, replica_groups=mesh['far_dp'=2,'next'=2,'row'=4,'pipe'=4,'far'=4,'core'=2] {'core'}, use_global_device_ids=true, to_apply=%region_0.0 | all-reduce | flops 1024 | bytes 8192 | tf_op jit(solution)/shard_map/psum | solution.py:239
  16.6 21.3 %psum.15.sums_ref = f32[8,128]{1,0:T(8,128)S(1)} all-reduce(f32[8,128]{1,0:T(8,128)S(1)} %psum.14), channel_id=1, replica_groups=mesh['far_dp'=2,'next'=2,'row'=4,'pipe'=4,'far'=4,'core'=2] {'far'}, use_global_device_ids=true, to_apply=%region_1.0 | all-reduce | flops 1024 | bytes 8192 | tf_op jit(solution)/shard_map/psum | solution.py:239
  37.8 0.0 all-to-all-done.parts_ref
  37.8 1.2 %gain_part.1 = f32[8,8,1536]{2,1,0:T(8,128)} custom-call(s32[1,128]{1,0:T(1,128)S(1)} %bitcast.6, f32[8,128]{1,0:T(8,128)S(1)} %psum.15.sums_ref, bf16[128,1536]{1,0:T(8,128)(2,1)S(1)} %get-tuple-element.29.x_ref, bf16[128,1536]{1,0:T(8,128)(2,1)S(1)} %get-tuple-element.25.cot_ref), custom_call_target="tpu_custom_call" | custom-call | tf_op jit(solution)/shard_map/gain_part/pallas_call | solution.py:22
  39.0 4.9 %all-to-all-start.1 = ((f32[8,8,1536]{2,1,0:T(8,128)}), f32[8,8,1536]{2,1,0:T(8,128)S(1)}, u32[]{:S(2)}, u32[]{:S(2)}) async-start(f32[8,8,1536]{2,1,0:T(8,128)} %gain_part.1), calls=%async_computation.1 | async-start | bytes 786432 | tf_op jit(solution)/shard_map/all_to_all | solution.py:199
  44.0 0.0 copy-start.2
  44.0 3.5 %collective-permute-start.2 = (f32[8,1536]{1,0:T(8,128)S(1)}, f32[8,1536]{1,0:T(8,128)S(1)}, u32[]{:S(2)}, u32[]{:S(2)}) collective-permute-start(f32[8,1536]{1,0:T(8,128)S(1)} %bias_near.1.bias_ref), channel_id=1, source_target_pairs={{0,256},{256,0},{1,257},{257,1},{2,258},{258,2},{3,259},{259,3},{4... | collective-permute-start | bytes 147464 | tf_op jit(solution)/shard_map/ppermute | solution.py:203
  47.5 0.0 copy-done.2
  47.5 1.0 %input_grad.1 = bf16[1,128,1536]{2,1,0:T(8,128)(2,1)S(1)} custom-call(s32[1,4]{1,0:T(1,128)S(1)} %copy-done.6, f32[8,128]{1,0:T(8,128)S(1)} %psum.15.sums_ref, bf16[128,1536]{1,0:T(8,128)(2,1)S(1)} %get-tuple-element.29.x_ref, bf16[128,1536]{1,0:T(8,128)(2,1)S(1)} %get-tuple-element.25.cot_ref, bf16[1,128,1536]{2,1,0:T(8,128)(2,1)S(1)} %copy-done.2, ...), custom_call_target="tpu_custom_call" | custom-call | tf_op jit(solution)/shard_map/input_grad/pallas_call | solution.py:22
  48.5 3.6 %all-to-all-done.1.parts_ref = f32[8,8,1536]{2,1,0:T(8,128)S(1)} async-done(((f32[8,8,1536]{2,1,0:T(8,128)}), f32[8,8,1536]{2,1,0:T(8,128)S(1)}, u32[]{:S(2)}, u32[]{:S(2)}) %all-to-all-start.1) | async-done | bytes 393248 | tf_op jit(solution)/shard_map/all_to_all | solution.py:199
  52.2 3.4 %collective-permute-start.1 = (f32[8,1536]{1,0:T(8,128)S(1)}, f32[8,1536]{1,0:T(8,128)S(1)}, u32[]{:S(2)}, u32[]{:S(2)}) collective-permute-start(f32[8,1536]{1,0:T(8,128)S(1)} %gain_near.1.gain_ref), channel_id=1, source_target_pairs={{0,256},{256,0},{1,257},{257,1},{2,258},{258,2},{3,259},{259,3},{4... | collective-permute-start | bytes 147464 | tf_op jit(solution)/shard_map/ppermute | solution.py:203
  55.6 2.7 %collective-permute-start.3 = (bf16[1,128,1536]{2,1,0:T(8,128)(2,1)S(1)}, bf16[1,128,1536]{2,1,0:T(8,128)(2,1)S(1)}, u32[]{:S(2)}, u32[]{:S(2)}) collective-permute-start(bf16[1,128,1536]{2,1,0:T(8,128)(2,1)S(1)} %input_grad.1), channel_id=1, source_target_pairs={{0,24},{8,0},{16,8},{24,16},{1,25},{9,1},{17,9},{25,17},{2,26},{10... | collective-permute-start | bytes 1179656 | tf_op jit(solution)/shard_map/ppermute | solution.py:266
  58.3 0.0 collective-permute-done.2.bias_far_ref
  58.3 1.3 %collective-permute-done.1.gain_far_ref = f32[8,1536]{1,0:T(8,128)S(1)} collective-permute-done((f32[8,1536]{1,0:T(8,128)S(1)}, f32[8,1536]{1,0:T(8,128)S(1)}, u32[]{:S(2)}, u32[]{:S(2)}) %collective-permute-start.1) | collective-permute-done | bytes 49184 | tf_op jit(solution)/shard_map/ppermute | solution.py:203
  59.6 1.0 %add_parts.1 = f32[8,16,1536]{2,1,0:T(8,128)} custom-call(f32[8,1536]{1,0:T(8,128)S(1)} %gain_near.1.gain_ref, f32[8,1536]{1,0:T(8,128)S(1)} %collective-permute-done.1.gain_far_ref, f32[8,1536]{1,0:T(8,128)S(1)} %bias_near.1.bias_ref, f32[8,1536]{1,0:T(8,128)S(1)} %collective-permute-done.2.bias_far_ref), custom_call_target="tpu_custom_call" | custom-call | flops 99999997952 | tf_op jit(solution)/shard_map/add_parts/pallas_call | solution.py:22
  60.6 0.0 copy-start.4
  60.6 3.7 %all-to-all-start.2 = ((f32[8,16,1536]{2,1,0:T(8,128)}), f32[8,16,1536]{2,1,0:T(8,128)S(1)}, u32[]{:S(2)}, u32[]{:S(2)}) async-start(f32[8,16,1536]{2,1,0:T(8,128)} %add_parts.1), calls=%async_computation.2 | async-start | bytes 1572864 | tf_op jit(solution)/shard_map/all_to_all | solution.py:199
  64.3 0.0 copy-done.4
  64.3 1.1 %normed.1 = bf16[1,128,1536]{2,1,0:T(8,128)(2,1)} custom-call(s32[1,128]{1,0:T(1,128)S(1)} %bitcast.7, f32[8,128]{1,0:T(8,128)S(1)} %psum.15.sums_ref, bf16[128,1536]{1,0:T(8,128)(2,1)S(1)} %get-tuple-element.29.x_ref, bf16[128,1536]{1,0:T(8,128)(2,1)S(1)} %gain_rows.1.gain_ref, bf16[1,64,1536]{2,1,0:T(8,128)(2,1)S(1)} %copy-done.4), custom_call_target="tpu_custom_call" | custom-call | tf_op jit(solution)/shard_map/normed/pallas_call | solution.py:22
  65.5 1.0 %collective-permute-done.3.value_ref = bf16[1,128,1536]{2,1,0:T(8,128)(2,1)S(1)} collective-permute-done((bf16[1,128,1536]{2,1,0:T(8,128)(2,1)S(1)}, bf16[1,128,1536]{2,1,0:T(8,128)(2,1)S(1)}, u32[]{:S(2)}, u32[]{:S(2)}) %collective-permute-start.3) | collective-permute-done | bytes 393248 | tf_op jit(solution)/shard_map/ppermute | solution.py:266
  66.5 0.8 %settle.1 = bf16[1,128,1536]{2,1,0:T(8,128)(2,1)} custom-call(bf16[1,128,1536]{2,1,0:T(8,128)(2,1)S(1)} %collective-permute-done.3.value_ref), custom_call_target="tpu_custom_call" | custom-call | flops 99999997952 | tf_op jit(solution)/shard_map/settle/pallas_call | solution.py:22
  67.2 6.5 %all-to-all-done.2.parts_ref = f32[8,16,1536]{2,1,0:T(8,128)S(1)} async-done(((f32[8,16,1536]{2,1,0:T(8,128)}), f32[8,16,1536]{2,1,0:T(8,128)S(1)}, u32[]{:S(2)}, u32[]{:S(2)}) %all-to-all-start.2) | async-done | bytes 786464 | tf_op jit(solution)/shard_map/all_to_all | solution.py:199
  73.7 0.9 %whole_grads.1 = (f32[8,8,1536]{2,1,0:T(8,128)}, f32[8,8,1536]{2,1,0:T(8,128)}) custom-call(f32[8,16,1536]{2,1,0:T(8,128)S(1)} %all-to-all-done.2.parts_ref), custom_call_target="tpu_custom_call" | custom-call | tf_op jit(solution)/shard_map/whole_grads/pallas_call | solution.py:22
  (2 shorter events, 0.0 us)
Async XLA Ops:
  0.6 1.5 %copy-start.6 = (s32[1,4]{1,0:T(1,128)S(1)}, s32[1,4]{1,0:T(1,128)}, u32[]{:S(2)}) copy-start(s32[1,4]{1,0:T(1,128)} %order_ref.3) | copy-start | bytes 52
  0.6 1.5 %copy-start.5 = (s32[128]{0:T(128)S(1)}, s32[128]{0:T(128)}, u32[]{:S(2)}) copy-start(s32[128]{0:T(128)} %param.14) | copy-start | bytes 1540
  0.7 13.1 %collective-permute-start = (bf16[1,128,1536]{2,1,0:T(8,128)(2,1)}, bf16[1,128,1536]{2,1,0:T(8,128)(2,1)S(1)}, u32[]{:S(2)}, u32[]{:S(2)}) collective-permute-start(bf16[1,128,1536]{2,1,0:T(8,128)(2,1)} %param.8), channel_id=1, source_target_pairs={{0,8},{8,16},{16,24},{1,9},{9,17},{17,25},{2,10},{10,18},{18,26},{... | collective-permute-start | bytes 1179656 | tf_op jit(solution)/shard_map/ppermute | solution.py:214
  2.1 1.0 %copy-start.1 = (bf16[1,128,1536]{2,1,0:T(8,128)(2,1)S(1)}, bf16[1,128,1536]{2,1,0:T(8,128)(2,1)}, u32[]{:S(2)}) copy-start(bf16[1,128,1536]{2,1,0:T(8,128)(2,1)} %cot_ref.1) | copy-start | bytes 1179652
  4.6 6.0 %copy-start = (bf16[128,1536]{1,0:T(8,128)(2,1)S(1)}, bf16[128,1536]{1,0:T(8,128)(2,1)}, u32[]{:S(2)}) copy-start(bf16[128,1536]{1,0:T(8,128)(2,1)} %emb_ref.1) | copy-start | bytes 1179652
  4.6 6.0 %copy-start.3 = (bf16[1,64,1536]{2,1,0:T(8,128)(2,1)S(1)}, bf16[1,64,1536]{2,1,0:T(8,128)(2,1)}, u32[]{:S(2)}) copy-start(bf16[1,64,1536]{2,1,0:T(8,128)(2,1)} %table_ref.1) | copy-start | bytes 589828
  4.6 33.2 %all-to-all-start = ((f32[8,8,1536]{2,1,0:T(8,128)}), f32[8,8,1536]{2,1,0:T(8,128)S(1)}, u32[]{:S(2)}, u32[]{:S(2)}) async-start(f32[8,8,1536]{2,1,0:T(8,128)} %get-tuple-element.23), calls=%async_computation | async-start | bytes 786432 | tf_op jit(solution)/shard_map/all_to_all | solution.py:199
  39.0 13.1 %all-to-all-start.1 = ((f32[8,8,1536]{2,1,0:T(8,128)}), f32[8,8,1536]{2,1,0:T(8,128)S(1)}, u32[]{:S(2)}, u32[]{:S(2)}) async-start(f32[8,8,1536]{2,1,0:T(8,128)} %gain_part.1), calls=%async_computation.1 | async-start | bytes 786432 | tf_op jit(solution)/shard_map/all_to_all | solution.py:199
  44.0 3.6 %copy-start.2 = (bf16[1,128,1536]{2,1,0:T(8,128)(2,1)S(1)}, bf16[1,128,1536]{2,1,0:T(8,128)(2,1)}, u32[]{:S(2)}) copy-start(bf16[1,128,1536]{2,1,0:T(8,128)(2,1)} %res_ref.1) | copy-start | bytes 1179652
  44.0 14.3 %collective-permute-start.2 = (f32[8,1536]{1,0:T(8,128)S(1)}, f32[8,1536]{1,0:T(8,128)S(1)}, u32[]{:S(2)}, u32[]{:S(2)}) collective-permute-start(f32[8,1536]{1,0:T(8,128)S(1)} %bias_near.1.bias_ref), channel_id=1, source_target_pairs={{0,256},{256,0},{1,257},{257,1},{2,258},{258,2},{3,259},{259,3},{4... | collective-permute-start | bytes 147464 | tf_op jit(solution)/shard_map/ppermute | solution.py:203
  52.2 7.4 %collective-permute-start.1 = (f32[8,1536]{1,0:T(8,128)S(1)}, f32[8,1536]{1,0:T(8,128)S(1)}, u32[]{:S(2)}, u32[]{:S(2)}) collective-permute-start(f32[8,1536]{1,0:T(8,128)S(1)} %gain_near.1.gain_ref), channel_id=1, source_target_pairs={{0,256},{256,0},{1,257},{257,1},{2,258},{258,2},{3,259},{259,3},{4... | collective-permute-start | bytes 147464 | tf_op jit(solution)/shard_map/ppermute | solution.py:203
  55.6 10.9 %collective-permute-start.3 = (bf16[1,128,1536]{2,1,0:T(8,128)(2,1)S(1)}, bf16[1,128,1536]{2,1,0:T(8,128)(2,1)S(1)}, u32[]{:S(2)}, u32[]{:S(2)}) collective-permute-start(bf16[1,128,1536]{2,1,0:T(8,128)(2,1)S(1)} %input_grad.1), channel_id=1, source_target_pairs={{0,24},{8,0},{16,8},{24,16},{1,25},{9,1},{17,9},{25,17},{2,26},{10... | collective-permute-start | bytes 1179656 | tf_op jit(solution)/shard_map/ppermute | solution.py:266
  60.6 3.7 %copy-start.4 = (bf16[1,64,1536]{2,1,0:T(8,128)(2,1)S(1)}, bf16[1,64,1536]{2,1,0:T(8,128)(2,1)}, u32[]{:S(2)}) copy-start(bf16[1,64,1536]{2,1,0:T(8,128)(2,1)} %bias_ref.1) | copy-start | bytes 589828
  60.6 13.1 %all-to-all-start.2 = ((f32[8,16,1536]{2,1,0:T(8,128)}), f32[8,16,1536]{2,1,0:T(8,128)S(1)}, u32[]{:S(2)}, u32[]{:S(2)}) async-start(f32[8,16,1536]{2,1,0:T(8,128)} %add_parts.1), calls=%async_computation.2 | async-start | bytes 1572864 | tf_op jit(solution)/shard_map/all_to_all | solution.py:199

commit v10 on v9

--- a/solution.py
+++ b/solution.py
@@ -18,7 +18,7 @@
 HBM = pl.BlockSpec(memory_space=pltpu.HBM)
 
 
-def call(kernel, name, outs, scratch, in_specs, *args, cover=0, out_specs=None):
+def call(kernel, name, outs, scratch, in_specs, *args, cover=0, out_specs=None, aliases=None):
     return pl.pallas_call(
         kernel,
         name=name,
@@ -26,6 +26,7 @@
         in_specs=in_specs,
         out_specs=jax.tree.map(lambda _: VMEM, outs) if out_specs is None else out_specs,
         scratch_shapes=scratch,
+        input_output_aliases=aliases or {},
         cost_estimate=pl.CostEstimate(flops=cover, transcendentals=0, bytes_accessed=0) if cover else None,
         compiler_params=pltpu.CompilerParams(vmem_limit_bytes=40 * 1024 * 1024),
     )(*args)
@@ -170,21 +171,36 @@
     out_ref[...] = added(parts_ref)
 
 
-def add_kernel(gain_ref, gain_far_ref, bias_ref, bias_far_ref, out_ref, total_scr, sems):
-    height = gain_ref.shape[0]
-    total_scr[:height, :] = gain_ref[...] + gain_far_ref[...]
-    total_scr[height:, :] = bias_ref[...] + bias_far_ref[...]
-    run_copies([pltpu.make_async_copy(total_scr, out_ref.at[k], sems.at[k]) for k in range(out_ref.shape[0])])
-
-
-def whole_kernel(parts_ref, gain_ref, bias_ref, sems):
-    height = gain_ref.shape[1]
+def copy_rows(total_scr, top, out_ref, sems):
+    height = total_scr.shape[0]
     run_copies(
         [
-            pltpu.make_async_copy(parts_ref.at[:, pl.ds(i * height, height), :], out_ref, sems.at[i])
-            for i, out_ref in enumerate((gain_ref, bias_ref))
+            pltpu.make_async_copy(total_scr, out_ref.at[k, pl.ds(top, height), :], sems.at[k])
+            for k in range(out_ref.shape[0])
         ]
     )
+
+
+def low_kernel(near_ref, far_ref, out_ref, total_scr, sems):
+    total_scr[...] = near_ref[...] + far_ref[...]
+    copy_rows(total_scr, total_scr.shape[0], out_ref, sems)
+
+
+def high_kernel(near_ref, far_ref, lower_ref, out_ref, total_scr, sems):
+    total_scr[...] = near_ref[...] + far_ref[...]
+    copy_rows(total_scr, 0, out_ref, sems)
+
+
+def whole_kernel(parts_ref, gain_ref, bias_ref, sems):
+    pieces, height, _ = gain_ref.shape
+    parts = sems.shape[1]
+    copies = []
+    for i, out_ref in enumerate((gain_ref, bias_ref)):
+        for j in range(parts):
+            here = pl.ds(j * (pieces // parts), pieces // parts)
+            source = parts_ref.at[here, pl.ds(i * height, height), :]
+            copies.append(pltpu.make_async_copy(source, out_ref.at[here], sems.at[i, j]))
+    run_copies(copies)
 
 
 def settle_kernel(value_ref, out_ref, sem):
@@ -243,7 +259,7 @@
         gain_kernel,
         "gain_part",
         shape(pieces, f32),
-        [pltpu.VMEM((2 * tokens, width), bf16), pltpu.VMEM(pieces, f32), sems((3,))],
+        [pltpu.VMEM((2 * tokens, width), bf16), pltpu.VMEM(pieces, f32), sems((6,))],
         [VMEM, VMEM, VMEM, VMEM],
         lang, sums, x, cot,
         out_specs=HBM,
@@ -265,14 +281,17 @@
     gain_near, back = lax.optimization_barrier((gain_near, back))
     returned = lax.ppermute(back, "pipe", [(i, (i - 1) % stages) for i in range(stages)])
     both = (2 * pieces[1], width)
+    room = [pltpu.VMEM(pieces[1:], f32), sems((near,))]
+    lower = call(low_kernel, "bias_rows", shape((near, *both), f32), room, [VMEM, VMEM], bias_near, bias_far, out_specs=HBM)
     total = call(
-        add_kernel,
+        high_kernel,
         "add_parts",
         shape((near, *both), f32),
-        [pltpu.VMEM(both, f32), sems((near,))],
-        [VMEM, VMEM, VMEM, VMEM],
-        gain_near, gain_far, bias_near, bias_far,
+        room,
+        [VMEM, VMEM, HBM],
+        gain_near, gain_far, lower,
         out_specs=HBM,
+        aliases={2: 0},
         cover=10**11,
     )
     totals = exchanged(total)
@@ -289,7 +308,7 @@
     totals, returned, normed = lax.optimization_barrier((totals, returned, normed))
     grads = shape(pieces, f32)
     gain_grad, bias_grad = call(
-        whole_kernel, "whole_grads", (grads, grads), [sems((2,))], [VMEM], totals, out_specs=(HBM, HBM)
+        whole_kernel, "whole_grads", (grads, grads), [sems((2, 4))], [VMEM], totals, out_specs=(HBM, HBM)
     )
     gain_grad, bias_grad = (g.reshape(1, langs, width) for g in (gain_grad, bias_grad))
     return normed, returned, gain_grad, bias_grad

time: 75.1 us -> 75.8 us (level); the launches traced: 74.6 us -> 74.5 us
  waiting for transfers between devices: 15.2 us -> 14.4 us
    ppermute x2, waiting for transfers between devices: 1.28 us -> 0.43 us  [from_far(): return lax.ppermute(total, 'far_dp', [(0, 1), (1, 0)])]
    pallas_call x11 -> x12, Pallas kernels: 8.23 us -> 8.97 us  [call(): pl.pallas_call(kernel, name=name, out_shape=outs, in_specs=in_specs, out_...]
  transfers between devices with their start and end apart: 7 -> 7, of which waited for: 5 -> 5; matrix products, arithmetic and copies ran while one was open for 0% -> 0% of each run, Pallas kernels for 8% -> 9%
where the time goes in v10:
time: 75.8 us; the launch traced here: 74.5 us
  starting transfers between devices  25.6 us (34%)
  blocking collectives  23.7 us (31%)
  waiting for transfers between devices  14.4 us (19%)
  Pallas kernels  8.97 us (12%)
  local copies, waits for them, and re-layouts  1.01 us (1%)
  between operations  0.82 us (1%)
    psum x2, blocking collectives, local(): sums = lax.psum(lax.psum(sums, 'core'), 'far')  23.7 us
    all_to_all x3, starting transfers between devices, exchanged(): return lax.all_to_all(pieces, NEAR, 0, 0)  14.6 us
    all_to_all x3, waiting for transfers between devices, exchanged(): return lax.all_to_all(pieces, NEAR, 0, 0)  9.96 us
    pallas_call x12, Pallas kernels, call(): pl.pallas_call(kernel, name=name, out_shape=outs, in_specs=in_specs, out_...  8.97 us
    ppermute x2, starting transfers between devices, from_far(): return lax.ppermute(total, 'far_dp', [(0, 1), (1, 0)])  6.89 us
    ppermute x1, waiting for transfers between devices, local(): lax.ppermute(section_out, 'pipe', [(i, i + 1) for i in range(stages - 1)])  2.84 us
    ppermute x1, starting transfers between devices, local(): lax.ppermute(back, 'pipe', [(i, (i - 1) % stages) for i in range(stages)])  2.73 us
  transfers between devices with their start and end apart: 7, of which 5 were waited for; matrix products, arithmetic and copies ran while one was open for 0% of the time, Pallas kernels for 9%

profile of v10, /device:TPU:6, one launch (start us, length us, event | category | flops | bytes accessed | tf_op | source)
XLA Modules:
  0.0 74.5 jit_solution(17107065963394935012)
XLA Ops:
  0.6 0.0 copy-start.6
  0.6 0.0 copy-start.5
  0.7 1.4 %collective-permute-start = (bf16[1,128,1536]{2,1,0:T(8,128)(2,1)}, bf16[1,128,1536]{2,1,0:T(8,128)(2,1)S(1)}, u32[]{:S(2)}, u32[]{:S(2)}) collective-permute-start(bf16[1,128,1536]{2,1,0:T(8,128)(2,1)} %param.8), channel_id=1, source_target_pairs={{0,8},{8,16},{16,24},{1,9},{9,17},{17,25},{2,10},{10,18},{18,26},{... | collective-permute-start | bytes 1179656 | tf_op jit(solution)/shard_map/ppermute | solution.py:230
  2.1 0.0 copy-done.6
  2.1 0.0 copy-done.5
  2.1 0.0 copy-start.1
  2.1 1.0 %copy-done.1 = bf16[1,128,1536]{2,1,0:T(8,128)(2,1)S(1)} copy-done((bf16[1,128,1536]{2,1,0:T(8,128)(2,1)S(1)}, bf16[1,128,1536]{2,1,0:T(8,128)(2,1)}, u32[]{:S(2)}) %copy-start.1) | copy-done | bytes 393240
  3.1 1.5 %bias_part.1 = (f32[8,8,1536]{2,1,0:T(8,128)}, bf16[128,1536]{1,0:T(8,128)(2,1)S(1)}) custom-call(s32[1,4]{1,0:T(1,128)S(1)} %copy-done.6, s32[1,128]{1,0:T(1,128)S(1)} %bitcast.4, bf16[1,128,1536]{2,1,0:T(8,128)(2,1)S(1)} %copy-done.1), custom_call_target="tpu_custom_call" | custom-call | tf_op jit(solution)/shard_map/bias_part/pallas_call | solution.py:22
  4.6 0.0 copy-start
  4.6 0.0 copy-start.3
  4.6 6.0 %all-to-all-start = ((f32[8,8,1536]{2,1,0:T(8,128)}), f32[8,8,1536]{2,1,0:T(8,128)S(1)}, u32[]{:S(2)}, u32[]{:S(2)}) async-start(f32[8,8,1536]{2,1,0:T(8,128)} %get-tuple-element.23), calls=%async_computation | async-start | bytes 786432 | tf_op jit(solution)/shard_map/all_to_all | solution.py:215
  10.6 0.0 copy-done
  10.6 0.0 copy-done.3
  10.6 0.3 gain_rows.1.gain_ref
  10.9 2.8 %collective-permute-done.recv_ref = bf16[1,128,1536]{2,1,0:T(8,128)(2,1)S(1)} collective-permute-done((bf16[1,128,1536]{2,1,0:T(8,128)(2,1)}, bf16[1,128,1536]{2,1,0:T(8,128)(2,1)S(1)}, u32[]{:S(2)}, u32[]{:S(2)}) %collective-permute-start) | collective-permute-done | bytes 393248 | tf_op jit(solution)/shard_map/ppermute | solution.py:230
  13.7 0.4 token_sums.1
  14.1 2.5 %psum.14 = f32[8,128]{1,0:T(8,128)S(1)} all-reduce(f32[8,128]{1,0:T(8,128)S(1)} %get-tuple-element.27), channel_id=1, replica_groups=mesh['far_dp'=2,'next'=2,'row'=4,'pipe'=4,'far'=4,'core'=2] {'core'}, use_global_device_ids=true, to_apply=%region_0.0 | all-reduce | flops 1024 | bytes 8192 | tf_op jit(solution)/shard_map/psum | solution.py:255
  16.6 21.3 %psum.15.sums_ref = f32[8,128]{1,0:T(8,128)S(1)} all-reduce(f32[8,128]{1,0:T(8,128)S(1)} %psum.14), channel_id=1, replica_groups=mesh['far_dp'=2,'next'=2,'row'=4,'pipe'=4,'far'=4,'core'=2] {'far'}, use_global_device_ids=true, to_apply=%region_1.0 | all-reduce | flops 1024 | bytes 8192 | tf_op jit(solution)/shard_map/psum | solution.py:255
  37.8 0.0 all-to-all-done.parts_ref
  37.8 1.2 %gain_part.1 = f32[8,8,1536]{2,1,0:T(8,128)} custom-call(s32[1,128]{1,0:T(1,128)S(1)} %bitcast.6, f32[8,128]{1,0:T(8,128)S(1)} %psum.15.sums_ref, bf16[128,1536]{1,0:T(8,128)(2,1)S(1)} %get-tuple-element.29.x_ref, bf16[128,1536]{1,0:T(8,128)(2,1)S(1)} %get-tuple-element.25.cot_ref), custom_call_target="tpu_custom_call" | custom-call | tf_op jit(solution)/shard_map/gain_part/pallas_call | solution.py:22
  39.1 4.9 %all-to-all-start.1 = ((f32[8,8,1536]{2,1,0:T(8,128)}), f32[8,8,1536]{2,1,0:T(8,128)S(1)}, u32[]{:S(2)}, u32[]{:S(2)}) async-start(f32[8,8,1536]{2,1,0:T(8,128)} %gain_part.1), calls=%async_computation.1 | async-start | bytes 786432 | tf_op jit(solution)/shard_map/all_to_all | solution.py:215
  44.0 0.0 copy-start.2
  44.0 3.5 %collective-permute-start.2 = (f32[8,1536]{1,0:T(8,128)S(1)}, f32[8,1536]{1,0:T(8,128)S(1)}, u32[]{:S(2)}, u32[]{:S(2)}) collective-permute-start(f32[8,1536]{1,0:T(8,128)S(1)} %bias_near.1.near_ref), channel_id=1, source_target_pairs={{0,256},{256,0},{1,257},{257,1},{2,258},{258,2},{3,259},{259,3},{4... | collective-permute-start | bytes 147464 | tf_op jit(solution)/shard_map/ppermute | solution.py:219
  47.5 0.0 copy-done.2
  47.5 1.0 %input_grad.1 = bf16[1,128,1536]{2,1,0:T(8,128)(2,1)S(1)} custom-call(s32[1,4]{1,0:T(1,128)S(1)} %copy-done.6, f32[8,128]{1,0:T(8,128)S(1)} %psum.15.sums_ref, bf16[128,1536]{1,0:T(8,128)(2,1)S(1)} %get-tuple-element.29.x_ref, bf16[128,1536]{1,0:T(8,128)(2,1)S(1)} %get-tuple-element.25.cot_ref, bf16[1,128,1536]{2,1,0:T(8,128)(2,1)S(1)} %copy-done.2, ...), custom_call_target="tpu_custom_call" | custom-call | tf_op jit(solution)/shard_map/input_grad/pallas_call | solution.py:22
  48.6 3.6 %all-to-all-done.1.parts_ref = f32[8,8,1536]{2,1,0:T(8,128)S(1)} async-done(((f32[8,8,1536]{2,1,0:T(8,128)}), f32[8,8,1536]{2,1,0:T(8,128)S(1)}, u32[]{:S(2)}, u32[]{:S(2)}) %all-to-all-start.1) | async-done | bytes 393248 | tf_op jit(solution)/shard_map/all_to_all | solution.py:215
  52.2 3.4 %collective-permute-start.1 = (f32[8,1536]{1,0:T(8,128)S(1)}, f32[8,1536]{1,0:T(8,128)S(1)}, u32[]{:S(2)}, u32[]{:S(2)}) collective-permute-start(f32[8,1536]{1,0:T(8,128)S(1)} %gain_near.1.near_ref), channel_id=1, source_target_pairs={{0,256},{256,0},{1,257},{257,1},{2,258},{258,2},{3,259},{259,3},{4... | collective-permute-start | bytes 147464 | tf_op jit(solution)/shard_map/ppermute | solution.py:219
  55.6 2.7 %collective-permute-start.3 = (bf16[1,128,1536]{2,1,0:T(8,128)(2,1)S(1)}, bf16[1,128,1536]{2,1,0:T(8,128)(2,1)S(1)}, u32[]{:S(2)}, u32[]{:S(2)}) collective-permute-start(bf16[1,128,1536]{2,1,0:T(8,128)(2,1)S(1)} %input_grad.1), channel_id=1, source_target_pairs={{0,24},{8,0},{16,8},{24,16},{1,25},{9,1},{17,9},{25,17},{2,26},{10... | collective-permute-start | bytes 1179656 | tf_op jit(solution)/shard_map/ppermute | solution.py:282
  58.3 0.0 collective-permute-done.2.far_ref
  58.3 0.8 %bias_rows.1.lower_ref = f32[8,16,1536]{2,1,0:T(8,128)} custom-call(f32[8,1536]{1,0:T(8,128)S(1)} %bias_near.1.near_ref, f32[8,1536]{1,0:T(8,128)S(1)} %collective-permute-done.2.far_ref), custom_call_target="tpu_custom_call" | custom-call | tf_op jit(solution)/shard_map/bias_rows/pallas_call | solution.py:22
  59.2 0.4 collective-permute-done.1.far_ref
  59.6 0.8 %add_parts.1 = f32[8,16,1536]{2,1,0:T(8,128)} custom-call(f32[8,1536]{1,0:T(8,128)S(1)} %gain_near.1.near_ref, f32[8,1536]{1,0:T(8,128)S(1)} %collective-permute-done.1.far_ref, f32[8,16,1536]{2,1,0:T(8,128)} %bias_rows.1.lower_ref), custom_call_target="tpu_custom_call", output_to_operand_aliasing={{}: (2, {})} | custom-call | flops 99999997952 | tf_op jit(solution)/shard_map/add_parts/pallas_call | solution.py:22
  60.5 0.0 copy-start.4
  60.5 3.7 %all-to-all-start.2 = ((f32[8,16,1536]{2,1,0:T(8,128)}), f32[8,16,1536]{2,1,0:T(8,128)S(1)}, u32[]{:S(2)}, u32[]{:S(2)}) async-start(f32[8,16,1536]{2,1,0:T(8,128)} %add_parts.1), calls=%async_computation.2 | async-start | bytes 1572864 | tf_op jit(solution)/shard_map/all_to_all | solution.py:215
  64.2 0.0 copy-done.4
  64.2 1.1 %normed.1 = bf16[1,128,1536]{2,1,0:T(8,128)(2,1)} custom-call(s32[1,128]{1,0:T(1,128)S(1)} %bitcast.7, f32[8,128]{1,0:T(8,128)S(1)} %psum.15.sums_ref, bf16[128,1536]{1,0:T(8,128)(2,1)S(1)} %get-tuple-element.29.x_ref, bf16[128,1536]{1,0:T(8,128)(2,1)S(1)} %gain_rows.1.gain_ref, bf16[1,64,1536]{2,1,0:T(8,128)(2,1)S(1)} %copy-done.4), custom_call_target="tpu_custom_call" | custom-call | tf_op jit(solution)/shard_map/normed/pallas_call | solution.py:22
  65.3 1.2 %collective-permute-done.3.value_ref = bf16[1,128,1536]{2,1,0:T(8,128)(2,1)S(1)} collective-permute-done((bf16[1,128,1536]{2,1,0:T(8,128)(2,1)S(1)}, bf16[1,128,1536]{2,1,0:T(8,128)(2,1)S(1)}, u32[]{:S(2)}, u32[]{:S(2)}) %collective-permute-start.3) | collective-permute-done | bytes 393248 | tf_op jit(solution)/shard_map/ppermute | solution.py:282
  66.5 0.8 %settle.1 = bf16[1,128,1536]{2,1,0:T(8,128)(2,1)} custom-call(bf16[1,128,1536]{2,1,0:T(8,128)(2,1)S(1)} %collective-permute-done.3.value_ref), custom_call_target="tpu_custom_call" | custom-call | flops 99999997952 | tf_op jit(solution)/shard_map/settle/pallas_call | solution.py:22
  67.2 6.3 %all-to-all-done.2.parts_ref = f32[8,16,1536]{2,1,0:T(8,128)S(1)} async-done(((f32[8,16,1536]{2,1,0:T(8,128)}), f32[8,16,1536]{2,1,0:T(8,128)S(1)}, u32[]{:S(2)}, u32[]{:S(2)}) %all-to-all-start.2) | async-done | bytes 786464 | tf_op jit(solution)/shard_map/all_to_all | solution.py:215
  73.6 0.9 %whole_grads.1 = (f32[8,8,1536]{2,1,0:T(8,128)}, f32[8,8,1536]{2,1,0:T(8,128)}) custom-call(f32[8,16,1536]{2,1,0:T(8,128)S(1)} %all-to-all-done.2.parts_ref), custom_call_target="tpu_custom_call" | custom-call | tf_op jit(solution)/shard_map/whole_grads/pallas_call | solution.py:22
  (2 shorter events, 0.0 us)
Async XLA Ops:
  0.6 1.5 %copy-start.6 = (s32[1,4]{1,0:T(1,128)S(1)}, s32[1,4]{1,0:T(1,128)}, u32[]{:S(2)}) copy-start(s32[1,4]{1,0:T(1,128)} %order_ref.3) | copy-start | bytes 52
  0.6 1.5 %copy-start.5 = (s32[128]{0:T(128)S(1)}, s32[128]{0:T(128)}, u32[]{:S(2)}) copy-start(s32[128]{0:T(128)} %param.14) | copy-start | bytes 1540
  0.7 13.1 %collective-permute-start = (bf16[1,128,1536]{2,1,0:T(8,128)(2,1)}, bf16[1,128,1536]{2,1,0:T(8,128)(2,1)S(1)}, u32[]{:S(2)}, u32[]{:S(2)}) collective-permute-start(bf16[1,128,1536]{2,1,0:T(8,128)(2,1)} %param.8), channel_id=1, source_target_pairs={{0,8},{8,16},{16,24},{1,9},{9,17},{17,25},{2,10},{10,18},{18,26},{... | collective-permute-start | bytes 1179656 | tf_op jit(solution)/shard_map/ppermute | solution.py:230
  2.1 1.0 %copy-start.1 = (bf16[1,128,1536]{2,1,0:T(8,128)(2,1)S(1)}, bf16[1,128,1536]{2,1,0:T(8,128)(2,1)}, u32[]{:S(2)}) copy-start(bf16[1,128,1536]{2,1,0:T(8,128)(2,1)} %cot_ref.1) | copy-start | bytes 1179652
  4.6 6.0 %copy-start = (bf16[128,1536]{1,0:T(8,128)(2,1)S(1)}, bf16[128,1536]{1,0:T(8,128)(2,1)}, u32[]{:S(2)}) copy-start(bf16[128,1536]{1,0:T(8,128)(2,1)} %emb_ref.1) | copy-start | bytes 1179652
  4.6 6.0 %copy-start.3 = (bf16[1,64,1536]{2,1,0:T(8,128)(2,1)S(1)}, bf16[1,64,1536]{2,1,0:T(8,128)(2,1)}, u32[]{:S(2)}) copy-start(bf16[1,64,1536]{2,1,0:T(8,128)(2,1)} %table_ref.1) | copy-start | bytes 589828
  4.6 33.2 %all-to-all-start = ((f32[8,8,1536]{2,1,0:T(8,128)}), f32[8,8,1536]{2,1,0:T(8,128)S(1)}, u32[]{:S(2)}, u32[]{:S(2)}) async-start(f32[8,8,1536]{2,1,0:T(8,128)} %get-tuple-element.23), calls=%async_computation | async-start | bytes 786432 | tf_op jit(solution)/shard_map/all_to_all | solution.py:215
  39.1 13.1 %all-to-all-start.1 = ((f32[8,8,1536]{2,1,0:T(8,128)}), f32[8,8,1536]{2,1,0:T(8,128)S(1)}, u32[]{:S(2)}, u32[]{:S(2)}) async-start(f32[8,8,1536]{2,1,0:T(8,128)} %gain_part.1), calls=%async_computation.1 | async-start | bytes 786432 | tf_op jit(solution)/shard_map/all_to_all | solution.py:215
  44.0 3.6 %copy-start.2 = (bf16[1,128,1536]{2,1,0:T(8,128)(2,1)S(1)}, bf16[1,128,1536]{2,1,0:T(8,128)(2,1)}, u32[]{:S(2)}) copy-start(bf16[1,128,1536]{2,1,0:T(8,128)(2,1)} %res_ref.1) | copy-start | bytes 1179652
  44.0 14.3 %collective-permute-start.2 = (f32[8,1536]{1,0:T(8,128)S(1)}, f32[8,1536]{1,0:T(8,128)S(1)}, u32[]{:S(2)}, u32[]{:S(2)}) collective-permute-start(f32[8,1536]{1,0:T(8,128)S(1)} %bias_near.1.near_ref), channel_id=1, source_target_pairs={{0,256},{256,0},{1,257},{257,1},{2,258},{258,2},{3,259},{259,3},{4... | collective-permute-start | bytes 147464 | tf_op jit(solution)/shard_map/ppermute | solution.py:219
  52.2 7.4 %collective-permute-start.1 = (f32[8,1536]{1,0:T(8,128)S(1)}, f32[8,1536]{1,0:T(8,128)S(1)}, u32[]{:S(2)}, u32[]{:S(2)}) collective-permute-start(f32[8,1536]{1,0:T(8,128)S(1)} %gain_near.1.near_ref), channel_id=1, source_target_pairs={{0,256},{256,0},{1,257},{257,1},{2,258},{258,2},{3,259},{259,3},{4... | collective-permute-start | bytes 147464 | tf_op jit(solution)/shard_map/ppermute | solution.py:219
  55.6 10.9 %collective-permute-start.3 = (bf16[1,128,1536]{2,1,0:T(8,128)(2,1)S(1)}, bf16[1,128,1536]{2,1,0:T(8,128)(2,1)S(1)}, u32[]{:S(2)}, u32[]{:S(2)}) collective-permute-start(bf16[1,128,1536]{2,1,0:T(8,128)(2,1)S(1)} %input_grad.1), channel_id=1, source_target_pairs={{0,24},{8,0},{16,8},{24,16},{1,25},{9,1},{17,9},{25,17},{2,26},{10... | collective-permute-start | bytes 1179656 | tf_op jit(solution)/shard_map/ppermute | solution.py:282
  60.5 3.7 %copy-start.4 = (bf16[1,64,1536]{2,1,0:T(8,128)(2,1)S(1)}, bf16[1,64,1536]{2,1,0:T(8,128)(2,1)}, u32[]{:S(2)}) copy-start(bf16[1,64,1536]{2,1,0:T(8,128)(2,1)} %bias_ref.1) | copy-start | bytes 589828
  60.5 13.1 %all-to-all-start.2 = ((f32[8,16,1536]{2,1,0:T(8,128)}), f32[8,16,1536]{2,1,0:T(8,128)S(1)}, u32[]{:S(2)}, u32[]{:S(2)}) async-start(f32[8,16,1536]{2,1,0:T(8,128)} %add_parts.1), calls=%async_computation.2 | async-start | bytes 1572864 | tf_op jit(solution)/shard_map/all_to_all | solution.py:215

commit v11 on v9

--- a/solution.py
+++ b/solution.py
@@ -250,7 +250,6 @@
     )
     gain_mine = exchanged(gain_part)
     bias_near = call(total_kernel, "bias_near", shape(pieces[1:], f32), [], [VMEM], bias_mine)
-    bias_far = from_far(bias_near)
     back = call(
         grad_kernel,
         "input_grad",
@@ -259,11 +258,11 @@
         [SMEM, VMEM, VMEM, VMEM, VMEM, VMEM],
         mb_order, sums, x, cot, cot_res, gain_rows,
     )
+    returned = lax.ppermute(back, "pipe", [(i, (i - 1) % stages) for i in range(stages)])
     gain_mine, back, bias_near = lax.optimization_barrier((gain_mine, back, bias_near))
     gain_near = call(total_kernel, "gain_near", shape(pieces[1:], f32), [], [VMEM], gain_mine)
-    gain_far = from_far(gain_near)
-    gain_near, back = lax.optimization_barrier((gain_near, back))
-    returned = lax.ppermute(back, "pipe", [(i, (i - 1) % stages) for i in range(stages)])
+    gain_near, bias_near = lax.optimization_barrier((gain_near, bias_near))
+    gain_far, bias_far = from_far(gain_near), from_far(bias_near)
     both = (2 * pieces[1], width)
     total = call(
         add_kernel,
@@ -273,7 +272,6 @@
         [VMEM, VMEM, VMEM, VMEM],
         gain_near, gain_far, bias_near, bias_far,
         out_specs=HBM,
-        cover=10**11,
     )
     totals = exchanged(total)
     sums, total = lax.optimization_barrier((sums, total))

time: 75.1 us -> 78.1 us (1.040)
  waiting for transfers between devices: 15.2 us -> 18 us
    ppermute x2, waiting for transfers between devices: 1.28 us -> 4.04 us  [from_far(): return lax.ppermute(total, 'far_dp', [(0, 1), (1, 0)])]
    all_to_all x3, waiting for transfers between devices: 10.1 us -> 11.2 us  [exchanged(): return lax.all_to_all(pieces, NEAR, 0, 0)]
    ppermute x1, waiting for transfers between devices: 1 us -> 0.01 us  [local(): lax.ppermute(back, 'pipe', [(i, (i - 1) % stages) for i in range(stages)])]
where the time goes in v11:
time: 78.1 us; the launch traced here: 77.5 us
  starting transfers between devices  25.5 us (33%)
  blocking collectives  23.7 us (30%)
  waiting for transfers between devices  18 us (23%)
  Pallas kernels  8.22 us (11%)
  local copies, waits for them, and re-layouts  1.3 us (2%)
  between operations  0.81 us (1%)
    psum x2, blocking collectives, local(): sums = lax.psum(lax.psum(sums, 'core'), 'far')  23.7 us
    all_to_all x3, starting transfers between devices, exchanged(): return lax.all_to_all(pieces, NEAR, 0, 0)  14.6 us
    all_to_all x3, waiting for transfers between devices, exchanged(): return lax.all_to_all(pieces, NEAR, 0, 0)  11.2 us
    pallas_call x11, Pallas kernels, call(): pl.pallas_call(kernel, name=name, out_shape=outs, in_specs=in_specs, out_...  8.22 us
    ppermute x2, starting transfers between devices, from_far(): return lax.ppermute(total, 'far_dp', [(0, 1), (1, 0)])  6.74 us
    ppermute x2, waiting for transfers between devices, from_far(): return lax.ppermute(total, 'far_dp', [(0, 1), (1, 0)])  4.04 us
    ppermute x1, waiting for transfers between devices, local(): lax.ppermute(section_out, 'pipe', [(i, i + 1) for i in range(stages - 1)])  2.84 us
    ppermute x1, starting transfers between devices, local(): lax.ppermute(back, 'pipe', [(i, (i - 1) % stages) for i in range(stages)])  2.74 us
  transfers between devices with their start and end apart: 7, of which 5 were waited for; matrix products, arithmetic and copies ran while one was open for 0% of the time, Pallas kernels for 8%

profile of v11, /device:TPU:6, one launch (start us, length us, event | category | flops | bytes accessed | tf_op | source)
XLA Modules:
  0.0 77.5 jit_solution(16800427574094122594)
XLA Ops:
  0.6 0.0 copy-start.6
  0.6 0.0 copy-start.5
  0.7 1.4 %collective-permute-start = (bf16[1,128,1536]{2,1,0:T(8,128)(2,1)}, bf16[1,128,1536]{2,1,0:T(8,128)(2,1)S(1)}, u32[]{:S(2)}, u32[]{:S(2)}) collective-permute-start(bf16[1,128,1536]{2,1,0:T(8,128)(2,1)} %param.8), channel_id=1, source_target_pairs={{0,8},{8,16},{16,24},{1,9},{9,17},{17,25},{2,10},{10,18},{18,26},{... | collective-permute-start | bytes 1179656 | tf_op jit(solution)/shard_map/ppermute | solution.py:214
  2.1 0.0 copy-done.6
  2.1 0.0 copy-done.5
  2.1 0.0 copy-start.1
  2.1 1.0 %copy-done.1 = bf16[1,128,1536]{2,1,0:T(8,128)(2,1)S(1)} copy-done((bf16[1,128,1536]{2,1,0:T(8,128)(2,1)S(1)}, bf16[1,128,1536]{2,1,0:T(8,128)(2,1)}, u32[]{:S(2)}) %copy-start.1) | copy-done | bytes 393240
  3.1 1.5 %bias_part.1 = (f32[8,8,1536]{2,1,0:T(8,128)}, bf16[128,1536]{1,0:T(8,128)(2,1)S(1)}) custom-call(s32[1,4]{1,0:T(1,128)S(1)} %copy-done.6, s32[1,128]{1,0:T(1,128)S(1)} %bitcast.4, bf16[1,128,1536]{2,1,0:T(8,128)(2,1)S(1)} %copy-done.1), custom_call_target="tpu_custom_call" | custom-call | tf_op jit(solution)/shard_map/bias_part/pallas_call | solution.py:22
  4.6 0.0 copy-start
  4.6 0.0 copy-start.3
  4.6 6.0 %all-to-all-start = ((f32[8,8,1536]{2,1,0:T(8,128)}), f32[8,8,1536]{2,1,0:T(8,128)S(1)}, u32[]{:S(2)}, u32[]{:S(2)}) async-start(f32[8,8,1536]{2,1,0:T(8,128)} %get-tuple-element.22), calls=%async_computation | async-start | bytes 786432 | tf_op jit(solution)/shard_map/all_to_all | solution.py:199
  10.6 0.0 copy-done
  10.6 0.0 copy-done.3
  10.6 0.3 gain_rows.1.gain_ref
  10.9 2.8 %collective-permute-done.recv_ref = bf16[1,128,1536]{2,1,0:T(8,128)(2,1)S(1)} collective-permute-done((bf16[1,128,1536]{2,1,0:T(8,128)(2,1)}, bf16[1,128,1536]{2,1,0:T(8,128)(2,1)S(1)}, u32[]{:S(2)}, u32[]{:S(2)}) %collective-permute-start) | collective-permute-done | bytes 393248 | tf_op jit(solution)/shard_map/ppermute | solution.py:214
  13.7 0.4 token_sums.1
  14.1 2.5 %psum.14 = f32[8,128]{1,0:T(8,128)S(1)} all-reduce(f32[8,128]{1,0:T(8,128)S(1)} %get-tuple-element.26), channel_id=1, replica_groups=mesh['far_dp'=2,'next'=2,'row'=4,'pipe'=4,'far'=4,'core'=2] {'core'}, use_global_device_ids=true, to_apply=%region_0.0 | all-reduce | flops 1024 | bytes 8192 | tf_op jit(solution)/shard_map/psum | solution.py:239
  16.6 21.3 %psum.15.sums_ref = f32[8,128]{1,0:T(8,128)S(1)} all-reduce(f32[8,128]{1,0:T(8,128)S(1)} %psum.14), channel_id=1, replica_groups=mesh['far_dp'=2,'next'=2,'row'=4,'pipe'=4,'far'=4,'core'=2] {'far'}, use_global_device_ids=true, to_apply=%region_1.0 | all-reduce | flops 1024 | bytes 8192 | tf_op jit(solution)/shard_map/psum | solution.py:239
  37.8 0.0 all-to-all-done.parts_ref
  37.8 1.2 %gain_part.1 = f32[8,8,1536]{2,1,0:T(8,128)} custom-call(s32[1,128]{1,0:T(1,128)S(1)} %bitcast.6, f32[8,128]{1,0:T(8,128)S(1)} %psum.15.sums_ref, bf16[128,1536]{1,0:T(8,128)(2,1)S(1)} %get-tuple-element.28.x_ref, bf16[128,1536]{1,0:T(8,128)(2,1)S(1)} %get-tuple-element.24.cot_ref), custom_call_target="tpu_custom_call" | custom-call | tf_op jit(solution)/shard_map/gain_part/pallas_call | solution.py:22
  39.0 0.0 copy-start.2
  39.1 5.0 %all-to-all-start.1 = ((f32[8,8,1536]{2,1,0:T(8,128)}), f32[8,8,1536]{2,1,0:T(8,128)S(1)}, u32[]{:S(2)}, u32[]{:S(2)}) async-start(f32[8,8,1536]{2,1,0:T(8,128)} %gain_part.1), calls=%async_computation.1 | async-start | bytes 786432 | tf_op jit(solution)/shard_map/all_to_all | solution.py:199
  44.1 0.0 copy-done.2
  44.1 1.0 %input_grad.1 = bf16[1,128,1536]{2,1,0:T(8,128)(2,1)S(1)} custom-call(s32[1,4]{1,0:T(1,128)S(1)} %copy-done.6, f32[8,128]{1,0:T(8,128)S(1)} %psum.15.sums_ref, bf16[128,1536]{1,0:T(8,128)(2,1)S(1)} %get-tuple-element.28.x_ref, bf16[128,1536]{1,0:T(8,128)(2,1)S(1)} %get-tuple-element.24.cot_ref, bf16[1,128,1536]{2,1,0:T(8,128)(2,1)S(1)} %copy-done.2, ...), custom_call_target="tpu_custom_call" | custom-call | tf_op jit(solution)/shard_map/input_grad/pallas_call | solution.py:22
  45.1 2.7 %collective-permute-start.3 = (bf16[1,128,1536]{2,1,0:T(8,128)(2,1)S(1)}, bf16[1,128,1536]{2,1,0:T(8,128)(2,1)S(1)}, u32[]{:S(2)}, u32[]{:S(2)}) collective-permute-start(bf16[1,128,1536]{2,1,0:T(8,128)(2,1)S(1)} %input_grad.1), channel_id=1, source_target_pairs={{0,24},{8,0},{16,8},{24,16},{1,25},{9,1},{17,9},{25,17},{2,26},{10... | collective-permute-start | bytes 1179656 | tf_op jit(solution)/shard_map/ppermute | solution.py:261
  47.9 4.0 %all-to-all-done.1.parts_ref = f32[8,8,1536]{2,1,0:T(8,128)S(1)} async-done(((f32[8,8,1536]{2,1,0:T(8,128)}), f32[8,8,1536]{2,1,0:T(8,128)S(1)}, u32[]{:S(2)}, u32[]{:S(2)}) %all-to-all-start.1) | async-done | bytes 393248 | tf_op jit(solution)/shard_map/all_to_all | solution.py:199
  51.9 3.4 %collective-permute-start.1 = (f32[8,1536]{1,0:T(8,128)S(1)}, f32[8,1536]{1,0:T(8,128)S(1)}, u32[]{:S(2)}, u32[]{:S(2)}) collective-permute-start(f32[8,1536]{1,0:T(8,128)S(1)} %gain_near.1.gain_ref), channel_id=1, source_target_pairs={{0,256},{256,0},{1,257},{257,1},{2,258},{258,2},{3,259},{259,3},{4... | collective-permute-start | bytes 147464 | tf_op jit(solution)/shard_map/ppermute | solution.py:203
  55.3 3.4 %collective-permute-start.2 = (f32[8,1536]{1,0:T(8,128)S(1)}, f32[8,1536]{1,0:T(8,128)S(1)}, u32[]{:S(2)}, u32[]{:S(2)}) collective-permute-start(f32[8,1536]{1,0:T(8,128)S(1)} %bias_near.1.bias_ref), channel_id=1, source_target_pairs={{0,256},{256,0},{1,257},{257,1},{2,258},{258,2},{3,259},{259,3},{4... | collective-permute-start | bytes 147464 | tf_op jit(solution)/shard_map/ppermute | solution.py:203
  58.6 0.7 collective-permute-done.1.gain_far_ref
  59.3 3.4 %collective-permute-done.2.bias_far_ref = f32[8,1536]{1,0:T(8,128)S(1)} collective-permute-done((f32[8,1536]{1,0:T(8,128)S(1)}, f32[8,1536]{1,0:T(8,128)S(1)}, u32[]{:S(2)}, u32[]{:S(2)}) %collective-permute-start.2) | collective-permute-done | bytes 49184 | tf_op jit(solution)/shard_map/ppermute | solution.py:203
  62.7 1.0 %add_parts.1 = f32[8,16,1536]{2,1,0:T(8,128)} custom-call(f32[8,1536]{1,0:T(8,128)S(1)} %gain_near.1.gain_ref, f32[8,1536]{1,0:T(8,128)S(1)} %collective-permute-done.1.gain_far_ref, f32[8,1536]{1,0:T(8,128)S(1)} %bias_near.1.bias_ref, f32[8,1536]{1,0:T(8,128)S(1)} %collective-permute-done.2.bias_far_ref), custom_call_target="tpu_custom_call" | custom-call | tf_op jit(solution)/shard_map/add_parts/pallas_call | solution.py:22
  63.7 3.6 %all-to-all-start.2 = ((f32[8,16,1536]{2,1,0:T(8,128)}), f32[8,16,1536]{2,1,0:T(8,128)S(1)}, u32[]{:S(2)}, u32[]{:S(2)}) async-start(f32[8,16,1536]{2,1,0:T(8,128)} %add_parts.1), calls=%async_computation.2 | async-start | bytes 1572864 | tf_op jit(solution)/shard_map/all_to_all | solution.py:199
  67.2 0.0 copy-start.4
  67.3 0.0 collective-permute-done.3.value_ref
  67.3 0.8 settle.1
  68.0 0.3 copy-done.4
  68.3 1.1 %normed.1 = bf16[1,128,1536]{2,1,0:T(8,128)(2,1)} custom-call(s32[1,128]{1,0:T(1,128)S(1)} %bitcast.7, f32[8,128]{1,0:T(8,128)S(1)} %psum.15.sums_ref, bf16[128,1536]{1,0:T(8,128)(2,1)S(1)} %get-tuple-element.28.x_ref, bf16[128,1536]{1,0:T(8,128)(2,1)S(1)} %gain_rows.1.gain_ref, bf16[1,64,1536]{2,1,0:T(8,128)(2,1)S(1)} %copy-done.4), custom_call_target="tpu_custom_call" | custom-call | tf_op jit(solution)/shard_map/normed/pallas_call | solution.py:22
  69.4 7.2 %all-to-all-done.2.parts_ref = f32[8,16,1536]{2,1,0:T(8,128)S(1)} async-done(((f32[8,16,1536]{2,1,0:T(8,128)}), f32[8,16,1536]{2,1,0:T(8,128)S(1)}, u32[]{:S(2)}, u32[]{:S(2)}) %all-to-all-start.2) | async-done | bytes 786464 | tf_op jit(solution)/shard_map/all_to_all | solution.py:199
  76.7 0.9 %whole_grads.1 = (f32[8,8,1536]{2,1,0:T(8,128)}, f32[8,8,1536]{2,1,0:T(8,128)}) custom-call(f32[8,16,1536]{2,1,0:T(8,128)S(1)} %all-to-all-done.2.parts_ref), custom_call_target="tpu_custom_call" | custom-call | tf_op jit(solution)/shard_map/whole_grads/pallas_call | solution.py:22
  (2 shorter events, 0.0 us)
Async XLA Ops:
  0.6 1.5 %copy-start.6 = (s32[1,4]{1,0:T(1,128)S(1)}, s32[1,4]{1,0:T(1,128)}, u32[]{:S(2)}) copy-start(s32[1,4]{1,0:T(1,128)} %order_ref.3) | copy-start | bytes 52
  0.6 1.5 %copy-start.5 = (s32[128]{0:T(128)S(1)}, s32[128]{0:T(128)}, u32[]{:S(2)}) copy-start(s32[128]{0:T(128)} %param.14) | copy-start | bytes 1540
  0.7 13.1 %collective-permute-start = (bf16[1,128,1536]{2,1,0:T(8,128)(2,1)}, bf16[1,128,1536]{2,1,0:T(8,128)(2,1)S(1)}, u32[]{:S(2)}, u32[]{:S(2)}) collective-permute-start(bf16[1,128,1536]{2,1,0:T(8,128)(2,1)} %param.8), channel_id=1, source_target_pairs={{0,8},{8,16},{16,24},{1,9},{9,17},{17,25},{2,10},{10,18},{18,26},{... | collective-permute-start | bytes 1179656 | tf_op jit(solution)/shard_map/ppermute | solution.py:214
  2.1 1.0 %copy-start.1 = (bf16[1,128,1536]{2,1,0:T(8,128)(2,1)S(1)}, bf16[1,128,1536]{2,1,0:T(8,128)(2,1)}, u32[]{:S(2)}) copy-start(bf16[1,128,1536]{2,1,0:T(8,128)(2,1)} %cot_ref.1) | copy-start | bytes 1179652
  4.6 6.0 %copy-start = (bf16[128,1536]{1,0:T(8,128)(2,1)S(1)}, bf16[128,1536]{1,0:T(8,128)(2,1)}, u32[]{:S(2)}) copy-start(bf16[128,1536]{1,0:T(8,128)(2,1)} %emb_ref.1) | copy-start | bytes 1179652
  4.6 6.0 %copy-start.3 = (bf16[1,64,1536]{2,1,0:T(8,128)(2,1)S(1)}, bf16[1,64,1536]{2,1,0:T(8,128)(2,1)}, u32[]{:S(2)}) copy-start(bf16[1,64,1536]{2,1,0:T(8,128)(2,1)} %table_ref.1) | copy-start | bytes 589828
  4.6 33.2 %all-to-all-start = ((f32[8,8,1536]{2,1,0:T(8,128)}), f32[8,8,1536]{2,1,0:T(8,128)S(1)}, u32[]{:S(2)}, u32[]{:S(2)}) async-start(f32[8,8,1536]{2,1,0:T(8,128)} %get-tuple-element.22), calls=%async_computation | async-start | bytes 786432 | tf_op jit(solution)/shard_map/all_to_all | solution.py:199
  39.0 5.1 %copy-start.2 = (bf16[1,128,1536]{2,1,0:T(8,128)(2,1)S(1)}, bf16[1,128,1536]{2,1,0:T(8,128)(2,1)}, u32[]{:S(2)}) copy-start(bf16[1,128,1536]{2,1,0:T(8,128)(2,1)} %res_ref.1) | copy-start | bytes 1179652
  39.1 12.8 %all-to-all-start.1 = ((f32[8,8,1536]{2,1,0:T(8,128)}), f32[8,8,1536]{2,1,0:T(8,128)S(1)}, u32[]{:S(2)}, u32[]{:S(2)}) async-start(f32[8,8,1536]{2,1,0:T(8,128)} %gain_part.1), calls=%async_computation.1 | async-start | bytes 786432 | tf_op jit(solution)/shard_map/all_to_all | solution.py:199
  45.1 22.1 %collective-permute-start.3 = (bf16[1,128,1536]{2,1,0:T(8,128)(2,1)S(1)}, bf16[1,128,1536]{2,1,0:T(8,128)(2,1)S(1)}, u32[]{:S(2)}, u32[]{:S(2)}) collective-permute-start(bf16[1,128,1536]{2,1,0:T(8,128)(2,1)S(1)} %input_grad.1), channel_id=1, source_target_pairs={{0,24},{8,0},{16,8},{24,16},{1,25},{9,1},{17,9},{25,17},{2,26},{10... | collective-permute-start | bytes 1179656 | tf_op jit(solution)/shard_map/ppermute | solution.py:261
  51.9 7.4 %collective-permute-start.1 = (f32[8,1536]{1,0:T(8,128)S(1)}, f32[8,1536]{1,0:T(8,128)S(1)}, u32[]{:S(2)}, u32[]{:S(2)}) collective-permute-start(f32[8,1536]{1,0:T(8,128)S(1)} %gain_near.1.gain_ref), channel_id=1, source_target_pairs={{0,256},{256,0},{1,257},{257,1},{2,258},{258,2},{3,259},{259,3},{4... | collective-permute-start | bytes 147464 | tf_op jit(solution)/shard_map/ppermute | solution.py:203
  55.3 7.4 %collective-permute-start.2 = (f32[8,1536]{1,0:T(8,128)S(1)}, f32[8,1536]{1,0:T(8,128)S(1)}, u32[]{:S(2)}, u32[]{:S(2)}) collective-permute-start(f32[8,1536]{1,0:T(8,128)S(1)} %bias_near.1.bias_ref), channel_id=1, source_target_pairs={{0,256},{256,0},{1,257},{257,1},{2,258},{258,2},{3,259},{259,3},{4... | collective-permute-start | bytes 147464 | tf_op jit(solution)/shard_map/ppermute | solution.py:203
  63.7 13.0 %all-to-all-start.2 = ((f32[8,16,1536]{2,1,0:T(8,128)}), f32[8,16,1536]{2,1,0:T(8,128)S(1)}, u32[]{:S(2)}, u32[]{:S(2)}) async-start(f32[8,16,1536]{2,1,0:T(8,128)} %add_parts.1), calls=%async_computation.2 | async-start | bytes 1572864 | tf_op jit(solution)/shard_map/all_to_all | solution.py:199
  67.2 1.1 %copy-start.4 = (bf16[1,64,1536]{2,1,0:T(8,128)(2,1)S(1)}, bf16[1,64,1536]{2,1,0:T(8,128)(2,1)}, u32[]{:S(2)}) copy-start(bf16[1,64,1536]{2,1,0:T(8,128)(2,1)} %bias_ref.1) | copy-start | bytes 589828

commit v12 on v9

--- a/solution.py
+++ b/solution.py
@@ -236,7 +236,7 @@
         first, received, embedded, cot, gain_rows,
         cover=10**11,
     )
-    sums = lax.psum(lax.psum(sums, "core"), "far")
+    sums = lax.psum(lax.psum(sums, "far"), "core")
     sums, bias_mine = lax.optimization_barrier((sums, bias_mine))
 
     gain_part = call(

time: 75.1 us -> 77.6 us (1.033); the launches traced: 74.6 us -> 76 us
  waiting for transfers between devices: 15.2 us -> 16.7 us
where the time goes in v12:
time: 77.6 us; the launch traced here: 76 us
  starting transfers between devices  25.6 us (33%)
  blocking collectives  23.7 us (31%)
  waiting for transfers between devices  16.7 us (22%)
  Pallas kernels  8.23 us (11%)
  local copies, waits for them, and re-layouts  1.01 us (1%)
  between operations  0.81 us (1%)
    psum x2, blocking collectives, local(): sums = lax.psum(lax.psum(sums, 'far'), 'core')  23.7 us
    all_to_all x3, starting transfers between devices, exchanged(): return lax.all_to_all(pieces, NEAR, 0, 0)  14.6 us
    all_to_all x3, waiting for transfers between devices, exchanged(): return lax.all_to_all(pieces, NEAR, 0, 0)  10.9 us
    pallas_call x11, Pallas kernels, call(): pl.pallas_call(kernel, name=name, out_shape=outs, in_specs=in_specs, out_...  8.23 us
    ppermute x2, starting transfers between devices, from_far(): return lax.ppermute(total, 'far_dp', [(0, 1), (1, 0)])  6.85 us
    ppermute x1, waiting for transfers between devices, local(): lax.ppermute(section_out, 'pipe', [(i, i + 1) for i in range(stages - 1)])  2.84 us
    ppermute x1, starting transfers between devices, local(): lax.ppermute(back, 'pipe', [(i, (i - 1) % stages) for i in range(stages)])  2.74 us
    ppermute x1, waiting for transfers between devices, local(): lax.ppermute(back, 'pipe', [(i, (i - 1) % stages) for i in range(stages)])  1.74 us
  transfers between devices with their start and end apart: 7, of which 5 were waited for; matrix products, arithmetic and copies ran while one was open for 0% of the time, Pallas kernels for 8%

profile of v12, /device:TPU:6, one launch (start us, length us, event | category | flops | bytes accessed | tf_op | source)
XLA Modules:
  0.0 76.0 jit_solution(10675887846854845807)
XLA Ops:
  0.6 0.0 copy-start.6
  0.6 0.0 copy-start.5
  0.7 1.4 %collective-permute-start = (bf16[1,128,1536]{2,1,0:T(8,128)(2,1)}, bf16[1,128,1536]{2,1,0:T(8,128)(2,1)S(1)}, u32[]{:S(2)}, u32[]{:S(2)}) collective-permute-start(bf16[1,128,1536]{2,1,0:T(8,128)(2,1)} %param.8), channel_id=1, source_target_pairs={{0,8},{8,16},{16,24},{1,9},{9,17},{17,25},{2,10},{10,18},{18,26},{... | collective-permute-start | bytes 1179656 | tf_op jit(solution)/shard_map/ppermute | solution.py:214
  2.1 0.0 copy-done.6
  2.1 0.0 copy-done.5
  2.1 0.0 copy-start.1
  2.1 1.0 %copy-done.1 = bf16[1,128,1536]{2,1,0:T(8,128)(2,1)S(1)} copy-done((bf16[1,128,1536]{2,1,0:T(8,128)(2,1)S(1)}, bf16[1,128,1536]{2,1,0:T(8,128)(2,1)}, u32[]{:S(2)}) %copy-start.1) | copy-done | bytes 393240
  3.1 1.5 %bias_part.1 = (f32[8,8,1536]{2,1,0:T(8,128)}, bf16[128,1536]{1,0:T(8,128)(2,1)S(1)}) custom-call(s32[1,4]{1,0:T(1,128)S(1)} %copy-done.6, s32[1,128]{1,0:T(1,128)S(1)} %bitcast.4, bf16[1,128,1536]{2,1,0:T(8,128)(2,1)S(1)} %copy-done.1), custom_call_target="tpu_custom_call" | custom-call | tf_op jit(solution)/shard_map/bias_part/pallas_call | solution.py:22
  4.6 0.0 copy-start
  4.6 0.0 copy-start.3
  4.6 6.0 %all-to-all-start = ((f32[8,8,1536]{2,1,0:T(8,128)}), f32[8,8,1536]{2,1,0:T(8,128)S(1)}, u32[]{:S(2)}, u32[]{:S(2)}) async-start(f32[8,8,1536]{2,1,0:T(8,128)} %get-tuple-element.23), calls=%async_computation | async-start | bytes 786432 | tf_op jit(solution)/shard_map/all_to_all | solution.py:199
  10.6 0.0 copy-done
  10.6 0.0 copy-done.3
  10.6 0.3 gain_rows.1.gain_ref
  10.9 2.8 %collective-permute-done.recv_ref = bf16[1,128,1536]{2,1,0:T(8,128)(2,1)S(1)} collective-permute-done((bf16[1,128,1536]{2,1,0:T(8,128)(2,1)}, bf16[1,128,1536]{2,1,0:T(8,128)(2,1)S(1)}, u32[]{:S(2)}, u32[]{:S(2)}) %collective-permute-start) | collective-permute-done | bytes 393248 | tf_op jit(solution)/shard_map/ppermute | solution.py:214
  13.7 0.4 token_sums.1
  14.1 21.2 %psum.14 = f32[8,128]{1,0:T(8,128)S(1)} all-reduce(f32[8,128]{1,0:T(8,128)S(1)} %get-tuple-element.27), channel_id=1, replica_groups=mesh['far_dp'=2,'next'=2,'row'=4,'pipe'=4,'far'=4,'core'=2] {'far'}, use_global_device_ids=true, to_apply=%region_0.0 | all-reduce | flops 1024 | bytes 8192 | tf_op jit(solution)/shard_map/psum | solution.py:239
  35.4 2.5 %psum.15.sums_ref = f32[8,128]{1,0:T(8,128)S(1)} all-reduce(f32[8,128]{1,0:T(8,128)S(1)} %psum.14), channel_id=1, replica_groups=mesh['far_dp'=2,'next'=2,'row'=4,'pipe'=4,'far'=4,'core'=2] {'core'}, use_global_device_ids=true, to_apply=%region_1.0 | all-reduce | flops 1024 | bytes 8192 | tf_op jit(solution)/shard_map/psum | solution.py:239
  37.8 0.0 all-to-all-done.parts_ref
  37.8 1.2 %gain_part.1 = f32[8,8,1536]{2,1,0:T(8,128)} custom-call(s32[1,128]{1,0:T(1,128)S(1)} %bitcast.6, f32[8,128]{1,0:T(8,128)S(1)} %psum.15.sums_ref, bf16[128,1536]{1,0:T(8,128)(2,1)S(1)} %get-tuple-element.29.x_ref, bf16[128,1536]{1,0:T(8,128)(2,1)S(1)} %get-tuple-element.25.cot_ref), custom_call_target="tpu_custom_call" | custom-call | tf_op jit(solution)/shard_map/gain_part/pallas_call | solution.py:22
  39.0 4.9 %all-to-all-start.1 = ((f32[8,8,1536]{2,1,0:T(8,128)}), f32[8,8,1536]{2,1,0:T(8,128)S(1)}, u32[]{:S(2)}, u32[]{:S(2)}) async-start(f32[8,8,1536]{2,1,0:T(8,128)} %gain_part.1), calls=%async_computation.1 | async-start | bytes 786432 | tf_op jit(solution)/shard_map/all_to_all | solution.py:199
  44.0 0.0 copy-start.2
  44.0 3.5 %collective-permute-start.2 = (f32[8,1536]{1,0:T(8,128)S(1)}, f32[8,1536]{1,0:T(8,128)S(1)}, u32[]{:S(2)}, u32[]{:S(2)}) collective-permute-start(f32[8,1536]{1,0:T(8,128)S(1)} %bias_near.1.bias_ref), channel_id=1, source_target_pairs={{0,256},{256,0},{1,257},{257,1},{2,258},{258,2},{3,259},{259,3},{4... | collective-permute-start | bytes 147464 | tf_op jit(solution)/shard_map/ppermute | solution.py:203
  47.5 0.0 copy-done.2
  47.5 1.0 %input_grad.1 = bf16[1,128,1536]{2,1,0:T(8,128)(2,1)S(1)} custom-call(s32[1,4]{1,0:T(1,128)S(1)} %copy-done.6, f32[8,128]{1,0:T(8,128)S(1)} %psum.15.sums_ref, bf16[128,1536]{1,0:T(8,128)(2,1)S(1)} %get-tuple-element.29.x_ref, bf16[128,1536]{1,0:T(8,128)(2,1)S(1)} %get-tuple-element.25.cot_ref, bf16[1,128,1536]{2,1,0:T(8,128)(2,1)S(1)} %copy-done.2, ...), custom_call_target="tpu_custom_call" | custom-call | tf_op jit(solution)/shard_map/input_grad/pallas_call | solution.py:22
  48.6 4.5 %all-to-all-done.1.parts_ref = f32[8,8,1536]{2,1,0:T(8,128)S(1)} async-done(((f32[8,8,1536]{2,1,0:T(8,128)}), f32[8,8,1536]{2,1,0:T(8,128)S(1)}, u32[]{:S(2)}, u32[]{:S(2)}) %all-to-all-start.1) | async-done | bytes 393248 | tf_op jit(solution)/shard_map/all_to_all | solution.py:199
  53.1 3.3 %collective-permute-start.1 = (f32[8,1536]{1,0:T(8,128)S(1)}, f32[8,1536]{1,0:T(8,128)S(1)}, u32[]{:S(2)}, u32[]{:S(2)}) collective-permute-start(f32[8,1536]{1,0:T(8,128)S(1)} %gain_near.1.gain_ref), channel_id=1, source_target_pairs={{0,256},{256,0},{1,257},{257,1},{2,258},{258,2},{3,259},{259,3},{4... | collective-permute-start | bytes 147464 | tf_op jit(solution)/shard_map/ppermute | solution.py:203
  56.4 2.7 %collective-permute-start.3 = (bf16[1,128,1536]{2,1,0:T(8,128)(2,1)S(1)}, bf16[1,128,1536]{2,1,0:T(8,128)(2,1)S(1)}, u32[]{:S(2)}, u32[]{:S(2)}) collective-permute-start(bf16[1,128,1536]{2,1,0:T(8,128)(2,1)S(1)} %input_grad.1), channel_id=1, source_target_pairs={{0,24},{8,0},{16,8},{24,16},{1,25},{9,1},{17,9},{25,17},{2,26},{10... | collective-permute-start | bytes 1179656 | tf_op jit(solution)/shard_map/ppermute | solution.py:266
  59.2 0.0 collective-permute-done.2.bias_far_ref
  59.2 1.2 %collective-permute-done.1.gain_far_ref = f32[8,1536]{1,0:T(8,128)S(1)} collective-permute-done((f32[8,1536]{1,0:T(8,128)S(1)}, f32[8,1536]{1,0:T(8,128)S(1)}, u32[]{:S(2)}, u32[]{:S(2)}) %collective-permute-start.1) | collective-permute-done | bytes 49184 | tf_op jit(solution)/shard_map/ppermute | solution.py:203
  60.4 1.0 %add_parts.1 = f32[8,16,1536]{2,1,0:T(8,128)} custom-call(f32[8,1536]{1,0:T(8,128)S(1)} %gain_near.1.gain_ref, f32[8,1536]{1,0:T(8,128)S(1)} %collective-permute-done.1.gain_far_ref, f32[8,1536]{1,0:T(8,128)S(1)} %bias_near.1.bias_ref, f32[8,1536]{1,0:T(8,128)S(1)} %collective-permute-done.2.bias_far_ref), custom_call_target="tpu_custom_call" | custom-call | flops 99999997952 | tf_op jit(solution)/shard_map/add_parts/pallas_call | solution.py:22
  61.4 0.0 copy-start.4
  61.4 3.7 %all-to-all-start.2 = ((f32[8,16,1536]{2,1,0:T(8,128)}), f32[8,16,1536]{2,1,0:T(8,128)S(1)}, u32[]{:S(2)}, u32[]{:S(2)}) async-start(f32[8,16,1536]{2,1,0:T(8,128)} %add_parts.1), calls=%async_computation.2 | async-start | bytes 1572864 | tf_op jit(solution)/shard_map/all_to_all | solution.py:199
  65.1 0.0 copy-done.4
  65.1 1.1 %normed.1 = bf16[1,128,1536]{2,1,0:T(8,128)(2,1)} custom-call(s32[1,128]{1,0:T(1,128)S(1)} %bitcast.7, f32[8,128]{1,0:T(8,128)S(1)} %psum.15.sums_ref, bf16[128,1536]{1,0:T(8,128)(2,1)S(1)} %get-tuple-element.29.x_ref, bf16[128,1536]{1,0:T(8,128)(2,1)S(1)} %gain_rows.1.gain_ref, bf16[1,64,1536]{2,1,0:T(8,128)(2,1)S(1)} %copy-done.4), custom_call_target="tpu_custom_call" | custom-call | tf_op jit(solution)/shard_map/normed/pallas_call | solution.py:22
  66.3 1.7 %collective-permute-done.3.value_ref = bf16[1,128,1536]{2,1,0:T(8,128)(2,1)S(1)} collective-permute-done((bf16[1,128,1536]{2,1,0:T(8,128)(2,1)S(1)}, bf16[1,128,1536]{2,1,0:T(8,128)(2,1)S(1)}, u32[]{:S(2)}, u32[]{:S(2)}) %collective-permute-start.3) | collective-permute-done | bytes 393248 | tf_op jit(solution)/shard_map/ppermute | solution.py:266
  68.0 0.8 settle.1
  68.8 6.4 %all-to-all-done.2.parts_ref = f32[8,16,1536]{2,1,0:T(8,128)S(1)} async-done(((f32[8,16,1536]{2,1,0:T(8,128)}), f32[8,16,1536]{2,1,0:T(8,128)S(1)}, u32[]{:S(2)}, u32[]{:S(2)}) %all-to-all-start.2) | async-done | bytes 786464 | tf_op jit(solution)/shard_map/all_to_all | solution.py:199
  75.1 0.9 %whole_grads.1 = (f32[8,8,1536]{2,1,0:T(8,128)}, f32[8,8,1536]{2,1,0:T(8,128)}) custom-call(f32[8,16,1536]{2,1,0:T(8,128)S(1)} %all-to-all-done.2.parts_ref), custom_call_target="tpu_custom_call" | custom-call | tf_op jit(solution)/shard_map/whole_grads/pallas_call | solution.py:22
  (2 shorter events, 0.0 us)
Async XLA Ops:
  0.6 1.5 %copy-start.6 = (s32[1,4]{1,0:T(1,128)S(1)}, s32[1,4]{1,0:T(1,128)}, u32[]{:S(2)}) copy-start(s32[1,4]{1,0:T(1,128)} %order_ref.3) | copy-start | bytes 52
  0.6 1.5 %copy-start.5 = (s32[128]{0:T(128)S(1)}, s32[128]{0:T(128)}, u32[]{:S(2)}) copy-start(s32[128]{0:T(128)} %param.14) | copy-start | bytes 1540
  0.7 13.1 %collective-permute-start = (bf16[1,128,1536]{2,1,0:T(8,128)(2,1)}, bf16[1,128,1536]{2,1,0:T(8,128)(2,1)S(1)}, u32[]{:S(2)}, u32[]{:S(2)}) collective-permute-start(bf16[1,128,1536]{2,1,0:T(8,128)(2,1)} %param.8), channel_id=1, source_target_pairs={{0,8},{8,16},{16,24},{1,9},{9,17},{17,25},{2,10},{10,18},{18,26},{... | collective-permute-start | bytes 1179656 | tf_op jit(solution)/shard_map/ppermute | solution.py:214
  2.1 1.0 %copy-start.1 = (bf16[1,128,1536]{2,1,0:T(8,128)(2,1)S(1)}, bf16[1,128,1536]{2,1,0:T(8,128)(2,1)}, u32[]{:S(2)}) copy-start(bf16[1,128,1536]{2,1,0:T(8,128)(2,1)} %cot_ref.1) | copy-start | bytes 1179652
  4.6 6.0 %copy-start = (bf16[128,1536]{1,0:T(8,128)(2,1)S(1)}, bf16[128,1536]{1,0:T(8,128)(2,1)}, u32[]{:S(2)}) copy-start(bf16[128,1536]{1,0:T(8,128)(2,1)} %emb_ref.1) | copy-start | bytes 1179652
  4.6 6.0 %copy-start.3 = (bf16[1,64,1536]{2,1,0:T(8,128)(2,1)S(1)}, bf16[1,64,1536]{2,1,0:T(8,128)(2,1)}, u32[]{:S(2)}) copy-start(bf16[1,64,1536]{2,1,0:T(8,128)(2,1)} %table_ref.1) | copy-start | bytes 589828
  4.6 33.2 %all-to-all-start = ((f32[8,8,1536]{2,1,0:T(8,128)}), f32[8,8,1536]{2,1,0:T(8,128)S(1)}, u32[]{:S(2)}, u32[]{:S(2)}) async-start(f32[8,8,1536]{2,1,0:T(8,128)} %get-tuple-element.23), calls=%async_computation | async-start | bytes 786432 | tf_op jit(solution)/shard_map/all_to_all | solution.py:199
  39.0 14.0 %all-to-all-start.1 = ((f32[8,8,1536]{2,1,0:T(8,128)}), f32[8,8,1536]{2,1,0:T(8,128)S(1)}, u32[]{:S(2)}, u32[]{:S(2)}) async-start(f32[8,8,1536]{2,1,0:T(8,128)} %gain_part.1), calls=%async_computation.1 | async-start | bytes 786432 | tf_op jit(solution)/shard_map/all_to_all | solution.py:199
  44.0 3.6 %copy-start.2 = (bf16[1,128,1536]{2,1,0:T(8,128)(2,1)S(1)}, bf16[1,128,1536]{2,1,0:T(8,128)(2,1)}, u32[]{:S(2)}) copy-start(bf16[1,128,1536]{2,1,0:T(8,128)(2,1)} %res_ref.1) | copy-start | bytes 1179652
  44.0 15.2 %collective-permute-start.2 = (f32[8,1536]{1,0:T(8,128)S(1)}, f32[8,1536]{1,0:T(8,128)S(1)}, u32[]{:S(2)}, u32[]{:S(2)}) collective-permute-start(f32[8,1536]{1,0:T(8,128)S(1)} %bias_near.1.bias_ref), channel_id=1, source_target_pairs={{0,256},{256,0},{1,257},{257,1},{2,258},{258,2},{3,259},{259,3},{4... | collective-permute-start | bytes 147464 | tf_op jit(solution)/shard_map/ppermute | solution.py:203
  53.1 7.3 %collective-permute-start.1 = (f32[8,1536]{1,0:T(8,128)S(1)}, f32[8,1536]{1,0:T(8,128)S(1)}, u32[]{:S(2)}, u32[]{:S(2)}) collective-permute-start(f32[8,1536]{1,0:T(8,128)S(1)} %gain_near.1.gain_ref), channel_id=1, source_target_pairs={{0,256},{256,0},{1,257},{257,1},{2,258},{258,2},{3,259},{259,3},{4... | collective-permute-start | bytes 147464 | tf_op jit(solution)/shard_map/ppermute | solution.py:203
  56.4 11.6 %collective-permute-start.3 = (bf16[1,128,1536]{2,1,0:T(8,128)(2,1)S(1)}, bf16[1,128,1536]{2,1,0:T(8,128)(2,1)S(1)}, u32[]{:S(2)}, u32[]{:S(2)}) collective-permute-start(bf16[1,128,1536]{2,1,0:T(8,128)(2,1)S(1)} %input_grad.1), channel_id=1, source_target_pairs={{0,24},{8,0},{16,8},{24,16},{1,25},{9,1},{17,9},{25,17},{2,26},{10... | collective-permute-start | bytes 1179656 | tf_op jit(solution)/shard_map/ppermute | solution.py:266
  61.4 3.7 %copy-start.4 = (bf16[1,64,1536]{2,1,0:T(8,128)(2,1)S(1)}, bf16[1,64,1536]{2,1,0:T(8,128)(2,1)}, u32[]{:S(2)}) copy-start(bf16[1,64,1536]{2,1,0:T(8,128)(2,1)} %bias_ref.1) | copy-start | bytes 589828
  61.4 13.7 %all-to-all-start.2 = ((f32[8,16,1536]{2,1,0:T(8,128)}), f32[8,16,1536]{2,1,0:T(8,128)S(1)}, u32[]{:S(2)}, u32[]{:S(2)}) async-start(f32[8,16,1536]{2,1,0:T(8,128)} %add_parts.1), calls=%async_computation.2 | async-start | bytes 1572864 | tf_op jit(solution)/shard_map/all_to_all | solution.py:199

commit v13 on v9

--- a/solution.py
+++ b/solution.py
@@ -251,6 +251,10 @@
     gain_mine = exchanged(gain_part)
     bias_near = call(total_kernel, "bias_near", shape(pieces[1:], f32), [], [VMEM], bias_mine)
     bias_far = from_far(bias_near)
+    gain_mine, bias_near = lax.optimization_barrier((gain_mine, bias_near))
+    gain_near = call(total_kernel, "gain_near", shape(pieces[1:], f32), [], [VMEM], gain_mine)
+    gain_far = from_far(gain_near)
+    gain_near, sums = lax.optimization_barrier((gain_near, sums))
     back = call(
         grad_kernel,
         "input_grad",
@@ -259,10 +263,6 @@
         [SMEM, VMEM, VMEM, VMEM, VMEM, VMEM],
         mb_order, sums, x, cot, cot_res, gain_rows,
     )
-    gain_mine, back, bias_near = lax.optimization_barrier((gain_mine, back, bias_near))
-    gain_near = call(total_kernel, "gain_near", shape(pieces[1:], f32), [], [VMEM], gain_mine)
-    gain_far = from_far(gain_near)
-    gain_near, back = lax.optimization_barrier((gain_near, back))
     returned = lax.ppermute(back, "pipe", [(i, (i - 1) % stages) for i in range(stages)])
     both = (2 * pieces[1], width)
     total = call(

time: 75.1 us -> 76.1 us (1.013); the launches traced: 74.6 us -> 74.6 us
    ppermute x2, waiting for transfers between devices: 1.28 us -> 0.26 us  [from_far(): return lax.ppermute(total, 'far_dp', [(0, 1), (1, 0)])]
    ppermute x1, waiting for transfers between devices: 1 us -> 2.02 us  [local(): lax.ppermute(back, 'pipe', [(i, (i - 1) % stages) for i in range(stages)])]
where the time goes in v13:
time: 76.1 us; the launch traced here: 74.6 us
  starting transfers between devices  25.6 us (34%)
  blocking collectives  23.7 us (31%)
  waiting for transfers between devices  15.2 us (20%)
  Pallas kernels  8.22 us (11%)
  local copies, waits for them, and re-layouts  1.01 us (1%)
  between operations  0.81 us (1%)
    psum x2, blocking collectives, local(): sums = lax.psum(lax.psum(sums, 'core'), 'far')  23.7 us
    all_to_all x3, starting transfers between devices, exchanged(): return lax.all_to_all(pieces, NEAR, 0, 0)  14.6 us
    all_to_all x3, waiting for transfers between devices, exchanged(): return lax.all_to_all(pieces, NEAR, 0, 0)  10.1 us
    pallas_call x11, Pallas kernels, call(): pl.pallas_call(kernel, name=name, out_shape=outs, in_specs=in_specs, out_...  8.22 us
    ppermute x2, starting transfers between devices, from_far(): return lax.ppermute(total, 'far_dp', [(0, 1), (1, 0)])  6.89 us
    ppermute x1, waiting for transfers between devices, local(): lax.ppermute(section_out, 'pipe', [(i, i + 1) for i in range(stages - 1)])  2.84 us
    ppermute x1, starting transfers between devices, local(): lax.ppermute(back, 'pipe', [(i, (i - 1) % stages) for i in range(stages)])  2.73 us
    ppermute x1, waiting for transfers between devices, local(): lax.ppermute(back, 'pipe', [(i, (i - 1) % stages) for i in range(stages)])  2.02 us
  transfers between devices with their start and end apart: 7, of which 5 were waited for; matrix products, arithmetic and copies ran while one was open for 0% of the time, Pallas kernels for 8%

profile of v13, /device:TPU:6, one launch (start us, length us, event | category | flops | bytes accessed | tf_op | source)
XLA Modules:
  0.0 74.6 jit_solution(13904008434599356019)
XLA Ops:
  0.6 0.0 copy-start.6
  0.6 0.0 copy-start.5
  0.7 1.4 %collective-permute-start = (bf16[1,128,1536]{2,1,0:T(8,128)(2,1)}, bf16[1,128,1536]{2,1,0:T(8,128)(2,1)S(1)}, u32[]{:S(2)}, u32[]{:S(2)}) collective-permute-start(bf16[1,128,1536]{2,1,0:T(8,128)(2,1)} %param.8), channel_id=1, source_target_pairs={{0,8},{8,16},{16,24},{1,9},{9,17},{17,25},{2,10},{10,18},{18,26},{... | collective-permute-start | bytes 1179656 | tf_op jit(solution)/shard_map/ppermute | solution.py:214
  2.1 0.0 copy-done.6
  2.1 0.0 copy-done.5
  2.1 0.0 copy-start.1
  2.1 1.0 %copy-done.1 = bf16[1,128,1536]{2,1,0:T(8,128)(2,1)S(1)} copy-done((bf16[1,128,1536]{2,1,0:T(8,128)(2,1)S(1)}, bf16[1,128,1536]{2,1,0:T(8,128)(2,1)}, u32[]{:S(2)}) %copy-start.1) | copy-done | bytes 393240
  3.1 1.5 %bias_part.1 = (f32[8,8,1536]{2,1,0:T(8,128)}, bf16[128,1536]{1,0:T(8,128)(2,1)S(1)}) custom-call(s32[1,4]{1,0:T(1,128)S(1)} %copy-done.6, s32[1,128]{1,0:T(1,128)S(1)} %bitcast.4, bf16[1,128,1536]{2,1,0:T(8,128)(2,1)S(1)} %copy-done.1), custom_call_target="tpu_custom_call" | custom-call | tf_op jit(solution)/shard_map/bias_part/pallas_call | solution.py:22
  4.6 0.0 copy-start
  4.6 0.0 copy-start.3
  4.6 6.0 %all-to-all-start = ((f32[8,8,1536]{2,1,0:T(8,128)}), f32[8,8,1536]{2,1,0:T(8,128)S(1)}, u32[]{:S(2)}, u32[]{:S(2)}) async-start(f32[8,8,1536]{2,1,0:T(8,128)} %get-tuple-element.22), calls=%async_computation | async-start | bytes 786432 | tf_op jit(solution)/shard_map/all_to_all | solution.py:199
  10.6 0.0 copy-done
  10.6 0.0 copy-done.3
  10.6 0.3 gain_rows.1.gain_ref
  10.9 2.8 %collective-permute-done.recv_ref = bf16[1,128,1536]{2,1,0:T(8,128)(2,1)S(1)} collective-permute-done((bf16[1,128,1536]{2,1,0:T(8,128)(2,1)}, bf16[1,128,1536]{2,1,0:T(8,128)(2,1)S(1)}, u32[]{:S(2)}, u32[]{:S(2)}) %collective-permute-start) | collective-permute-done | bytes 393248 | tf_op jit(solution)/shard_map/ppermute | solution.py:214
  13.7 0.4 token_sums.1
  14.1 2.5 %psum.14 = f32[8,128]{1,0:T(8,128)S(1)} all-reduce(f32[8,128]{1,0:T(8,128)S(1)} %get-tuple-element.26), channel_id=1, replica_groups=mesh['far_dp'=2,'next'=2,'row'=4,'pipe'=4,'far'=4,'core'=2] {'core'}, use_global_device_ids=true, to_apply=%region_0.0 | all-reduce | flops 1024 | bytes 8192 | tf_op jit(solution)/shard_map/psum | solution.py:239
  16.6 21.3 %psum.15.sums_ref = f32[8,128]{1,0:T(8,128)S(1)} all-reduce(f32[8,128]{1,0:T(8,128)S(1)} %psum.14), channel_id=1, replica_groups=mesh['far_dp'=2,'next'=2,'row'=4,'pipe'=4,'far'=4,'core'=2] {'far'}, use_global_device_ids=true, to_apply=%region_1.0 | all-reduce | flops 1024 | bytes 8192 | tf_op jit(solution)/shard_map/psum | solution.py:239
  37.8 0.0 all-to-all-done.parts_ref
  37.8 1.2 %gain_part.1 = f32[8,8,1536]{2,1,0:T(8,128)} custom-call(s32[1,128]{1,0:T(1,128)S(1)} %bitcast.6, f32[8,128]{1,0:T(8,128)S(1)} %psum.15.sums_ref, bf16[128,1536]{1,0:T(8,128)(2,1)S(1)} %get-tuple-element.28.x_ref, bf16[128,1536]{1,0:T(8,128)(2,1)S(1)} %get-tuple-element.24.cot_ref), custom_call_target="tpu_custom_call" | custom-call | tf_op jit(solution)/shard_map/gain_part/pallas_call | solution.py:22
  39.0 4.9 %all-to-all-start.1 = ((f32[8,8,1536]{2,1,0:T(8,128)}), f32[8,8,1536]{2,1,0:T(8,128)S(1)}, u32[]{:S(2)}, u32[]{:S(2)}) async-start(f32[8,8,1536]{2,1,0:T(8,128)} %gain_part.1), calls=%async_computation.1 | async-start | bytes 786432 | tf_op jit(solution)/shard_map/all_to_all | solution.py:199
  44.0 0.0 copy-start.2
  44.0 3.5 %collective-permute-start.2 = (f32[8,1536]{1,0:T(8,128)S(1)}, f32[8,1536]{1,0:T(8,128)S(1)}, u32[]{:S(2)}, u32[]{:S(2)}) collective-permute-start(f32[8,1536]{1,0:T(8,128)S(1)} %bias_near.1.bias_ref), channel_id=1, source_target_pairs={{0,256},{256,0},{1,257},{257,1},{2,258},{258,2},{3,259},{259,3},{4... | collective-permute-start | bytes 147464 | tf_op jit(solution)/shard_map/ppermute | solution.py:203
  47.5 4.6 %all-to-all-done.1.parts_ref = f32[8,8,1536]{2,1,0:T(8,128)S(1)} async-done(((f32[8,8,1536]{2,1,0:T(8,128)}), f32[8,8,1536]{2,1,0:T(8,128)S(1)}, u32[]{:S(2)}, u32[]{:S(2)}) %all-to-all-start.1) | async-done | bytes 393248 | tf_op jit(solution)/shard_map/all_to_all | solution.py:199
  52.2 3.4 %collective-permute-start.1 = (f32[8,1536]{1,0:T(8,128)S(1)}, f32[8,1536]{1,0:T(8,128)S(1)}, u32[]{:S(2)}, u32[]{:S(2)}) collective-permute-start(f32[8,1536]{1,0:T(8,128)S(1)} %gain_near.1.gain_ref), channel_id=1, source_target_pairs={{0,256},{256,0},{1,257},{257,1},{2,258},{258,2},{3,259},{259,3},{4... | collective-permute-start | bytes 147464 | tf_op jit(solution)/shard_map/ppermute | solution.py:203
  55.6 0.0 copy-done.2
  55.6 1.0 %input_grad.1 = bf16[1,128,1536]{2,1,0:T(8,128)(2,1)S(1)} custom-call(s32[1,4]{1,0:T(1,128)S(1)} %copy-done.6, f32[8,128]{1,0:T(8,128)S(1)} %psum.15.sums_ref, bf16[128,1536]{1,0:T(8,128)(2,1)S(1)} %get-tuple-element.28.x_ref, bf16[128,1536]{1,0:T(8,128)(2,1)S(1)} %get-tuple-element.24.cot_ref, bf16[1,128,1536]{2,1,0:T(8,128)(2,1)S(1)} %copy-done.2, ...), custom_call_target="tpu_custom_call" | custom-call | tf_op jit(solution)/shard_map/input_grad/pallas_call | solution.py:22
  56.6 2.7 %collective-permute-start.3 = (bf16[1,128,1536]{2,1,0:T(8,128)(2,1)S(1)}, bf16[1,128,1536]{2,1,0:T(8,128)(2,1)S(1)}, u32[]{:S(2)}, u32[]{:S(2)}) collective-permute-start(bf16[1,128,1536]{2,1,0:T(8,128)(2,1)S(1)} %input_grad.1), channel_id=1, source_target_pairs={{0,24},{8,0},{16,8},{24,16},{1,25},{9,1},{17,9},{25,17},{2,26},{10... | collective-permute-start | bytes 1179656 | tf_op jit(solution)/shard_map/ppermute | solution.py:266
  59.3 0.0 collective-permute-done.2.bias_far_ref
  59.3 0.3 collective-permute-done.1.gain_far_ref
  59.6 1.0 %add_parts.1 = f32[8,16,1536]{2,1,0:T(8,128)} custom-call(f32[8,1536]{1,0:T(8,128)S(1)} %gain_near.1.gain_ref, f32[8,1536]{1,0:T(8,128)S(1)} %collective-permute-done.1.gain_far_ref, f32[8,1536]{1,0:T(8,128)S(1)} %bias_near.1.bias_ref, f32[8,1536]{1,0:T(8,128)S(1)} %collective-permute-done.2.bias_far_ref), custom_call_target="tpu_custom_call" | custom-call | flops 99999997952 | tf_op jit(solution)/shard_map/add_parts/pallas_call | solution.py:22
  60.6 0.0 copy-start.4
  60.6 3.7 %all-to-all-start.2 = ((f32[8,16,1536]{2,1,0:T(8,128)}), f32[8,16,1536]{2,1,0:T(8,128)S(1)}, u32[]{:S(2)}, u32[]{:S(2)}) async-start(f32[8,16,1536]{2,1,0:T(8,128)} %add_parts.1), calls=%async_computation.2 | async-start | bytes 1572864 | tf_op jit(solution)/shard_map/all_to_all | solution.py:199
  64.3 0.0 copy-done.4
  64.3 1.1 %normed.1 = bf16[1,128,1536]{2,1,0:T(8,128)(2,1)} custom-call(s32[1,128]{1,0:T(1,128)S(1)} %bitcast.7, f32[8,128]{1,0:T(8,128)S(1)} %psum.15.sums_ref, bf16[128,1536]{1,0:T(8,128)(2,1)S(1)} %get-tuple-element.28.x_ref, bf16[128,1536]{1,0:T(8,128)(2,1)S(1)} %gain_rows.1.gain_ref, bf16[1,64,1536]{2,1,0:T(8,128)(2,1)S(1)} %copy-done.4), custom_call_target="tpu_custom_call" | custom-call | tf_op jit(solution)/shard_map/normed/pallas_call | solution.py:22
  65.5 2.0 %collective-permute-done.3.value_ref = bf16[1,128,1536]{2,1,0:T(8,128)(2,1)S(1)} collective-permute-done((bf16[1,128,1536]{2,1,0:T(8,128)(2,1)S(1)}, bf16[1,128,1536]{2,1,0:T(8,128)(2,1)S(1)}, u32[]{:S(2)}, u32[]{:S(2)}) %collective-permute-start.3) | collective-permute-done | bytes 393248 | tf_op jit(solution)/shard_map/ppermute | solution.py:266
  67.5 0.8 %settle.1 = bf16[1,128,1536]{2,1,0:T(8,128)(2,1)} custom-call(bf16[1,128,1536]{2,1,0:T(8,128)(2,1)S(1)} %collective-permute-done.3.value_ref), custom_call_target="tpu_custom_call" | custom-call | flops 99999997952 | tf_op jit(solution)/shard_map/settle/pallas_call | solution.py:22
  68.2 5.5 %all-to-all-done.2.parts_ref = f32[8,16,1536]{2,1,0:T(8,128)S(1)} async-done(((f32[8,16,1536]{2,1,0:T(8,128)}), f32[8,16,1536]{2,1,0:T(8,128)S(1)}, u32[]{:S(2)}, u32[]{:S(2)}) %all-to-all-start.2) | async-done | bytes 786464 | tf_op jit(solution)/shard_map/all_to_all | solution.py:199
  73.7 0.9 %whole_grads.1 = (f32[8,8,1536]{2,1,0:T(8,128)}, f32[8,8,1536]{2,1,0:T(8,128)}) custom-call(f32[8,16,1536]{2,1,0:T(8,128)S(1)} %all-to-all-done.2.parts_ref), custom_call_target="tpu_custom_call" | custom-call | tf_op jit(solution)/shard_map/whole_grads/pallas_call | solution.py:22
  (2 shorter events, 0.0 us)
Async XLA Ops:
  0.6 1.5 %copy-start.6 = (s32[1,4]{1,0:T(1,128)S(1)}, s32[1,4]{1,0:T(1,128)}, u32[]{:S(2)}) copy-start(s32[1,4]{1,0:T(1,128)} %order_ref.3) | copy-start | bytes 52
  0.6 1.5 %copy-start.5 = (s32[128]{0:T(128)S(1)}, s32[128]{0:T(128)}, u32[]{:S(2)}) copy-start(s32[128]{0:T(128)} %param.14) | copy-start | bytes 1540
  0.7 13.1 %collective-permute-start = (bf16[1,128,1536]{2,1,0:T(8,128)(2,1)}, bf16[1,128,1536]{2,1,0:T(8,128)(2,1)S(1)}, u32[]{:S(2)}, u32[]{:S(2)}) collective-permute-start(bf16[1,128,1536]{2,1,0:T(8,128)(2,1)} %param.8), channel_id=1, source_target_pairs={{0,8},{8,16},{16,24},{1,9},{9,17},{17,25},{2,10},{10,18},{18,26},{... | collective-permute-start | bytes 1179656 | tf_op jit(solution)/shard_map/ppermute | solution.py:214
  2.1 1.0 %copy-start.1 = (bf16[1,128,1536]{2,1,0:T(8,128)(2,1)S(1)}, bf16[1,128,1536]{2,1,0:T(8,128)(2,1)}, u32[]{:S(2)}) copy-start(bf16[1,128,1536]{2,1,0:T(8,128)(2,1)} %cot_ref.1) | copy-start | bytes 1179652
  4.6 6.0 %copy-start = (bf16[128,1536]{1,0:T(8,128)(2,1)S(1)}, bf16[128,1536]{1,0:T(8,128)(2,1)}, u32[]{:S(2)}) copy-start(bf16[128,1536]{1,0:T(8,128)(2,1)} %emb_ref.1) | copy-start | bytes 1179652
  4.6 6.0 %copy-start.3 = (bf16[1,64,1536]{2,1,0:T(8,128)(2,1)S(1)}, bf16[1,64,1536]{2,1,0:T(8,128)(2,1)}, u32[]{:S(2)}) copy-start(bf16[1,64,1536]{2,1,0:T(8,128)(2,1)} %table_ref.1) | copy-start | bytes 589828
  4.6 33.2 %all-to-all-start = ((f32[8,8,1536]{2,1,0:T(8,128)}), f32[8,8,1536]{2,1,0:T(8,128)S(1)}, u32[]{:S(2)}, u32[]{:S(2)}) async-start(f32[8,8,1536]{2,1,0:T(8,128)} %get-tuple-element.22), calls=%async_computation | async-start | bytes 786432 | tf_op jit(solution)/shard_map/all_to_all | solution.py:199
  39.0 13.1 %all-to-all-start.1 = ((f32[8,8,1536]{2,1,0:T(8,128)}), f32[8,8,1536]{2,1,0:T(8,128)S(1)}, u32[]{:S(2)}, u32[]{:S(2)}) async-start(f32[8,8,1536]{2,1,0:T(8,128)} %gain_part.1), calls=%async_computation.1 | async-start | bytes 786432 | tf_op jit(solution)/shard_map/all_to_all | solution.py:199
  44.0 11.6 %copy-start.2 = (bf16[1,128,1536]{2,1,0:T(8,128)(2,1)S(1)}, bf16[1,128,1536]{2,1,0:T(8,128)(2,1)}, u32[]{:S(2)}) copy-start(bf16[1,128,1536]{2,1,0:T(8,128)(2,1)} %res_ref.1) | copy-start | bytes 1179652
  44.0 15.3 %collective-permute-start.2 = (f32[8,1536]{1,0:T(8,128)S(1)}, f32[8,1536]{1,0:T(8,128)S(1)}, u32[]{:S(2)}, u32[]{:S(2)}) collective-permute-start(f32[8,1536]{1,0:T(8,128)S(1)} %bias_near.1.bias_ref), channel_id=1, source_target_pairs={{0,256},{256,0},{1,257},{257,1},{2,258},{258,2},{3,259},{259,3},{4... | collective-permute-start | bytes 147464 | tf_op jit(solution)/shard_map/ppermute | solution.py:203
  52.2 7.4 %collective-permute-start.1 = (f32[8,1536]{1,0:T(8,128)S(1)}, f32[8,1536]{1,0:T(8,128)S(1)}, u32[]{:S(2)}, u32[]{:S(2)}) collective-permute-start(f32[8,1536]{1,0:T(8,128)S(1)} %gain_near.1.gain_ref), channel_id=1, source_target_pairs={{0,256},{256,0},{1,257},{257,1},{2,258},{258,2},{3,259},{259,3},{4... | collective-permute-start | bytes 147464 | tf_op jit(solution)/shard_map/ppermute | solution.py:203
  56.6 10.9 %collective-permute-start.3 = (bf16[1,128,1536]{2,1,0:T(8,128)(2,1)S(1)}, bf16[1,128,1536]{2,1,0:T(8,128)(2,1)S(1)}, u32[]{:S(2)}, u32[]{:S(2)}) collective-permute-start(bf16[1,128,1536]{2,1,0:T(8,128)(2,1)S(1)} %input_grad.1), channel_id=1, source_target_pairs={{0,24},{8,0},{16,8},{24,16},{1,25},{9,1},{17,9},{25,17},{2,26},{10... | collective-permute-start | bytes 1179656 | tf_op jit(solution)/shard_map/ppermute | solution.py:266
  60.6 3.7 %copy-start.4 = (bf16[1,64,1536]{2,1,0:T(8,128)(2,1)S(1)}, bf16[1,64,1536]{2,1,0:T(8,128)(2,1)}, u32[]{:S(2)}) copy-start(bf16[1,64,1536]{2,1,0:T(8,128)(2,1)} %bias_ref.1) | copy-start | bytes 589828
  60.6 13.1 %all-to-all-start.2 = ((f32[8,16,1536]{2,1,0:T(8,128)}), f32[8,16,1536]{2,1,0:T(8,128)S(1)}, u32[]{:S(2)}, u32[]{:S(2)}) async-start(f32[8,16,1536]{2,1,0:T(8,128)} %add_parts.1), calls=%async_computation.2 | async-start | bytes 1572864 | tf_op jit(solution)/shard_map/all_to_all | solution.py:199

commit v14 on v9

--- a/solution.py
+++ b/solution.py
@@ -243,7 +243,7 @@
         gain_kernel,
         "gain_part",
         shape(pieces, f32),
-        [pltpu.VMEM((2 * tokens, width), bf16), pltpu.VMEM(pieces, f32), sems((3,))],
+        [pltpu.VMEM((2 * tokens, width), bf16), pltpu.VMEM(pieces, f32), sems((6,))],
         [VMEM, VMEM, VMEM, VMEM],
         lang, sums, x, cot,
         out_specs=HBM,

time: 75.1 us -> 75.2 us (level)
  no operation moved by 1% of the time
where the time goes in v14:
time: 75.2 us; the launch traced here: 74.6 us
  starting transfers between devices  25.6 us (34%)
  blocking collectives  23.7 us (32%)
  waiting for transfers between devices  15.2 us (20%)
  Pallas kernels  8.25 us (11%)
  local copies, waits for them, and re-layouts  1.01 us (1%)
  between operations  0.81 us (1%)
    psum x2, blocking collectives, local(): sums = lax.psum(lax.psum(sums, 'core'), 'far')  23.7 us
    all_to_all x3, starting transfers between devices, exchanged(): return lax.all_to_all(pieces, NEAR, 0, 0)  14.6 us
    all_to_all x3, waiting for transfers between devices, exchanged(): return lax.all_to_all(pieces, NEAR, 0, 0)  10.1 us
    pallas_call x11, Pallas kernels, call(): pl.pallas_call(kernel, name=name, out_shape=outs, in_specs=in_specs, out_...  8.25 us
    ppermute x2, starting transfers between devices, from_far(): return lax.ppermute(total, 'far_dp', [(0, 1), (1, 0)])  6.89 us
    ppermute x1, waiting for transfers between devices, local(): lax.ppermute(section_out, 'pipe', [(i, i + 1) for i in range(stages - 1)])  2.84 us
    ppermute x1, starting transfers between devices, local(): lax.ppermute(back, 'pipe', [(i, (i - 1) % stages) for i in range(stages)])  2.73 us
  transfers between devices with their start and end apart: 7, of which 5 were waited for; matrix products, arithmetic and copies ran while one was open for 0% of the time, Pallas kernels for 8%

profile of v14, /device:TPU:6, one launch (start us, length us, event | category | flops | bytes accessed | tf_op | source)
XLA Modules:
  0.0 74.6 jit_solution(5098845436782688568)
XLA Ops:
  0.6 0.0 copy-start.6
  0.6 0.0 copy-start.5
  0.7 1.4 %collective-permute-start = (bf16[1,128,1536]{2,1,0:T(8,128)(2,1)}, bf16[1,128,1536]{2,1,0:T(8,128)(2,1)S(1)}, u32[]{:S(2)}, u32[]{:S(2)}) collective-permute-start(bf16[1,128,1536]{2,1,0:T(8,128)(2,1)} %param.8), channel_id=1, source_target_pairs={{0,8},{8,16},{16,24},{1,9},{9,17},{17,25},{2,10},{10,18},{18,26},{... | collective-permute-start | bytes 1179656 | tf_op jit(solution)/shard_map/ppermute | solution.py:214
  2.1 0.0 copy-done.6
  2.1 0.0 copy-done.5
  2.1 0.0 copy-start.1
  2.1 1.0 %copy-done.1 = bf16[1,128,1536]{2,1,0:T(8,128)(2,1)S(1)} copy-done((bf16[1,128,1536]{2,1,0:T(8,128)(2,1)S(1)}, bf16[1,128,1536]{2,1,0:T(8,128)(2,1)}, u32[]{:S(2)}) %copy-start.1) | copy-done | bytes 393240
  3.1 1.5 %bias_part.1 = (f32[8,8,1536]{2,1,0:T(8,128)}, bf16[128,1536]{1,0:T(8,128)(2,1)S(1)}) custom-call(s32[1,4]{1,0:T(1,128)S(1)} %copy-done.6, s32[1,128]{1,0:T(1,128)S(1)} %bitcast.4, bf16[1,128,1536]{2,1,0:T(8,128)(2,1)S(1)} %copy-done.1), custom_call_target="tpu_custom_call" | custom-call | tf_op jit(solution)/shard_map/bias_part/pallas_call | solution.py:22
  4.6 0.0 copy-start
  4.6 0.0 copy-start.3
  4.6 6.0 %all-to-all-start = ((f32[8,8,1536]{2,1,0:T(8,128)}), f32[8,8,1536]{2,1,0:T(8,128)S(1)}, u32[]{:S(2)}, u32[]{:S(2)}) async-start(f32[8,8,1536]{2,1,0:T(8,128)} %get-tuple-element.23), calls=%async_computation | async-start | bytes 786432 | tf_op jit(solution)/shard_map/all_to_all | solution.py:199
  10.6 0.0 copy-done
  10.6 0.0 copy-done.3
  10.6 0.3 gain_rows.1.gain_ref
  10.9 2.8 %collective-permute-done.recv_ref = bf16[1,128,1536]{2,1,0:T(8,128)(2,1)S(1)} collective-permute-done((bf16[1,128,1536]{2,1,0:T(8,128)(2,1)}, bf16[1,128,1536]{2,1,0:T(8,128)(2,1)S(1)}, u32[]{:S(2)}, u32[]{:S(2)}) %collective-permute-start) | collective-permute-done | bytes 393248 | tf_op jit(solution)/shard_map/ppermute | solution.py:214
  13.7 0.4 token_sums.1
  14.1 2.5 %psum.14 = f32[8,128]{1,0:T(8,128)S(1)} all-reduce(f32[8,128]{1,0:T(8,128)S(1)} %get-tuple-element.27), channel_id=1, replica_groups=mesh['far_dp'=2,'next'=2,'row'=4,'pipe'=4,'far'=4,'core'=2] {'core'}, use_global_device_ids=true, to_apply=%region_0.0 | all-reduce | flops 1024 | bytes 8192 | tf_op jit(solution)/shard_map/psum | solution.py:239
  16.6 21.3 %psum.15.sums_ref = f32[8,128]{1,0:T(8,128)S(1)} all-reduce(f32[8,128]{1,0:T(8,128)S(1)} %psum.14), channel_id=1, replica_groups=mesh['far_dp'=2,'next'=2,'row'=4,'pipe'=4,'far'=4,'core'=2] {'far'}, use_global_device_ids=true, to_apply=%region_1.0 | all-reduce | flops 1024 | bytes 8192 | tf_op jit(solution)/shard_map/psum | solution.py:239
  37.8 0.0 all-to-all-done.parts_ref
  37.8 1.2 %gain_part.1 = f32[8,8,1536]{2,1,0:T(8,128)} custom-call(s32[1,128]{1,0:T(1,128)S(1)} %bitcast.6, f32[8,128]{1,0:T(8,128)S(1)} %psum.15.sums_ref, bf16[128,1536]{1,0:T(8,128)(2,1)S(1)} %get-tuple-element.29.x_ref, bf16[128,1536]{1,0:T(8,128)(2,1)S(1)} %get-tuple-element.25.cot_ref), custom_call_target="tpu_custom_call" | custom-call | tf_op jit(solution)/shard_map/gain_part/pallas_call | solution.py:22
  39.1 4.9 %all-to-all-start.1 = ((f32[8,8,1536]{2,1,0:T(8,128)}), f32[8,8,1536]{2,1,0:T(8,128)S(1)}, u32[]{:S(2)}, u32[]{:S(2)}) async-start(f32[8,8,1536]{2,1,0:T(8,128)} %gain_part.1), calls=%async_computation.1 | async-start | bytes 786432 | tf_op jit(solution)/shard_map/all_to_all | solution.py:199
  44.0 0.0 copy-start.2
  44.0 3.5 %collective-permute-start.2 = (f32[8,1536]{1,0:T(8,128)S(1)}, f32[8,1536]{1,0:T(8,128)S(1)}, u32[]{:S(2)}, u32[]{:S(2)}) collective-permute-start(f32[8,1536]{1,0:T(8,128)S(1)} %bias_near.1.bias_ref), channel_id=1, source_target_pairs={{0,256},{256,0},{1,257},{257,1},{2,258},{258,2},{3,259},{259,3},{4... | collective-permute-start | bytes 147464 | tf_op jit(solution)/shard_map/ppermute | solution.py:203
  47.5 0.0 copy-done.2
  47.5 1.0 %input_grad.1 = bf16[1,128,1536]{2,1,0:T(8,128)(2,1)S(1)} custom-call(s32[1,4]{1,0:T(1,128)S(1)} %copy-done.6, f32[8,128]{1,0:T(8,128)S(1)} %psum.15.sums_ref, bf16[128,1536]{1,0:T(8,128)(2,1)S(1)} %get-tuple-element.29.x_ref, bf16[128,1536]{1,0:T(8,128)(2,1)S(1)} %get-tuple-element.25.cot_ref, bf16[1,128,1536]{2,1,0:T(8,128)(2,1)S(1)} %copy-done.2, ...), custom_call_target="tpu_custom_call" | custom-call | tf_op jit(solution)/shard_map/input_grad/pallas_call | solution.py:22
  48.6 3.6 %all-to-all-done.1.parts_ref = f32[8,8,1536]{2,1,0:T(8,128)S(1)} async-done(((f32[8,8,1536]{2,1,0:T(8,128)}), f32[8,8,1536]{2,1,0:T(8,128)S(1)}, u32[]{:S(2)}, u32[]{:S(2)}) %all-to-all-start.1) | async-done | bytes 393248 | tf_op jit(solution)/shard_map/all_to_all | solution.py:199
  52.2 3.4 %collective-permute-start.1 = (f32[8,1536]{1,0:T(8,128)S(1)}, f32[8,1536]{1,0:T(8,128)S(1)}, u32[]{:S(2)}, u32[]{:S(2)}) collective-permute-start(f32[8,1536]{1,0:T(8,128)S(1)} %gain_near.1.gain_ref), channel_id=1, source_target_pairs={{0,256},{256,0},{1,257},{257,1},{2,258},{258,2},{3,259},{259,3},{4... | collective-permute-start | bytes 147464 | tf_op jit(solution)/shard_map/ppermute | solution.py:203
  55.6 2.7 %collective-permute-start.3 = (bf16[1,128,1536]{2,1,0:T(8,128)(2,1)S(1)}, bf16[1,128,1536]{2,1,0:T(8,128)(2,1)S(1)}, u32[]{:S(2)}, u32[]{:S(2)}) collective-permute-start(bf16[1,128,1536]{2,1,0:T(8,128)(2,1)S(1)} %input_grad.1), channel_id=1, source_target_pairs={{0,24},{8,0},{16,8},{24,16},{1,25},{9,1},{17,9},{25,17},{2,26},{10... | collective-permute-start | bytes 1179656 | tf_op jit(solution)/shard_map/ppermute | solution.py:266
  58.3 0.0 collective-permute-done.2.bias_far_ref
  58.3 1.3 %collective-permute-done.1.gain_far_ref = f32[8,1536]{1,0:T(8,128)S(1)} collective-permute-done((f32[8,1536]{1,0:T(8,128)S(1)}, f32[8,1536]{1,0:T(8,128)S(1)}, u32[]{:S(2)}, u32[]{:S(2)}) %collective-permute-start.1) | collective-permute-done | bytes 49184 | tf_op jit(solution)/shard_map/ppermute | solution.py:203
  59.6 1.0 %add_parts.1 = f32[8,16,1536]{2,1,0:T(8,128)} custom-call(f32[8,1536]{1,0:T(8,128)S(1)} %gain_near.1.gain_ref, f32[8,1536]{1,0:T(8,128)S(1)} %collective-permute-done.1.gain_far_ref, f32[8,1536]{1,0:T(8,128)S(1)} %bias_near.1.bias_ref, f32[8,1536]{1,0:T(8,128)S(1)} %collective-permute-done.2.bias_far_ref), custom_call_target="tpu_custom_call" | custom-call | flops 99999997952 | tf_op jit(solution)/shard_map/add_parts/pallas_call | solution.py:22
  60.6 0.0 copy-start.4
  60.6 3.7 %all-to-all-start.2 = ((f32[8,16,1536]{2,1,0:T(8,128)}), f32[8,16,1536]{2,1,0:T(8,128)S(1)}, u32[]{:S(2)}, u32[]{:S(2)}) async-start(f32[8,16,1536]{2,1,0:T(8,128)} %add_parts.1), calls=%async_computation.2 | async-start | bytes 1572864 | tf_op jit(solution)/shard_map/all_to_all | solution.py:199
  64.3 0.0 copy-done.4
  64.3 1.1 %normed.1 = bf16[1,128,1536]{2,1,0:T(8,128)(2,1)} custom-call(s32[1,128]{1,0:T(1,128)S(1)} %bitcast.7, f32[8,128]{1,0:T(8,128)S(1)} %psum.15.sums_ref, bf16[128,1536]{1,0:T(8,128)(2,1)S(1)} %get-tuple-element.29.x_ref, bf16[128,1536]{1,0:T(8,128)(2,1)S(1)} %gain_rows.1.gain_ref, bf16[1,64,1536]{2,1,0:T(8,128)(2,1)S(1)} %copy-done.4), custom_call_target="tpu_custom_call" | custom-call | tf_op jit(solution)/shard_map/normed/pallas_call | solution.py:22
  65.5 1.0 %collective-permute-done.3.value_ref = bf16[1,128,1536]{2,1,0:T(8,128)(2,1)S(1)} collective-permute-done((bf16[1,128,1536]{2,1,0:T(8,128)(2,1)S(1)}, bf16[1,128,1536]{2,1,0:T(8,128)(2,1)S(1)}, u32[]{:S(2)}, u32[]{:S(2)}) %collective-permute-start.3) | collective-permute-done | bytes 393248 | tf_op jit(solution)/shard_map/ppermute | solution.py:266
  66.5 0.8 %settle.1 = bf16[1,128,1536]{2,1,0:T(8,128)(2,1)} custom-call(bf16[1,128,1536]{2,1,0:T(8,128)(2,1)S(1)} %collective-permute-done.3.value_ref), custom_call_target="tpu_custom_call" | custom-call | flops 99999997952 | tf_op jit(solution)/shard_map/settle/pallas_call | solution.py:22
  67.2 6.5 %all-to-all-done.2.parts_ref = f32[8,16,1536]{2,1,0:T(8,128)S(1)} async-done(((f32[8,16,1536]{2,1,0:T(8,128)}), f32[8,16,1536]{2,1,0:T(8,128)S(1)}, u32[]{:S(2)}, u32[]{:S(2)}) %all-to-all-start.2) | async-done | bytes 786464 | tf_op jit(solution)/shard_map/all_to_all | solution.py:199
  73.7 0.9 %whole_grads.1 = (f32[8,8,1536]{2,1,0:T(8,128)}, f32[8,8,1536]{2,1,0:T(8,128)}) custom-call(f32[8,16,1536]{2,1,0:T(8,128)S(1)} %all-to-all-done.2.parts_ref), custom_call_target="tpu_custom_call" | custom-call | tf_op jit(solution)/shard_map/whole_grads/pallas_call | solution.py:22
  (2 shorter events, 0.0 us)
Async XLA Ops:
  0.6 1.5 %copy-start.6 = (s32[1,4]{1,0:T(1,128)S(1)}, s32[1,4]{1,0:T(1,128)}, u32[]{:S(2)}) copy-start(s32[1,4]{1,0:T(1,128)} %order_ref.3) | copy-start | bytes 52
  0.6 1.5 %copy-start.5 = (s32[128]{0:T(128)S(1)}, s32[128]{0:T(128)}, u32[]{:S(2)}) copy-start(s32[128]{0:T(128)} %param.14) | copy-start | bytes 1540
  0.7 13.1 %collective-permute-start = (bf16[1,128,1536]{2,1,0:T(8,128)(2,1)}, bf16[1,128,1536]{2,1,0:T(8,128)(2,1)S(1)}, u32[]{:S(2)}, u32[]{:S(2)}) collective-permute-start(bf16[1,128,1536]{2,1,0:T(8,128)(2,1)} %param.8), channel_id=1, source_target_pairs={{0,8},{8,16},{16,24},{1,9},{9,17},{17,25},{2,10},{10,18},{18,26},{... | collective-permute-start | bytes 1179656 | tf_op jit(solution)/shard_map/ppermute | solution.py:214
  2.1 1.0 %copy-start.1 = (bf16[1,128,1536]{2,1,0:T(8,128)(2,1)S(1)}, bf16[1,128,1536]{2,1,0:T(8,128)(2,1)}, u32[]{:S(2)}) copy-start(bf16[1,128,1536]{2,1,0:T(8,128)(2,1)} %cot_ref.1) | copy-start | bytes 1179652
  4.6 6.0 %copy-start = (bf16[128,1536]{1,0:T(8,128)(2,1)S(1)}, bf16[128,1536]{1,0:T(8,128)(2,1)}, u32[]{:S(2)}) copy-start(bf16[128,1536]{1,0:T(8,128)(2,1)} %emb_ref.1) | copy-start | bytes 1179652
  4.6 6.0 %copy-start.3 = (bf16[1,64,1536]{2,1,0:T(8,128)(2,1)S(1)}, bf16[1,64,1536]{2,1,0:T(8,128)(2,1)}, u32[]{:S(2)}) copy-start(bf16[1,64,1536]{2,1,0:T(8,128)(2,1)} %table_ref.1) | copy-start | bytes 589828
  4.6 33.2 %all-to-all-start = ((f32[8,8,1536]{2,1,0:T(8,128)}), f32[8,8,1536]{2,1,0:T(8,128)S(1)}, u32[]{:S(2)}, u32[]{:S(2)}) async-start(f32[8,8,1536]{2,1,0:T(8,128)} %get-tuple-element.23), calls=%async_computation | async-start | bytes 786432 | tf_op jit(solution)/shard_map/all_to_all | solution.py:199
  39.1 13.1 %all-to-all-start.1 = ((f32[8,8,1536]{2,1,0:T(8,128)}), f32[8,8,1536]{2,1,0:T(8,128)S(1)}, u32[]{:S(2)}, u32[]{:S(2)}) async-start(f32[8,8,1536]{2,1,0:T(8,128)} %gain_part.1), calls=%async_computation.1 | async-start | bytes 786432 | tf_op jit(solution)/shard_map/all_to_all | solution.py:199
  44.0 3.6 %copy-start.2 = (bf16[1,128,1536]{2,1,0:T(8,128)(2,1)S(1)}, bf16[1,128,1536]{2,1,0:T(8,128)(2,1)}, u32[]{:S(2)}) copy-start(bf16[1,128,1536]{2,1,0:T(8,128)(2,1)} %res_ref.1) | copy-start | bytes 1179652
  44.0 14.3 %collective-permute-start.2 = (f32[8,1536]{1,0:T(8,128)S(1)}, f32[8,1536]{1,0:T(8,128)S(1)}, u32[]{:S(2)}, u32[]{:S(2)}) collective-permute-start(f32[8,1536]{1,0:T(8,128)S(1)} %bias_near.1.bias_ref), channel_id=1, source_target_pairs={{0,256},{256,0},{1,257},{257,1},{2,258},{258,2},{3,259},{259,3},{4... | collective-permute-start | bytes 147464 | tf_op jit(solution)/shard_map/ppermute | solution.py:203
  52.2 7.4 %collective-permute-start.1 = (f32[8,1536]{1,0:T(8,128)S(1)}, f32[8,1536]{1,0:T(8,128)S(1)}, u32[]{:S(2)}, u32[]{:S(2)}) collective-permute-start(f32[8,1536]{1,0:T(8,128)S(1)} %gain_near.1.gain_ref), channel_id=1, source_target_pairs={{0,256},{256,0},{1,257},{257,1},{2,258},{258,2},{3,259},{259,3},{4... | collective-permute-start | bytes 147464 | tf_op jit(solution)/shard_map/ppermute | solution.py:203
  55.6 10.9 %collective-permute-start.3 = (bf16[1,128,1536]{2,1,0:T(8,128)(2,1)S(1)}, bf16[1,128,1536]{2,1,0:T(8,128)(2,1)S(1)}, u32[]{:S(2)}, u32[]{:S(2)}) collective-permute-start(bf16[1,128,1536]{2,1,0:T(8,128)(2,1)S(1)} %input_grad.1), channel_id=1, source_target_pairs={{0,24},{8,0},{16,8},{24,16},{1,25},{9,1},{17,9},{25,17},{2,26},{10... | collective-permute-start | bytes 1179656 | tf_op jit(solution)/shard_map/ppermute | solution.py:266
  60.6 3.7 %copy-start.4 = (bf16[1,64,1536]{2,1,0:T(8,128)(2,1)S(1)}, bf16[1,64,1536]{2,1,0:T(8,128)(2,1)}, u32[]{:S(2)}) copy-start(bf16[1,64,1536]{2,1,0:T(8,128)(2,1)} %bias_ref.1) | copy-start | bytes 589828
  60.6 13.1 %all-to-all-start.2 = ((f32[8,16,1536]{2,1,0:T(8,128)}), f32[8,16,1536]{2,1,0:T(8,128)S(1)}, u32[]{:S(2)}, u32[]{:S(2)}) async-start(f32[8,16,1536]{2,1,0:T(8,128)} %add_parts.1), calls=%async_computation.2 | async-start | bytes 1572864 | tf_op jit(solution)/shard_map/all_to_all | solution.py:199
